TPU v7x, 256 devices: a whole 4x4x8 slice. The times are simulated.
256 devices in a mesh: dp: 8 (over x_hi, y), fsdp: 16 (over z, core), tensor: 2 (over x_lo).
Axes of the slice: x: 4 (x_hi: 2, x_lo: 2; x = x_hi * 2 + x_lo), y: 4, z: 8, core: 2. Of those that a mesh axis runs over, the one named last changes fastest.
Arguments:
- attn_out: bfloat16 [16384, 2560], P(('dp', 'fsdp')), may hold values from -6 to 6
- cotangent: bfloat16 [16384, 5120], P(('dp', 'fsdp'), 'tensor'), may hold values from -6 to 6
- old_weights: bfloat16 [3, 2048, 4096], P(None, 'tensor', 'fsdp'), may hold values from -0.125 to 0.125
- depth_coef: float32 [2], replicated, may hold values from 0.3 to 1
- depth_pick: int32 [2], replicated, may hold values from 0 to 2
- in_blocks: bfloat16 [20, 2, 128, 128], replicated, may hold values from -0.3125 to 0.3125
- in_cols: int32 [20, 2], replicated, may hold values from 0 to 15, all different within a row
- out_blocks: bfloat16 [40, 2, 128, 128], P('tensor'), may hold values from -0.375 to 0.375
- out_cols: int32 [40, 2], P('tensor'), may hold values from 0 to 31, all different within a row
Outputs:
- grown_out: bfloat16 [16384, 5120], P(('dp', 'fsdp'), 'tensor')
- grad_attn: bfloat16 [16384, 2560], P(('dp', 'fsdp'), 'tensor')
- grad_in_blocks: float32 [20, 2, 128, 128], P('tensor')
- grad_out_blocks: float32 [40, 2, 128, 128], P('tensor')
Inputs may be any that keep to these rules, and one draw needn't show every extreme that they name: `in_cols`: each row names 2 different old head blocks; every old head block is named by some row. `out_cols`: each row names 2 different old width blocks; every old width block is named by some row.
All inputs are finite; a program needn't handle non-finite values.
Results may differ from a plain program's by a relative error of at most 0.0095.
Values may be sent and summed in bfloat16 or wider, within the bound.
No kernel may reach another device: no remote copies, remote signals or barrier semaphores. Data moves between devices by JAX's collectives and lax.ppermute only.
A program may use at most 64 MiB of HBM per device.

v0:
```python
import jax
import jax.numpy as jnp
from jax import lax
from jax.sharding import PartitionSpec as P

HEAD = 128
D_OLD = 4096
HG_OLD = 16
HG_NEW = 20
DEPTH_K = 2
BO_OLD = 32


def gathered_mix(mixed_weight):
    return lax.all_gather(mixed_weight, "fsdp", axis=1, tiled=True)


def local(
    attn_out,
    cotangent,
    old_weights,
    depth_coef,
    depth_pick,
    in_blocks,
    in_cols,
    out_blocks,
    out_cols,
):
    highest = lax.Precision.HIGHEST
    tok_rows = attn_out.shape[0]
    tensor_half = lax.axis_index("tensor")
    tensor_count = lax.axis_size("tensor")
    local_old = old_weights.shape[1]
    local_blocks = local_old // HEAD
    rows_in = HG_NEW // tensor_count
    mixed_weight = jnp.zeros(old_weights.shape[1:], jnp.float32)
    for layer_slot in range(DEPTH_K):
        picked = lax.dynamic_index_in_dim(old_weights, depth_pick[layer_slot], 0, keepdims=False)
        mixed_weight = mixed_weight + depth_coef[layer_slot] * picked.astype(jnp.float32)
    mixed_weight = mixed_weight.astype(jnp.bfloat16)
    attn_blocks = attn_out.reshape(tok_rows, HG_NEW, HEAD)
    products = jnp.einsum(
        "trd,rkde->trke", attn_blocks, in_blocks, preferred_element_type=jnp.float32
    )
    local_cols = tensor_half * local_blocks + jnp.arange(local_blocks, dtype=jnp.int32)
    in_hot = (in_cols[:, :, None] == local_cols[None, None, :]).astype(jnp.float32)
    hidden_local = jnp.einsum("trke,rkc->tce", products, in_hot, precision=highest)
    hidden_local = hidden_local.reshape(tok_rows, local_old).astype(jnp.bfloat16)
    full_mix = gathered_mix(mixed_weight)
    old_part = jnp.dot(hidden_local, full_mix, preferred_element_type=jnp.float32)
    old_out = lax.psum(old_part.astype(jnp.bfloat16), "tensor")
    old_selected = jnp.take(old_out.reshape(tok_rows, BO_OLD, HEAD), out_cols, axis=1)
    grown_out = jnp.einsum(
        "trkd,rkde->tre", old_selected, out_blocks, preferred_element_type=jnp.float32
    )
    grown_out = grown_out.reshape(tok_rows, -1).astype(jnp.bfloat16)
    cot_blocks = cotangent.reshape(tok_rows, out_blocks.shape[0], HEAD)
    backward_terms = jnp.einsum(
        "tre,rkde->trkd", cot_blocks, out_blocks, preferred_element_type=jnp.float32
    )
    out_hot = (out_cols[:, :, None] == jnp.arange(BO_OLD, dtype=jnp.int32)[None, None, :]).astype(
        jnp.float32
    )
    grad_part = jnp.einsum("trkd,rkc->tcd", backward_terms, out_hot, precision=highest).reshape(
        tok_rows, D_OLD
    )
    old_grad = lax.psum(grad_part.astype(jnp.bfloat16), "tensor")
    hidden_grad_local = jnp.einsum(
        "to,fo->tf", old_grad, full_mix, preferred_element_type=jnp.float32
    ).astype(jnp.bfloat16)
    hidden_grad = lax.all_gather(hidden_grad_local, "tensor", axis=1, tiled=True)
    my_in_blocks = lax.dynamic_slice_in_dim(in_blocks, tensor_half * rows_in, rows_in, 0)
    my_in_cols = lax.dynamic_slice_in_dim(in_cols, tensor_half * rows_in, rows_in, 0)
    grad_selected = jnp.take(hidden_grad.reshape(tok_rows, HG_OLD, HEAD), my_in_cols, axis=1)
    grad_attn = jnp.einsum(
        "trke,rkde->trd", grad_selected, my_in_blocks, preferred_element_type=jnp.float32
    )
    grad_attn = grad_attn.reshape(tok_rows, rows_in * HEAD).astype(jnp.bfloat16)
    my_attn = lax.dynamic_slice_in_dim(attn_blocks, tensor_half * rows_in, rows_in, 1)
    in_terms = jnp.einsum(
        "trd,trke->rkde", my_attn, grad_selected, preferred_element_type=jnp.float32
    )
    out_terms = jnp.einsum(
        "trkd,tre->rkde", old_selected, cot_blocks, preferred_element_type=jnp.float32
    )
    in_sum, out_sum = lax.psum((in_terms, out_terms), ("dp", "fsdp"))
    grad_scale = float(tok_rows * lax.axis_size("dp") * lax.axis_size("fsdp")) ** (-0.5)
    return (grown_out, grad_attn, in_sum * grad_scale, out_sum * grad_scale)


def solution(mesh):
    placed = (
        P(("dp", "fsdp"), None),
        P(("dp", "fsdp"), "tensor"),
        P(None, "tensor", "fsdp"),
        P(),
        P(),
        P(),
        P(),
        P("tensor", None, None, None),
        P("tensor", None),
    )
    return jax.shard_map(
        local,
        mesh=mesh,
        in_specs=placed,
        out_specs=(
            P(("dp", "fsdp"), "tensor"),
            P(("dp", "fsdp"), "tensor"),
            P("tensor", None, None, None),
            P("tensor", None, None, None),
        ),
        check_vma=False,
    )
```

profile of v0, /device:TPU:1, one launch (start us, length us, event | category | flops | bytes accessed | tf_op | source)
XLA Modules:
  0.0 1477.4 jit_solution(9573268355496351866)
XLA Ops:
  7.2 0.0 copy-start
  7.2 0.0 all-gather.3.cloned.1.call-start
  7.2 1.3 fusion.55
  11.2 1.3 fusion.54
  13.8 3.5 add_convert_fusion
  17.3 0.0 all-gather.3.cloned.1.call-update
  17.3 0.0 all-reduce.7.cloned.1.call-start
  17.3 1.5 copy.27
  18.9 2.0 fusion.56
  20.9 3.6 copy.45
  24.5 0.3 copy.34
  24.9 2.0 fusion.57
  26.9 3.6 copy.51
  30.4 3.3 bitcast_convert_fusion
  33.8 1.4 copy.71
  35.2 3.0 fusion.24
  38.2 48.5 %all-gather.3.cloned.1.call-done = bf16[1,1024,4096]{2,1,0:T(8,128)(2,1)} async-done(((bf16[1,1024,256]{2,1,0:T(8,128)(2,1)}), bf16[1,1024,4096]{2,1,0:T(8,128)(2,1)}) %all-gather.3.cloned.1.call-update) | async-done | bytes 8388624 | tf_op jit(solution)/shard_map/all_gather | solution.py:15
  86.7 4.7 fusion.13
  91.4 1.3 copy.72
  92.6 0.0 all-reduce.7.cloned.1.call-update
  92.6 0.0 all-reduce.5.cloned.1.call-start
  92.7 0.1 compare_and_fusion
  92.8 0.1 copy.35
  92.9 0.1 reshape.66
  93.0 0.1 copy.33
  93.1 0.1 copy.29
  93.2 0.1 reshape.58
  93.3 0.1 copy.26
  93.4 71.4 %all-reduce.7.cloned.1.call-done = (bf16[128,32,128]{2,0,1:T(8,128)(2,1)}, bf16[128,4096]{1,0:T(8,128)(2,1)}) async-done(((bf16[128,32,128]{2,0,1:T(8,128)(2,1)}, bf16[128,4096]{1,0:T(8,128)(2,1)}), (bf16[128,32,128]{2,0,1:T(8,128)(2,1)}, bf16[128,4096]{1,0:T(8,128)(2,1)})) %all-reduce.7.cloned.1.call-update) | async-done | bytes 2097168 | tf_op jit(solution)/shard_map/psum | solution.py:51
  164.8 6.6 fusion.27
  171.4 7.9 all_gather.7
  179.3 0.1 copy_bitcast_fusion.2
  179.4 0.7 gather_fusion.1
  180.1 1.1 copy.37
  181.2 3.1 gather_fusion
  184.3 1.8 copy.30
  186.1 2.0 fusion.17
  188.1 1.4 convolution_bitcast_fusion
  189.6 0.0 all-reduce.5.cloned.1.call-update
  189.6 1.1 copy-done.4
  190.6 2.2 fusion.23
  192.9 1.9 copy.42
  194.7 0.6 fusion.16
  195.3 1.1 copy.41
  196.4 1269.2 %all-reduce.5.cloned.1.call-done = (f32[10,2,128,128]{2,3,1,0:T(8,128)}, f32[20,2,128,128]{3,2,1,0:T(8,128)}) async-done(((f32[10,2,128,128]{2,3,1,0:T(8,128)}, f32[20,2,128,128]{3,2,1,0:T(8,128)}), (f32[10,2,128,128]{2,3,1,0:T(8,128)}, f32[20,2,128,128]{3,2,1,0:T(8,128)})) %all-reduce.5.cloned.1.call-update) | async-done | bytes 3932176 | tf_op jit(solution)/shard_map/psum | solution.py:86
  1465.7 3.6 broadcast_multiply_fusion
  1469.3 0.1 broadcast_multiply_fusion.1
  1469.4 1.5 copy.43
  (23 shorter events, 0.1 us)
Async XLA Ops:
  7.2 17.7 %copy-start = (bf16[20,2,128,128]{3,2,1,0:T(8,128)(2,1)S(1)}, bf16[20,2,128,128]{3,2,1,0:T(8,128)(2,1)}, u32[]{:S(2)}) copy-start(bf16[20,2,128,128]{3,2,1,0:T(8,128)(2,1)} %param.16) | copy-start | bytes 3932164
  7.2 79.5 %all-gather.3.cloned.1.call-start = ((), (), s32[]{:S(2)}) async-start(), calls=%async_computation | async-start | bytes 8912896 | tf_op jit(solution)/shard_map/all_gather | solution.py:15
  17.3 1.6 copy-start.6
  17.3 147.5 %all-reduce.7.cloned.1.call-start = ((), (), s32[]{:S(2)}) async-start(), calls=%async_computation.2 | async-start | bytes 4194304 | tf_op jit(solution)/shard_map/psum | solution.py:51
  18.8 2.1 copy-start.1
  20.9 3.6 copy-start.7
  26.9 3.6 copy-start.9
  33.8 1.4 copy-start.8
  92.6 1373.0 %all-reduce.5.cloned.1.call-start = ((), (), s32[]{:S(2)}) async-start(), calls=%async_computation.1 | async-start | bytes 7864320 | tf_op jit(solution)/shard_map/psum | solution.py:86
  186.0 2.1 copy-start.2
  186.1 2.1 copy-start.3
  189.6 1.1 copy-start.4
  1465.7 3.6 copy-start.5
Sparse Core Ops, SparseCore 0:
  17.4 69.2 all-gather.2
  92.8 71.9 all-reduce.6
  189.7 1275.9 all-reduce.4
where the time goes:
time: 1480 us
  waiting for transfers between devices  1390 us (94%)
  matrix products  28 us (2%)
  local copies, waits for them, and re-layouts  27.2 us (2%)
  between operations  17.8 us (1%)
    psum x1, waiting for transfers between devices, local(): in_sum, out_sum = lax.psum((in_terms, out_terms), ('dp', 'fsdp'))  1270 us
    psum x1, waiting for transfers between devices, local(): old_out = lax.psum(old_part.astype(jnp.bfloat16), 'tensor')  71.4 us
    all_gather x1, waiting for transfers between devices, gathered_mix(): return lax.all_gather(mixed_weight, 'fsdp', axis=1, tiled=True)  48.5 us
  transfers between devices with their start and end apart: 3, of which 3 were waited for; matrix products, arithmetic and copies ran while one was open for 2% of the time, Pallas kernels for 0%

commit v1 on v0

--- a/solution.py
+++ b/solution.py
@@ -1,6 +1,7 @@
 import jax
 import jax.numpy as jnp
 from jax import lax
+from jax.sharding import Mesh
 from jax.sharding import PartitionSpec as P
 
 HEAD = 128
@@ -11,8 +12,44 @@
 BO_OLD = 32
 
 
+PEERS = ("xh", "y", "z")
+
+
 def gathered_mix(mixed_weight):
-    return lax.all_gather(mixed_weight, "fsdp", axis=1, tiled=True)
+    return lax.all_gather(mixed_weight, ("z", "c"), axis=1, tiled=True)
+
+
+def pair_sum(part):
+    other = lax.ppermute(part, "xl", [(0, 1), (1, 0)])
+    return (part.astype(jnp.float32) + other.astype(jnp.float32)).astype(jnp.bfloat16)
+
+
+def token_sum(in_terms, out_terms, scale):
+    core = lax.axis_index("c")
+    peers = lax.axis_size(PEERS)
+    ri, ro = in_terms.shape[0] // 2, out_terms.shape[0] // 2
+
+    def half(which):
+        a = lax.dynamic_slice_in_dim(in_terms, which * ri, ri, 0).reshape(-1, HEAD)
+        b = lax.dynamic_slice_in_dim(out_terms, which * ro, ro, 0).reshape(-1, HEAD)
+        return jnp.concatenate([a, b], axis=0)
+
+    swap = [(0, 1), (1, 0)]
+    other = lax.ppermute(half(1 - core).astype(jnp.bfloat16), "c", swap)
+    mine = (half(core) + other.astype(jnp.float32)).astype(jnp.bfloat16)
+    rows = mine.shape[0]
+    mine = mine.reshape(peers, rows // peers, HEAD)
+    parts = lax.all_to_all(mine, PEERS, 0, 0, tiled=True)
+    total = (jnp.sum(parts.astype(jnp.float32), axis=0) * scale).astype(jnp.bfloat16)
+    spread = jnp.broadcast_to(total[None], mine.shape)
+    full = lax.all_to_all(spread, PEERS, 0, 0, tiled=True).reshape(rows, HEAD)
+    theirs = lax.ppermute(full, "c", swap)
+    first = jnp.where(core == 0, full, theirs).astype(jnp.float32)
+    second = jnp.where(core == 0, theirs, full).astype(jnp.float32)
+    cut = ri * in_terms.shape[1] * HEAD
+    in_sum = jnp.concatenate([first[:cut], second[:cut]], 0).reshape(in_terms.shape)
+    out_sum = jnp.concatenate([first[cut:], second[cut:]], 0).reshape(out_terms.shape)
+    return in_sum, out_sum
 
 
 def local(
@@ -28,8 +65,8 @@
 ):
     highest = lax.Precision.HIGHEST
     tok_rows = attn_out.shape[0]
-    tensor_half = lax.axis_index("tensor")
-    tensor_count = lax.axis_size("tensor")
+    tensor_half = lax.axis_index("xl")
+    tensor_count = lax.axis_size("xl")
     local_old = old_weights.shape[1]
     local_blocks = local_old // HEAD
     rows_in = HG_NEW // tensor_count
@@ -48,7 +85,7 @@
     hidden_local = hidden_local.reshape(tok_rows, local_old).astype(jnp.bfloat16)
     full_mix = gathered_mix(mixed_weight)
     old_part = jnp.dot(hidden_local, full_mix, preferred_element_type=jnp.float32)
-    old_out = lax.psum(old_part.astype(jnp.bfloat16), "tensor")
+    old_out = pair_sum(old_part.astype(jnp.bfloat16))
     old_selected = jnp.take(old_out.reshape(tok_rows, BO_OLD, HEAD), out_cols, axis=1)
     grown_out = jnp.einsum(
         "trkd,rkde->tre", old_selected, out_blocks, preferred_element_type=jnp.float32
@@ -64,11 +101,11 @@
     grad_part = jnp.einsum("trkd,rkc->tcd", backward_terms, out_hot, precision=highest).reshape(
         tok_rows, D_OLD
     )
-    old_grad = lax.psum(grad_part.astype(jnp.bfloat16), "tensor")
+    old_grad = pair_sum(grad_part.astype(jnp.bfloat16))
     hidden_grad_local = jnp.einsum(
         "to,fo->tf", old_grad, full_mix, preferred_element_type=jnp.float32
     ).astype(jnp.bfloat16)
-    hidden_grad = lax.all_gather(hidden_grad_local, "tensor", axis=1, tiled=True)
+    hidden_grad = lax.all_gather(hidden_grad_local, "xl", axis=1, tiled=True)
     my_in_blocks = lax.dynamic_slice_in_dim(in_blocks, tensor_half * rows_in, rows_in, 0)
     my_in_cols = lax.dynamic_slice_in_dim(in_cols, tensor_half * rows_in, rows_in, 0)
     grad_selected = jnp.take(hidden_grad.reshape(tok_rows, HG_OLD, HEAD), my_in_cols, axis=1)
@@ -83,32 +120,34 @@
     out_terms = jnp.einsum(
         "trkd,tre->rkde", old_selected, cot_blocks, preferred_element_type=jnp.float32
     )
-    in_sum, out_sum = lax.psum((in_terms, out_terms), ("dp", "fsdp"))
-    grad_scale = float(tok_rows * lax.axis_size("dp") * lax.axis_size("fsdp")) ** (-0.5)
-    return (grown_out, grad_attn, in_sum * grad_scale, out_sum * grad_scale)
+    grad_scale = float(tok_rows * lax.axis_size(PEERS) * lax.axis_size("c")) ** (-0.5)
+    in_sum, out_sum = token_sum(in_terms, out_terms, grad_scale)
+    return (grown_out, grad_attn, in_sum, out_sum)
 
 
 def solution(mesh):
+    fine = Mesh(mesh.devices.reshape(2, 4, 8, 2, 2), ("xh", "y", "z", "c", "xl"))
+    tokens = ("xh", "y", "z", "c")
     placed = (
-        P(("dp", "fsdp"), None),
-        P(("dp", "fsdp"), "tensor"),
-        P(None, "tensor", "fsdp"),
+        P(tokens, None),
+        P(tokens, "xl"),
+        P(None, "xl", ("z", "c")),
         P(),
         P(),
         P(),
         P(),
-        P("tensor", None, None, None),
-        P("tensor", None),
+        P("xl", None, None, None),
+        P("xl", None),
     )
     return jax.shard_map(
         local,
-        mesh=mesh,
+        mesh=fine,
         in_specs=placed,
         out_specs=(
-            P(("dp", "fsdp"), "tensor"),
-            P(("dp", "fsdp"), "tensor"),
-            P("tensor", None, None, None),
-            P("tensor", None, None, None),
+            P(tokens, "xl"),
+            P(tokens, "xl"),
+            P("xl", None, None, None),
+            P("xl", None, None, None),
         ),
         check_vma=False,
     )

time: 1480 us -> 241 us (0.16)
  waiting for transfers between devices: 1390 us -> 44.9 us
  blocking collectives: 7.86 us -> 98.8 us
    psum x2 -> x0, waiting for transfers between devices: 1340 us -> none  [the longest x1 1270 us: local(): in_sum, out_sum = lax.psum((in_terms, out_terms), ('dp', 'fsdp'))]
    all_to_all x0 -> x2, blocking collectives: none -> 72.7 us  [the longest x1 38 us: token_sum(): parts = lax.all_to_all(mine, PEERS, 0, 0, tiled=True)]
    all_gather x1, blocking collectives: 7.86 us -> 26.1 us  [local(): hidden_grad = lax.all_gather(hidden_grad_local, 'xl', axis=1, tiled=True)]
  transfers between devices with their start and end apart: 3 -> 5, of which waited for: 3 -> 2; matrix products, arithmetic and copies ran while one was open for 2% -> 18% of each run, Pallas kernels for 0% -> 0%
where the time goes in v1:
time: 241 us; the launch traced here: 240 us
  blocking collectives  98.8 us (41%)
  waiting for transfers between devices  44.9 us (19%)
  local copies, waits for them, and re-layouts  30.4 us (13%)
  matrix products  28 us (12%)
  between operations  18.2 us (8%)
  other arithmetic  12.2 us (5%)
  starting transfers between devices  7.18 us (3%)
    all_gather x1, waiting for transfers between devices, gathered_mix(): return lax.all_gather(mixed_weight, ('z', 'c'), axis=1, tiled=True)  43.8 us
    all_to_all x1, blocking collectives, token_sum(): parts = lax.all_to_all(mine, PEERS, 0, 0, tiled=True)  38 us
    all_to_all x1, blocking collectives, token_sum(): full = lax.all_to_all(spread, PEERS, 0, 0, tiled=True).reshape(rows, HEAD)  34.7 us
    all_gather x1, blocking collectives, local(): hidden_grad = lax.all_gather(hidden_grad_local, 'xl', axis=1, tiled=True)  26.1 us
    unnamed x29, local copies, waits for them, and re-layouts  9.58 us
    dot_general x1, matrix products, local(): jnp.dot(hidden_local, full_mix, preferred_element_type=jnp.float32)  5.77 us
  transfers between devices with their start and end apart: 5, of which 2 were waited for; matrix products, arithmetic and copies ran while one was open for 18% of the time, Pallas kernels for 0%

profile of v1, /device:TPU:1, one launch (start us, length us, event | category | flops | bytes accessed | tf_op | source)
XLA Modules:
  0.0 239.7 jit_solution(4200298776029856514)
XLA Ops:
  7.2 1.4 fusion.55
  11.2 1.3 fusion.54
  13.8 3.4 %add_convert_fusion.3 = bf16[1,1024,256]{2,1,0:T(8,128)(2,1)} fusion(bf16[3,1024,256]{2,1,0:T(8,128)(2,1)} %param.11, s32[]{:T(128)S(6)} %select_n.56, f32[]{:T(128)} %bitcast.10, s32[]{:T(128)S(6)} %select_n.55, f32[]{:T(128)} %bitcast.8), kind=kLoop, calls=%fused_computation.34 | loop fusion | flops 1572864 | bytes 1572880 | tf_op jit(solution)/shard_map/convert_element_type | solution.py:77
  17.3 0.3 copy.33
  17.6 2.0 fusion.57
  19.6 3.6 %copy.46 = f32[20,2,128,128]{2,0,1,3:T(8,128)} copy(f32[20,2,128,128]{3,2,1,0:T(8,128)} %fusion.57) | data formatting | bytes 5242880 | tf_op jit(solution)/shard_map/tre,rkde->trkd/dot_general | solution.py:95
  23.1 3.3 %bitcast_convert_fusion = bf16[32,128,128]{2,0,1:T(8,128)(2,1)S(1)} fusion(f32[20,2,128,128]{2,0,1,3:T(8,128)} %copy.46, s32[20,2]{0,1:T(2,128)S(1)} %copy-done.11), kind=kOutput, calls=%fused_computation.12 | convolution fusion | flops 252183808 | bytes 3670176 | tf_op jit(solution)/shard_map/trkd,rkc->tcd/dot_general | solution.py:101
  26.5 1.5 copy.67
  27.9 2.0 collective-permute-start.1
  30.1 0.1 copy.32
  30.2 0.1 copy.25
  30.7 2.2 copy.26
  32.8 3.6 %fusion.56 = f32[20,2,128,128]{3,2,1,0:T(8,128)} fusion(bf16[20,2,128,128]{3,2,1,0:T(8,128)(2,1)} %param.14, bf16[128,20,128,1]{0,2,3,1:T(8,128)(2,1)} %bitcast.130), kind=kOutput, calls=%fused_computation.79 | convolution fusion | flops 167772160 | bytes 4587520 | tf_op jit(solution)/shard_map/trd,rkde->trke/dot_general | solution.py:79
  36.4 3.6 %copy.40 = f32[20,2,128,128]{2,0,1,3:T(8,128)} copy(f32[20,2,128,128]{3,2,1,0:T(8,128)} %fusion.56) | data formatting | bytes 5242880 | tf_op jit(solution)/shard_map/trd,rkde->trke/dot_general | solution.py:79
  40.0 3.0 %fusion.22 = bf16[8,128,128]{2,0,1:T(8,128)(2,1)S(1)} fusion(f32[20,2,128,128]{2,0,1,3:T(8,128)} %copy.40, s32[20,2]{0,1:T(2,128)S(1)} %copy-done.10, s32[8]{0:T(128)S(1)} %iota_add_fusion), kind=kOutput, calls=%fused_computation.29 | convolution fusion | flops 63045952 | bytes 2883776 | tf_op jit(solution)/shard_map/trke,rkc->tce/dot_general | solution.py:84
  43.0 43.8 %all-gather.3.cloned.1.call-done = bf16[1,1024,4096]{2,1,0:T(8,128)(2,1)} async-done(((bf16[1,1024,256]{2,1,0:T(8,128)(2,1)}), bf16[1,1024,4096]{2,1,0:T(8,128)(2,1)}) %all-gather.3.cloned.1.call-update) | async-done | bytes 8388624 | tf_op jit(solution)/shard_map/all_gather | solution.py:19
  86.8 5.8 %fusion.4 = bf16[128,4096]{1,0:T(8,128)(2,1)} fusion(bf16[1,1024,4096]{2,1,0:T(8,128)(2,1)} %all-gather.3.cloned.1.call-done, bf16[16,8,8,128]{3,2,1,0:T(8,128)(2,1)S(1)} %bitcast.137), kind=kOutput, calls=%fused_computation.6 | convolution fusion | flops 1074266112 | bytes 9699328 | tf_op jit(solution)/shard_map/dot_general | solution.py:87
  92.6 4.1 %fusion.25 = bf16[128,1024]{1,0:T(8,128)(2,1)S(1)} fusion(bf16[1,1024,4096]{2,1,0:T(8,128)(2,1)S(1)} %copy-done.1, bf16[128,4096]{1,0:T(8,128)(2,1)} %collective-permute-done.1, bf16[16,8,32,128]{3,2,1,0:T(8,128)(2,1)S(1)} %bitcast.125), kind=kOutput, calls=%fused_computation.30 | convolution fusion | flops 1075970048 | bytes 10747904 | tf_op jit(solution)/shard_map/to,fo->tf/dot_general | solution.py:105
  96.8 26.1 %all_gather.7 = bf16[128,2048]{1,0:T(8,128)(2,1)S(1)} all-gather(bf16[128,1024]{1,0:T(8,128)(2,1)S(1)} %fusion.25), channel_id=1, replica_groups=mesh['xh'=2,'y'=4,'z'=8,'c'=2,'xl'=2] {'xl'}, dimensions={1}, use_global_device_ids=true | all-gather | bytes 786432 | tf_op jit(solution)/shard_map/all_gather | solution.py:108
  122.9 0.1 copy_bitcast_fusion.2
  123.0 1.5 gather_fusion.1
  124.5 1.5 fusion.29
  126.1 1.0 copy-done.5
  127.1 1.9 copy_bitcast_fusion.1
  129.0 1.8 gather_fusion
  130.8 2.4 %copy.29 = bf16[20,2,128,128]{2,3,1,0:T(8,128)(2,1)} copy(bf16[20,2,128,128]{3,2,1,0:T(8,128)(2,1)} %bitcast.128) | data formatting | bytes 2621440 | tf_op jit(solution)/shard_map/jit(_take)/gather | solution.py:89
  133.2 1.9 fusion.15
  135.1 1.5 copy-done.2
  136.7 1.0 pad_maximum_fusion.2
  137.7 1.1 collective-permute-start.2
  138.9 1.4 constant_dynamic-slice_fusion
  140.3 1.1 collective-permute-done.2
  141.4 1.4 fusion.11
  142.8 0.2 reshape.90
  143.0 38.0 %all_to_all.10 = bf16[64,60,128]{2,1,0:T(8,128)(2,1)S(1)} all-to-all(bf16[64,60,128]{2,1,0:T(8,128)(2,1)S(1)} %reshape.90), channel_id=1, replica_groups=mesh['xh'=2,'y'=4,'z'=8,'c'=2,'xl'=2] {'xh','y','z'}, dimensions={0} | all-to-all | bytes 1966080 | tf_op jit(solution)/shard_map/all_to_all | solution.py:42
  180.9 0.2 convert_reduce_fusion
  181.1 0.2 broadcast_in_dim.40
  181.4 34.7 %all_to_all.11 = bf16[64,60,128]{2,1,0:T(8,128)(2,1)} all-to-all(bf16[64,60,128]{2,1,0:T(8,128)(2,1)S(1)} %broadcast_in_dim.40), channel_id=1, replica_groups=mesh['xh'=2,'y'=4,'z'=8,'c'=2,'xl'=2] {'xh','y','z'}, dimensions={0} | all-to-all | bytes 1966080 | tf_op jit(solution)/shard_map/all_to_all | solution.py:45
  216.2 2.2 reshape.91
  218.4 4.0 %collective-permute-start.3 = (bf16[3840,128]{1,0:T(8,128)(2,1)}, bf16[3840,128]{1,0:T(8,128)(2,1)}, u32[]{:S(2)}, u32[]{:S(2)}) collective-permute-start(bf16[3840,128]{1,0:T(8,128)(2,1)} %reshape.91), channel_id=1, source_target_pairs={{0,2},{2,0},{1,3},{3,1},{4,6},{6,4},{5,7},{7,5},{8,10},{10,8},{9,1... | collective-permute-start | bytes 2949128 | tf_op jit(solution)/shard_map/ppermute | solution.py:46
  222.3 2.2 fusion.21
  224.6 1.9 copy.38
  226.4 0.6 fusion.14
  227.1 1.1 copy.37
  228.2 0.2 copy-done.7
  228.3 1.5 select_convert_fusion.1
  230.1 1.7 pad_maximum_fusion
  231.7 1.1 pad_maximum_fusion.1
  (45 shorter events, 1.1 us)
Async XLA Ops:
  7.2 10.4 %copy-start = (bf16[20,2,128,128]{3,2,1,0:T(8,128)(2,1)S(1)}, bf16[20,2,128,128]{3,2,1,0:T(8,128)(2,1)}, u32[]{:S(2)}) copy-start(bf16[20,2,128,128]{3,2,1,0:T(8,128)(2,1)} %param.16) | copy-start | bytes 3932164
  7.2 10.1 %copy-start.9 = (bf16[128,2560]{1,0:T(8,128)(2,1)S(1)}, bf16[128,2560]{1,0:T(8,128)(2,1)}, u32[]{:S(2)}) copy-start(bf16[128,2560]{1,0:T(8,128)(2,1)} %param.10) | copy-start | bytes 1966084
  7.2 79.6 %all-gather.3.cloned.1.call-start = ((), (), s32[]{:S(2)}) async-start(), calls=%async_computation.2 | async-start | bytes 8912896 | tf_op jit(solution)/shard_map/all_gather | solution.py:19
  19.6 3.6 %copy-start.11 = (s32[20,2]{0,1:T(2,128)S(1)}, s32[20,2]{0,1:T(2,128)}, u32[]{:S(2)}) copy-start(s32[20,2]{0,1:T(2,128)} %param.17) | copy-start | bytes 484
  26.5 3.5 %copy-start.10 = (s32[20,2]{0,1:T(2,128)S(1)}, s32[20,2]{0,1:T(2,128)}, u32[]{:S(2)}) copy-start(s32[20,2]{0,1:T(2,128)} %param.15) | copy-start | bytes 484
  27.9 64.7 %collective-permute-start.1 = (bf16[128,4096]{1,0:T(8,128)(2,1)}, bf16[128,4096]{1,0:T(8,128)(2,1)}, u32[]{:S(2)}, u32[]{:S(2)}) collective-permute-start(bf16[128,4096]{1,0:T(8,128)(2,1)} %bitcast.123), channel_id=1, source_target_pairs={{0,1},{1,0},{2,3},{3,2},{4,5},{5,4},{6,7},{7,6},{8,9},{9,8},{10,11... | collective-permute-start | bytes 3145736 | tf_op jit(solution)/shard_map/ppermute | solution.py:23
  86.8 5.8 %copy-start.1 = (bf16[1,1024,4096]{2,1,0:T(8,128)(2,1)S(1)}, bf16[1,1024,4096]{2,1,0:T(8,128)(2,1)}, u32[]{:S(2)}) copy-start(bf16[1,1024,4096]{2,1,0:T(8,128)(2,1)} %all-gather.3.cloned.1.call-done) | copy-start | bytes 25165828
  92.6 34.5 %collective-permute-start = (bf16[128,4096]{1,0:T(8,128)(2,1)}, bf16[128,4096]{1,0:T(8,128)(2,1)}, u32[]{:S(2)}, u32[]{:S(2)}) collective-permute-start(bf16[128,4096]{1,0:T(8,128)(2,1)} %fusion.4), channel_id=1, source_target_pairs={{0,1},{1,0},{2,3},{3,2},{4,5},{5,4},{6,7},{7,6},{8,9},{9,8},{10,11... | collective-permute-start | bytes 3145736 | tf_op jit(solution)/shard_map/ppermute | solution.py:23
  96.8 27.8 %copy-start.4 = (bf16[128,2560]{0,1:T(8,128)(2,1)S(1)}, bf16[128,2560]{0,1:T(8,128)(2,1)}, u32[]{:S(2)}) copy-start(bf16[128,2560]{0,1:T(8,128)(2,1)} %copy.26) | copy-start | bytes 1966084
  126.0 1.1 copy-start.5
  135.1 1.5 copy-start.2
  136.6 2.2 copy-start.6
  137.7 3.7 %collective-permute-start.2 = (bf16[3840,128]{1,0:T(8,128)(2,1)}, bf16[3840,128]{1,0:T(8,128)(2,1)}, u32[]{:S(2)}, u32[]{:S(2)}) collective-permute-start(bf16[3840,128]{1,0:T(8,128)(2,1)} %pad_maximum_fusion.2), channel_id=1, source_target_pairs={{0,2},{2,0},{1,3},{3,1},{4,6},{6,4},{5,7},{7,5},{8,10},{10,8},{9,1... | collective-permute-start | bytes 2949128 | tf_op jit(solution)/shard_map/ppermute | solution.py:38
  181.4 40.9 %copy-start.8 = (bf16[20,128,128]{2,1,0:T(8,128)(2,1)S(1)}, bf16[20,128,128]{2,1,0:T(8,128)(2,1)}, u32[]{:S(2)}) copy-start(bf16[20,128,128]{2,1,0:T(8,128)(2,1)} %gather_fusion.1) | copy-start | bytes 1966084
  216.2 10.3 %copy-start.3 = (bf16[20,2,128,128]{2,3,1,0:T(8,128)(2,1)S(1)}, bf16[20,2,128,128]{2,3,1,0:T(8,128)(2,1)}, u32[]{:S(2)}) copy-start(bf16[20,2,128,128]{2,3,1,0:T(8,128)(2,1)} %copy.29) | copy-start | bytes 3932164
  218.4 9.8 %collective-permute-start.3 = (bf16[3840,128]{1,0:T(8,128)(2,1)}, bf16[3840,128]{1,0:T(8,128)(2,1)}, u32[]{:S(2)}, u32[]{:S(2)}) collective-permute-start(bf16[3840,128]{1,0:T(8,128)(2,1)} %reshape.91), channel_id=1, source_target_pairs={{0,2},{2,0},{1,3},{3,1},{4,6},{6,4},{5,7},{7,5},{8,10},{10,8},{9,1... | collective-permute-start | bytes 2949128 | tf_op jit(solution)/shard_map/ppermute | solution.py:46
  227.1 1.3 copy-start.7
Sparse Core Ops, SparseCore 0:
  17.4 69.4 all-gather.2

commit v2 on v1

v2 whole, which is shorter than its diff:
```python
import jax
import jax.numpy as jnp
from jax import lax
from jax.experimental import pallas as pl
from jax.experimental.pallas import tpu as pltpu
from jax.sharding import Mesh
from jax.sharding import PartitionSpec as P

HEAD = 128
D_OLD = 4096
HG_OLD = 16
HG_NEW = 20
L_OLD = 3
DEPTH_K = 2
BO_OLD = 32
PAIR = [(0, 1), (1, 0)]


def swap_cores(x):
    return lax.ppermute(x, "c", PAIR)


def swap_halves(x):
    return lax.ppermute(x, "xl", PAIR)


def add_pair(mine, other):
    return (mine.astype(jnp.float32) + other.astype(jnp.float32)).astype(jnp.bfloat16)


def arrival_place(cols):
    shard = cols // 2
    away = (shard // 2 - lax.axis_index("z")) % lax.axis_size("z")
    base = jnp.where(away < 4, 8 * away, 60 - 8 * away)
    return base + 2 * (shard % 2 != lax.axis_index("c")) + cols % 2


def forward(x, piece):
    if isinstance(piece, tuple):
        half = piece[0].shape[0]
        return forward(x[:, :half], piece[0]) + forward(x[:, half:], piece[1])
    return jnp.dot(x, piece, preferred_element_type=jnp.float32)


def backward(g, piece):
    if isinstance(piece, tuple):
        return jnp.concatenate([backward(g, part) for part in piece], axis=1)
    return lax.dot_general(
        g, piece, (((1,), (1,)), ((), ())), preferred_element_type=jnp.float32
    )


SMEM = pl.BlockSpec(memory_space=pltpu.SMEM)


def times(x, w, dims):
    return lax.dot_general(x, w, (dims, ((), ())), preferred_element_type=jnp.float32)


def scatter_blocks(x, blocks, place, slots, used, transposed):
    rows = blocks.shape[0]
    tok = x.shape[0]

    def kernel(place_ref, x_ref, w_ref, o_ref, acc_ref):
        acc_ref[...] = jnp.zeros_like(acc_ref)
        for r in range(rows):
            xr = x_ref[:, r * HEAD : (r + 1) * HEAD]
            if transposed:
                both = times(xr, w_ref[r].reshape(2 * HEAD, HEAD), ((1,), (1,)))
            else:
                both = times(xr, jnp.concatenate([w_ref[r, 0], w_ref[r, 1]], 1), ((1,), (0,)))
            for k in range(2):
                c = place_ref[r, k]
                acc_ref[c] = acc_ref[c] + both[:, k * HEAD : (k + 1) * HEAD]
        for c in range(used):
            o_ref[:, c * HEAD : (c + 1) * HEAD] = acc_ref[c].astype(jnp.bfloat16)

    full = pl.BlockSpec(memory_space=pltpu.VMEM)
    return pl.pallas_call(
        kernel,
        out_shape=jax.ShapeDtypeStruct((tok, used * HEAD), jnp.bfloat16),
        in_specs=[SMEM, full, full],
        out_specs=full,
        scratch_shapes=[pltpu.VMEM((slots, tok, HEAD), jnp.float32)],
    )(place, x, blocks)


def stage(dst, at, mine, other=None):
    for c in range(mine.shape[1] // HEAD):
        cols = slice(c * HEAD, (c + 1) * HEAD)
        block = mine[:, cols]
        if other is not None:
            block = add_pair(block, other[:, cols])
        dst[at + c] = block
    return at + mine.shape[1] // HEAD


def stage_all(chunk_refs, hg_refs, sel_ref, hg_ref):
    at = 0
    for i in range(0, len(chunk_refs), 2):
        at = stage(sel_ref, at, chunk_refs[i], chunk_refs[i + 1])
    stage(hg_ref, stage(hg_ref, 0, hg_refs[0]), hg_refs[1])


def local_grads(where, out_place, in_place, chunks, hidden_grads, attn_out, cotangent):
    tok = cotangent.shape[0]
    n_out, n_in = out_place.shape[0], in_place.shape[0]
    half_out, half_in = n_out // 2, n_in // 2
    pairs = 2 * (half_out + half_in)
    n_chunks = len(chunks)

    def kernel(where_ref, out_ref, in_ref, *refs):
        chunk_refs, refs = refs[:n_chunks], refs[n_chunks:]
        hg0, hg1, attn_ref, cot_ref, keep_ref, send_ref, sel, hg, attn, cot = refs
        stage_all(chunk_refs, (hg0, hg1), sel, hg)
        stage(attn, 0, attn_ref)
        stage(cot, 0, cot_ref)
        for which in range(2):
            core = (where_ref[0] + which) % 2
            dst = (keep_ref, send_ref)[which]
            at = 0
            for i in range(half_in):
                r = core * half_in + i
                rhs = jnp.concatenate([hg[in_ref[r, 0]], hg[in_ref[r, 1]]], 1)
                both = times(attn[r], rhs, ((0,), (0,))).astype(dst.dtype)
                for k in range(2):
                    dst[at : at + HEAD, :] = both[:, k * HEAD : (k + 1) * HEAD]
                    at += HEAD
            for i in range(half_out):
                r = core * half_out + i
                lhs = jnp.concatenate([sel[out_ref[r, 0]], sel[out_ref[r, 1]]], 1)
                dst[at : at + 2 * HEAD, :] = times(lhs, cot[r], ((0,), (0,))).astype(dst.dtype)
                at += 2 * HEAD

    def whole(x):
        return pl.BlockSpec(x.shape, lambda i, *_: (0,) * x.ndim)

    arrays = [*chunks, *hidden_grads]
    out_spec = pl.BlockSpec((pairs * HEAD, HEAD), lambda i, *_: (0, 0))
    return pl.pallas_call(
        kernel,
        grid_spec=pltpu.PrefetchScalarGridSpec(
            num_scalar_prefetch=3,
            grid=(1,),
            in_specs=[
                *[whole(x) for x in arrays],
                pl.BlockSpec((tok, n_in * HEAD), lambda i, w, *_: (0, w[1])),
                whole(cotangent),
            ],
            out_specs=[out_spec, out_spec],
            scratch_shapes=[
                pltpu.VMEM((BO_OLD, tok, HEAD), jnp.bfloat16),
                pltpu.VMEM((HG_OLD, tok, HEAD), jnp.bfloat16),
                pltpu.VMEM((n_in, tok, HEAD), jnp.bfloat16),
                pltpu.VMEM((n_out, tok, HEAD), jnp.bfloat16),
            ],
        ),
        out_shape=[
            jax.ShapeDtypeStruct((pairs * HEAD, HEAD), jnp.float32),
            jax.ShapeDtypeStruct((pairs * HEAD, HEAD), jnp.bfloat16),
        ],
    )(where, out_place, in_place, *arrays, attn_out, cotangent)


def local_outputs(where, out_place, in_place, chunks, hidden_grads, out_blocks, in_blocks):
    tok = chunks[0].shape[0]
    n_out, n_in = out_place.shape[0], in_place.shape[0]
    n_chunks = len(chunks)

    def kernel(where_ref, out_ref, in_ref, *refs):
        chunk_refs, refs = refs[:n_chunks], refs[n_chunks:]
        hg0, hg1, wo_ref, wi_ref, grown_ref, grad_ref, sel, hg = refs
        stage_all(chunk_refs, (hg0, hg1), sel, hg)
        for r in range(n_out):
            x = jnp.concatenate([sel[out_ref[r, 0]], sel[out_ref[r, 1]]], 1)
            y = times(x, wo_ref[r].reshape(2 * HEAD, HEAD), ((1,), (0,)))
            grown_ref[:, r * HEAD : (r + 1) * HEAD] = y.astype(jnp.bfloat16)
        for r in range(n_in):
            x = jnp.concatenate([hg[in_ref[r, 0]], hg[in_ref[r, 1]]], 1)
            w = jnp.concatenate([wi_ref[r, 0], wi_ref[r, 1]], 1)
            y = times(x, w, ((1,), (1,)))
            grad_ref[:, r * HEAD : (r + 1) * HEAD] = y.astype(jnp.bfloat16)

    def whole(x):
        return pl.BlockSpec(x.shape, lambda i, *_: (0,) * x.ndim)

    arrays = [*chunks, *hidden_grads]
    return pl.pallas_call(
        kernel,
        grid_spec=pltpu.PrefetchScalarGridSpec(
            num_scalar_prefetch=3,
            grid=(1,),
            in_specs=[
                *[whole(x) for x in arrays],
                whole(out_blocks),
                pl.BlockSpec((n_in, 2, HEAD, HEAD), lambda i, w, *_: (w[1], 0, 0, 0)),
            ],
            out_specs=[
                pl.BlockSpec((tok, n_out * HEAD), lambda i, *_: (0, 0)),
                pl.BlockSpec((tok, n_in * HEAD), lambda i, *_: (0, 0)),
            ],
            scratch_shapes=[
                pltpu.VMEM((BO_OLD, tok, HEAD), jnp.bfloat16),
                pltpu.VMEM((HG_OLD, tok, HEAD), jnp.bfloat16),
            ],
        ),
        out_shape=[
            jax.ShapeDtypeStruct((tok, n_out * HEAD), jnp.bfloat16),
            jax.ShapeDtypeStruct((tok, n_in * HEAD), jnp.bfloat16),
        ],
    )(where, out_place, in_place, *arrays, out_blocks, in_blocks)


def unpack_sums(where, mine, theirs, cut):
    rows = mine.shape[0]

    def kernel(where_ref, mine_ref, theirs_ref, in_ref, out_ref):
        for step, src in enumerate((mine_ref, theirs_ref)):

            @pl.when(pl.program_id(0) == step)
            def _():
                in_ref[0] = src[:cut, :].astype(jnp.float32)
                out_ref[0] = src[cut:, :].astype(jnp.float32)

    whole = pl.BlockSpec((rows, HEAD), lambda i, *_: (0, 0))
    return pl.pallas_call(
        kernel,
        grid_spec=pltpu.PrefetchScalarGridSpec(
            num_scalar_prefetch=1,
            grid=(2,),
            in_specs=[whole, whole],
            out_specs=[
                pl.BlockSpec((1, cut, HEAD), lambda i, w: ((w[0] + i) % 2, 0, 0)),
                pl.BlockSpec((1, rows - cut, HEAD), lambda i, w: ((w[0] + i) % 2, 0, 0)),
            ],
        ),
        out_shape=[
            jax.ShapeDtypeStruct((2, cut, HEAD), jnp.float32),
            jax.ShapeDtypeStruct((2, rows - cut, HEAD), jnp.float32),
        ],
    )(where, mine, theirs)


def token_sum(keep, send, scale):
    plane = ("xh", "y")
    n = lax.axis_size(plane)
    mine = (keep + swap_cores(send).astype(jnp.float32)).astype(jnp.bfloat16)
    rows = mine.shape[0]
    parts = lax.all_to_all(mine.reshape(n, rows // n, HEAD), plane, 0, 0, tiled=True)
    part = jnp.sum(parts.astype(jnp.float32), axis=0).astype(jnp.bfloat16)
    spread = jnp.broadcast_to(part[None], (lax.axis_size("z"),) + part.shape)
    parts = lax.all_to_all(spread, "z", 0, 0, tiled=True)
    part = (jnp.sum(parts.astype(jnp.float32), axis=0) * scale).astype(jnp.bfloat16)
    spread = jnp.broadcast_to(part[None], (n,) + part.shape)
    return lax.all_to_all(spread, plane, 0, 0, tiled=True).reshape(rows, HEAD)


def local(
    attn_out,
    cotangent,
    old_weights,
    depth_coef,
    depth_pick,
    in_blocks,
    in_cols,
    out_blocks,
    out_cols,
):
    tie = lax.optimization_barrier
    tok_rows = attn_out.shape[0]
    core = lax.axis_index("c")
    tensor_half = lax.axis_index("xl")
    local_old = old_weights.shape[1]
    local_blocks = local_old // HEAD
    rows_in = HG_NEW // lax.axis_size("xl")
    where = jnp.stack([core, tensor_half]).astype(jnp.int32)
    out_place = arrival_place(out_cols).astype(jnp.int32)
    own = in_cols // local_blocks == tensor_half
    hidden_place = jnp.where(own, in_cols % local_blocks, local_blocks)
    in_place = in_cols % local_blocks + jnp.where(own, 0, local_blocks)
    in_place = lax.dynamic_slice_in_dim(in_place, tensor_half * rows_in, rows_in, 0)

    mixed = jnp.zeros(old_weights.shape[1:], jnp.float32)
    for layer in range(L_OLD):
        weight = jnp.sum(jnp.where(depth_pick == layer, depth_coef, 0.0))
        mixed = mixed + weight * old_weights[layer].astype(jnp.float32)
    mixed = mixed.astype(jnp.bfloat16)

    n = lax.axis_size("z")
    up = [(i, (i + 1) % n) for i in range(n)]
    down = [(i, (i - 1) % n) for i in range(n)]

    def hop(a, b):
        return lax.ppermute(a, "z", up), lax.ppermute(b, "z", down)

    def forward_chunk(pieces):
        part = jnp.concatenate([forward(hidden, p) for p in pieces], axis=1)
        return part.astype(jnp.bfloat16)

    def backward_chunk(at, pieces):
        total = 0.0
        for i, p in enumerate(pieces):
            cols = slice((at + 2 * i) * HEAD, (at + 2 * i + 2) * HEAD)
            total = total + backward(old_grad[:, cols], p)
        return total

    a, b = hop(mixed, mixed)
    chunk0 = [mixed, swap_cores(mixed)]
    grad_part = scatter_blocks(cotangent, out_blocks, out_place, BO_OLD, BO_OLD, True)
    a, b, grad_part, attn_tied = tie((a, b, grad_part, attn_out))
    chunk1 = [a, swap_cores(a), b, swap_cores(b)]
    a, b = hop(a, b)
    grad_other = swap_halves(grad_part)
    hidden = scatter_blocks(
        attn_tied, in_blocks, hidden_place, local_blocks + 1, local_blocks, False
    )
    a, b, hidden = tie((a, b, hidden))
    chunk2 = [a, swap_cores(a), b, swap_cores(b)]
    a, b = hop(a, b)
    parts = [forward_chunk(chunk0), forward_chunk(chunk1)]
    a, b, parts[0], parts[1], hidden = tie((a, b, parts[0], parts[1], hidden))
    chunk3 = [a, swap_cores(a), b, swap_cores(b)]
    half = local_old // 2
    a, b = hop(a[:half], b[half:])
    chunk4 = [(a, b), (swap_cores(a), swap_cores(b))]
    chunks = [parts[0], swap_halves(parts[0]), parts[1], swap_halves(parts[1])]
    old_grad = add_pair(grad_part, grad_other)
    hidden_grad = 0.0
    for at, pieces in ((4, chunk1), (12, chunk2), (20, chunk3), (28, chunk4)):
        if at > 4:
            part = forward_chunk(pieces)
            chunks += [part, swap_halves(part)]
        else:
            hidden_grad = backward_chunk(0, chunk0)
        hidden_grad = hidden_grad + backward_chunk(at, pieces)
    hidden_grad = hidden_grad.astype(jnp.bfloat16)
    hidden_grads = [hidden_grad, swap_halves(hidden_grad)]
    keep, send = local_grads(
        where, out_place, in_place, chunks, hidden_grads, attn_out, cotangent
    )
    grown_out, grad_attn = local_outputs(
        where, out_place, in_place, chunks, hidden_grads, out_blocks, in_blocks
    )
    grad_scale = float(tok_rows * lax.axis_size(("xh", "y", "z", "c"))) ** (-0.5)
    full = token_sum(keep, send, grad_scale)
    in_sum, out_sum = unpack_sums(where, full, swap_cores(full), rows_in * HEAD)
    in_sum = in_sum.reshape(rows_in, 2, HEAD, HEAD)
    out_sum = out_sum.reshape(out_cols.shape[0], 2, HEAD, HEAD)
    return (grown_out, grad_attn, in_sum, out_sum)


def solution(mesh):
    fine = Mesh(mesh.devices.reshape(2, 4, 8, 2, 2), ("xh", "y", "z", "c", "xl"))
    tokens = ("xh", "y", "z", "c")
    placed = (
        P(tokens, None),
        P(tokens, "xl"),
        P(None, "xl", ("z", "c")),
        P(),
        P(),
        P(),
        P(),
        P("xl", None, None, None),
        P("xl", None),
    )
    return jax.shard_map(
        local,
        mesh=fine,
        in_specs=placed,
        out_specs=(
            P(tokens, "xl"),
            P(tokens, "xl"),
            P("xl", None, None, None),
            P("xl", None, None, None),
        ),
        check_vma=False,
    )
```

time: 241 us -> 200 us (0.83)
  blocking collectives: 98.8 us -> 68.2 us
  local copies, waits for them, and re-layouts: 30.4 us -> 3.55 us
  starting transfers between devices: 7.18 us -> 32.5 us
  Pallas kernels: 0 us -> 21.2 us
  between operations: 18.2 us -> 1.23 us
  matrix products: 28 us -> 19.5 us
  other arithmetic: 12.2 us -> 9.67 us
    all_gather x1 -> x0, waiting for transfers between devices: 43.8 us -> none  [gathered_mix(): return lax.all_gather(mixed_weight, ('z', 'c'), axis=1, tiled=True)]
    ppermute x4 -> x26, waiting for transfers between devices: 1.07 us -> 43.5 us  [the longest x8 24.8 us: hop(): return (lax.ppermute(a, 'z', up), lax.ppermute(b, 'z', down))]
    all_gather x1 -> x0, blocking collectives: 26.1 us -> none  [local(): hidden_grad = lax.all_gather(hidden_grad_local, 'xl', axis=1, tiled=True)]
    ppermute x4 -> x26, starting transfers between devices: 7.14 us -> 32.5 us  [the longest x11 14.1 us: swap_cores(): return lax.ppermute(x, 'c', PAIR)]
    pallas_call x0 -> x5, Pallas kernels: none -> 21.2 us  [the longest x2 6.16 us: scatter_blocks(): pl.pallas_call(kernel, out_shape=jax.ShapeDtypeStruct((tok, used * HEAD),...]
    dot_general x10 -> x36, matrix products: 28 us -> 19.5 us  [the longest x18 10.2 us: forward(): return jnp.dot(x, piece, preferred_element_type=jnp.float32)]
    dot_general x2 -> x0, local copies, waits for them, and re-layouts: 7.13 us -> none  [the longest x1 3.57 us: local(): jnp.einsum('tre,rkde->trkd', cot_blocks, out_blocks, preferred_element_ty...]
    unnamed x29 -> x38, local copies, waits for them, and re-layouts: 9.58 us -> 3.26 us
  transfers between devices with their start and end apart: 5 -> 26, of which waited for: 2 -> 7; matrix products, arithmetic and copies ran while one was open for 18% -> 11% of each run, Pallas kernels for 0% -> 6%
where the time goes in v2:
time: 200 us; the launch traced here: 199 us
  blocking collectives  68.2 us (34%)
  waiting for transfers between devices  43.5 us (22%)
  starting transfers between devices  32.5 us (16%)
  Pallas kernels  21.2 us (11%)
  matrix products  19.5 us (10%)
  other arithmetic  9.67 us (5%)
  local copies, waits for them, and re-layouts  3.55 us (2%)
    all_to_all x1, blocking collectives, token_sum(): parts = lax.all_to_all(spread, 'z', 0, 0, tiled=True)  29.2 us
    ppermute x8, waiting for transfers between devices, hop(): return (lax.ppermute(a, 'z', up), lax.ppermute(b, 'z', down))  24.8 us
    all_to_all x1, blocking collectives, token_sum(): lax.all_to_all(mine.reshape(n, rows // n, HEAD), plane, 0, 0, tiled=True)  21.5 us
    all_to_all x1, blocking collectives, token_sum(): return lax.all_to_all(spread, plane, 0, 0, tiled=True).reshape(rows, HEAD)  17.4 us
    ppermute x7, waiting for transfers between devices, swap_halves(): return lax.ppermute(x, 'xl', PAIR)  16 us
    ppermute x11, starting transfers between devices, swap_cores(): return lax.ppermute(x, 'c', PAIR)  14.1 us
    ppermute x8, starting transfers between devices, hop(): return (lax.ppermute(a, 'z', up), lax.ppermute(b, 'z', down))  12.5 us
    dot_general x18, matrix products, forward(): return jnp.dot(x, piece, preferred_element_type=jnp.float32)  10.2 us
  transfers between devices with their start and end apart: 26, of which 7 were waited for; matrix products, arithmetic and copies ran while one was open for 11% of the time, Pallas kernels for 6%

profile of v2, /device:TPU:1, one launch (start us, length us, event | category | flops | bytes accessed | tf_op | source)
XLA Modules:
  0.0 199.3 jit_solution(12795099285775591832)
XLA Ops:
  0.6 1.3 fusion.62
  1.9 3.6 %fusion.13 = bf16[1024,256]{1,0:T(8,128)(2,1)S(1)} fusion(bf16[3,1024,256]{2,1,0:T(8,128)(2,1)} %param.11, f32[]{:T(128)} %get-tuple-element.41, f32[]{:T(128)} %get-tuple-element.42, f32[]{:T(128)} %get-tuple-element.40), kind=kLoop, calls=%fused_computation.37 | loop fusion | flops 2359296 | bytes 2097164 | tf_op jit(solution)/shard_map/add | solution.py:286
  5.5 2.5 %collective-permute-start = (bf16[1024,256]{1,0:T(8,128)(2,1)S(1)}, bf16[1024,256]{1,0:T(8,128)(2,1)}, u32[]{:S(2)}, u32[]{:S(2)}) collective-permute-start(bf16[1024,256]{1,0:T(8,128)(2,1)S(1)} %fusion.13), channel_id=1, source_target_pairs={{0,4},{4,8},{8,12},{12,16},{16,20},{20,24},{24,28},{28,0},{1,5},{5... | collective-permute-start | bytes 1572872 | tf_op jit(solution)/shard_map/ppermute | solution.py:294
  8.1 4.0 %collective-permute-start.1 = (bf16[1024,256]{1,0:T(8,128)(2,1)S(1)}, bf16[1024,256]{1,0:T(8,128)(2,1)S(1)}, u32[]{:S(2)}, u32[]{:S(2)}) collective-permute-start(bf16[1024,256]{1,0:T(8,128)(2,1)S(1)} %fusion.13), channel_id=1, source_target_pairs={{0,28},{4,0},{8,4},{12,8},{16,12},{20,16},{24,20},{28,24},{1,29},{... | collective-permute-start | bytes 1572872 | tf_op jit(solution)/shard_map/ppermute | solution.py:294
  12.2 0.6 fusion.55.place_ref.out_ref
  12.8 3.3 %shard_map.120 = bf16[128,4096]{1,0:T(8,128)(2,1)} custom-call(s32[20,2]{1,0:T(8,128)} %fusion.55.place_ref.out_ref, bf16[128,2560]{1,0:T(8,128)(2,1)} %refs_13_.3, bf16[20,2,128,128]{3,2,1,0:T(8,128)(2,1)} %refs_12_.2), custom_call_target="tpu_custom_call" | custom-call | tf_op jit(solution)/shard_map/pallas_call | solution.py:79
  16.2 7.6 %collective-permute-done = bf16[1024,256]{1,0:T(8,128)(2,1)} collective-permute-done((bf16[1024,256]{1,0:T(8,128)(2,1)S(1)}, bf16[1024,256]{1,0:T(8,128)(2,1)}, u32[]{:S(2)}, u32[]{:S(2)}) %collective-permute-start) | collective-permute-done | bytes 524320 | tf_op jit(solution)/shard_map/ppermute | solution.py:294
  23.7 2.7 %collective-permute-start.3 = (bf16[1024,256]{1,0:T(8,128)(2,1)S(1)}, bf16[1024,256]{1,0:T(8,128)(2,1)S(1)}, u32[]{:S(2)}, u32[]{:S(2)}) collective-permute-start(bf16[1024,256]{1,0:T(8,128)(2,1)S(1)} %collective-permute-done.1), channel_id=1, source_target_pairs={{0,28},{4,0},{8,4},{12,8},{16,12},{20,16},{24,20},{28,24},{1,29},{... | collective-permute-start | bytes 1572872 | tf_op jit(solution)/shard_map/ppermute | solution.py:294
  26.4 1.8 collective-permute-start.6
  29.5 2.8 %shard_map.121 = bf16[128,1024]{1,0:T(8,128)(2,1)} custom-call(s32[20,2]{1,0:T(8,128)} %get-tuple-element.43.place_ref, bf16[128,2560]{1,0:T(8,128)(2,1)} %refs_12_.3, bf16[20,2,128,128]{3,2,1,0:T(8,128)(2,1)} %refs_13_.2), custom_call_target="tpu_custom_call" | custom-call | tf_op jit(solution)/shard_map/pallas_call | solution.py:79
  32.3 5.2 %collective-permute-done.2 = bf16[1024,256]{1,0:T(8,128)(2,1)} collective-permute-done((bf16[1024,256]{1,0:T(8,128)(2,1)}, bf16[1024,256]{1,0:T(8,128)(2,1)}, u32[]{:S(2)}, u32[]{:S(2)}) %collective-permute-start.2) | collective-permute-done | bytes 524320 | tf_op jit(solution)/shard_map/ppermute | solution.py:294
  37.5 1.2 collective-permute-start.22
  38.7 1.4 convolution_convert_fusion.11
  40.1 1.2 convolution_convert_fusion.9
  41.3 2.5 %collective-permute-start.12 = (bf16[1024,256]{1,0:T(8,128)(2,1)S(1)}, bf16[1024,256]{1,0:T(8,128)(2,1)S(1)}, u32[]{:S(2)}, u32[]{:S(2)}) collective-permute-start(bf16[1024,256]{1,0:T(8,128)(2,1)S(1)} %collective-permute-done.3), channel_id=1, source_target_pairs={{0,2},{2,0},{1,3},{3,1},{4,6},{6,4},{5,7},{7,5},{8,10},{10,8},{9,1... | collective-permute-start | bytes 1572872 | tf_op jit(solution)/shard_map/ppermute | solution.py:20
  43.7 1.2 convolution_convert_fusion.13
  44.9 1.2 collective-permute-start.5
  46.2 1.3 convolution_convert_fusion.10
  48.2 0.7 collective-permute-start.11
  48.8 1.3 convolution_convert_fusion.8
  50.1 12.0 %collective-permute-done.4 = bf16[1024,256]{1,0:T(8,128)(2,1)S(1)} collective-permute-done((bf16[1024,256]{1,0:T(8,128)(2,1)}, bf16[1024,256]{1,0:T(8,128)(2,1)S(1)}, u32[]{:S(2)}, u32[]{:S(2)}) %collective-permute-start.4) | collective-permute-done | bytes 524320 | tf_op jit(solution)/shard_map/ppermute | solution.py:294
  62.2 1.2 collective-permute-start.15
  64.1 1.3 convolution_convert_fusion.7
  66.1 1.5 collective-permute-start.17
  68.8 1.0 collective-permute-start.13
  69.7 1.3 fusion.34
  71.1 1.3 fusion.38
  72.4 1.4 fusion.5
  74.4 1.4 fusion.3
  76.1 1.5 collective-permute-start.20
  79.5 1.0 collective-permute-start.9
  82.5 0.6 collective-permute-start.23
  83.6 1.0 collective-permute-start.16
  84.6 4.4 %collective-permute-done.9.refs_1_ = bf16[128,512]{1,0:T(8,128)(2,1)S(1)} collective-permute-done((bf16[128,512]{1,0:T(8,128)(2,1)S(1)}, bf16[128,512]{1,0:T(8,128)(2,1)S(1)}, u32[]{:S(2)}, u32[]{:S(2)}) %collective-permute-start.9) | collective-permute-done | bytes 131104 | tf_op jit(solution)/shard_map/ppermute | solution.py:24
  89.0 0.6 copy-done.14
  91.4 11.6 %collective-permute-done.21.refs_9_ = bf16[128,512]{1,0:T(8,128)(2,1)S(1)} collective-permute-done((bf16[128,512]{1,0:T(8,128)(2,1)S(1)}, bf16[128,512]{1,0:T(8,128)(2,1)S(1)}, u32[]{:S(2)}, u32[]{:S(2)}) %collective-permute-start.21) | collective-permute-done | bytes 131104 | tf_op jit(solution)/shard_map/ppermute | solution.py:24
  103.8 0.7 copy-done.12
  104.5 5.6 %shard_map.123 = (f32[3840,128]{1,0:T(8,128)}, bf16[3840,128]{1,0:T(8,128)(2,1)}) custom-call(s32[2]{0:T(128)} %pad_add_fusion.where_ref, s32[20,2]{1,0:T(8,128)} %fusion.55.place_ref.out_ref, s32[10,2]{1,0:T(8,128)} %dynamic-slice_add_fusion.in_ref, bf16[128,512]{1,0:T(8,128)(2,1)} %copy-done.7, bf16[128,512]{1,0:T(8,128)(2,1)} %copy-done.14, ...), custom_call_target="tpu_custom_call" | custom-call | tf_op jit(solution)/shard_map/pallas_call | solution.py:140
  110.2 1.2 collective-permute-start.24
  111.4 2.4 %collective-permute-done.24 = bf16[3840,128]{1,0:T(8,128)(2,1)S(1)} collective-permute-done((bf16[3840,128]{1,0:T(8,128)(2,1)}, bf16[3840,128]{1,0:T(8,128)(2,1)S(1)}, u32[]{:S(2)}, u32[]{:S(2)}) %collective-permute-start.24) | collective-permute-done | bytes 983072 | tf_op jit(solution)/shard_map/ppermute | solution.py:20
  113.8 1.7 add_convert_fusion.1
  115.6 21.5 %all_to_all.15 = bf16[8,480,128]{2,1,0:T(8,128)(2,1)S(1)} all-to-all(bf16[8,480,128]{2,1,0:T(8,128)(2,1)S(1)} %bitcast.60), channel_id=1, replica_groups=mesh['xh'=2,'y'=4,'z'=8,'c'=2,'xl'=2] {'xh','y'}, dimensions={0} | all-to-all | bytes 1966080 | tf_op jit(solution)/shard_map/all_to_all | solution.py:249
  137.4 29.2 %all_to_all.16 = bf16[8,480,128]{2,1,0:T(8,128)(2,1)S(1)} all-to-all(bf16[8,480,128]{2,1,0:T(8,128)(2,1)S(1)} %broadcast_in_dim.25), channel_id=1, replica_groups=mesh['xh'=2,'y'=4,'z'=8,'c'=2,'xl'=2] {'z'}, dimensions={0} | all-to-all | bytes 1966080 | tf_op jit(solution)/shard_map/all_to_all | solution.py:252
  166.9 17.4 %all_to_all.17 = bf16[8,480,128]{2,1,0:T(8,128)(2,1)S(1)} all-to-all(bf16[8,480,128]{2,1,0:T(8,128)(2,1)S(1)} %broadcast_in_dim.26), channel_id=1, replica_groups=mesh['xh'=2,'y'=4,'z'=8,'c'=2,'xl'=2] {'xh','y'}, dimensions={0} | all-to-all | bytes 1966080 | tf_op jit(solution)/shard_map/all_to_all | solution.py:255
  184.3 4.6 %collective-permute-start.25 = (bf16[3840,128]{1,0:T(8,128)(2,1)S(1)}, bf16[3840,128]{1,0:T(8,128)(2,1)S(1)}, u32[]{:S(2)}, u32[]{:S(2)}) collective-permute-start(bf16[3840,128]{1,0:T(8,128)(2,1)S(1)} %bitcast.58), channel_id=1, source_target_pairs={{0,2},{2,0},{1,3},{3,1},{4,6},{6,4},{5,7},{7,5},{8,10},{10,8},{9,1... | collective-permute-start | bytes 2949128 | tf_op jit(solution)/shard_map/ppermute | solution.py:20
  188.9 5.1 %shard_map.122 = (bf16[128,2560]{1,0:T(8,128)(2,1)}, bf16[128,1280]{1,0:T(8,128)(2,1)}) custom-call(s32[2]{0:T(128)} %pad_add_fusion.where_ref, s32[20,2]{1,0:T(8,128)} %fusion.55.place_ref.out_ref, s32[10,2]{1,0:T(8,128)} %dynamic-slice_add_fusion.in_ref, bf16[128,512]{1,0:T(8,128)(2,1)} %copy-done.7, bf16[128,512]{1,0:T(8,128)(2,1)} %copy-done.14, ...), custom_call_target="tpu_custom_call" | custom-call | tf_op jit(solution)/shard_map/pallas_call | solution.py:188
  194.0 1.0 copy-done.13
  195.0 4.3 %shard_map.124 = (f32[2,1280,128]{2,1,0:T(8,128)}, f32[2,2560,128]{2,1,0:T(8,128)}) custom-call(s32[2]{0:T(128)} %pad_add_fusion.where_ref, bf16[3840,128]{1,0:T(8,128)(2,1)} %bitcast.59, bf16[3840,128]{1,0:T(8,128)(2,1)} %copy-done.13), custom_call_target="tpu_custom_call" | custom-call | tf_op jit(solution)/shard_map/pallas_call | solution.py:226
  (106 shorter events, 12.7 us)
Async XLA Ops:
  0.6 11.5 %copy-start.16 = (s32[20,2]{0,1:T(2,128)S(1)}, s32[20,2]{0,1:T(2,128)}, u32[]{:S(2)}) copy-start(s32[20,2]{0,1:T(2,128)} %param.17) | copy-start | bytes 484
  5.5 22.7 %copy-start.17 = (s32[20,2]{0,1:T(2,128)S(1)}, s32[20,2]{0,1:T(2,128)}, u32[]{:S(2)}) copy-start(s32[20,2]{0,1:T(2,128)} %param.15) | copy-start | bytes 484
  5.5 18.2 %collective-permute-start = (bf16[1024,256]{1,0:T(8,128)(2,1)S(1)}, bf16[1024,256]{1,0:T(8,128)(2,1)}, u32[]{:S(2)}, u32[]{:S(2)}) collective-permute-start(bf16[1024,256]{1,0:T(8,128)(2,1)S(1)} %fusion.13), channel_id=1, source_target_pairs={{0,4},{4,8},{8,12},{12,16},{16,20},{20,24},{24,28},{28,0},{1,5},{5... | collective-permute-start | bytes 1572872 | tf_op jit(solution)/shard_map/ppermute | solution.py:294
  8.1 15.7 %collective-permute-start.1 = (bf16[1024,256]{1,0:T(8,128)(2,1)S(1)}, bf16[1024,256]{1,0:T(8,128)(2,1)S(1)}, u32[]{:S(2)}, u32[]{:S(2)}) collective-permute-start(bf16[1024,256]{1,0:T(8,128)(2,1)S(1)} %fusion.13), channel_id=1, source_target_pairs={{0,28},{4,0},{8,4},{12,8},{16,12},{20,16},{24,20},{28,24},{1,29},{... | collective-permute-start | bytes 1572872 | tf_op jit(solution)/shard_map/ppermute | solution.py:294
  16.2 21.3 %copy-start.1 = (bf16[128,4096]{1,0:T(8,128)(2,1)S(1)}, bf16[128,4096]{1,0:T(8,128)(2,1)}, u32[]{:S(2)}) copy-start(bf16[128,4096]{1,0:T(8,128)(2,1)} %shard_map.120) | copy-start | bytes 3145732
  23.7 13.8 %collective-permute-start.2 = (bf16[1024,256]{1,0:T(8,128)(2,1)}, bf16[1024,256]{1,0:T(8,128)(2,1)}, u32[]{:S(2)}, u32[]{:S(2)}) collective-permute-start(bf16[1024,256]{1,0:T(8,128)(2,1)} %collective-permute-done), channel_id=1, source_target_pairs={{0,4},{4,8},{8,12},{12,16},{16,20},{20,24},{24,28},{28,0},{1,5},{5... | collective-permute-start | bytes 1572872 | tf_op jit(solution)/shard_map/ppermute | solution.py:294
  23.7 15.0 %collective-permute-start.3 = (bf16[1024,256]{1,0:T(8,128)(2,1)S(1)}, bf16[1024,256]{1,0:T(8,128)(2,1)S(1)}, u32[]{:S(2)}, u32[]{:S(2)}) collective-permute-start(bf16[1024,256]{1,0:T(8,128)(2,1)S(1)} %collective-permute-done.1), channel_id=1, source_target_pairs={{0,28},{4,0},{8,4},{12,8},{16,12},{20,16},{24,20},{28,24},{1,29},{... | collective-permute-start | bytes 1572872 | tf_op jit(solution)/shard_map/ppermute | solution.py:294
  26.4 21.1 %collective-permute-start.6 = (bf16[1024,256]{1,0:T(8,128)(2,1)S(1)}, bf16[1024,256]{1,0:T(8,128)(2,1)S(1)}, u32[]{:S(2)}, u32[]{:S(2)}) collective-permute-start(bf16[1024,256]{1,0:T(8,128)(2,1)S(1)} %fusion.13), channel_id=1, source_target_pairs={{0,2},{2,0},{1,3},{3,1},{4,6},{6,4},{5,7},{7,5},{8,10},{10,8},{9,1... | collective-permute-start | bytes 1572872 | tf_op jit(solution)/shard_map/ppermute | solution.py:20
  28.9 19.2 %collective-permute-start.8 = (bf16[1024,256]{1,0:T(8,128)(2,1)S(1)}, bf16[1024,256]{1,0:T(8,128)(2,1)}, u32[]{:S(2)}, u32[]{:S(2)}) collective-permute-start(bf16[1024,256]{1,0:T(8,128)(2,1)S(1)} %collective-permute-done.1), channel_id=1, source_target_pairs={{0,2},{2,0},{1,3},{3,1},{4,6},{6,4},{5,7},{7,5},{8,10},{10,8},{9,1... | collective-permute-start | bytes 1572872 | tf_op jit(solution)/shard_map/ppermute | solution.py:20
  29.0 16.0 %collective-permute-start.7 = (bf16[1024,256]{1,0:T(8,128)(2,1)}, bf16[1024,256]{1,0:T(8,128)(2,1)}, u32[]{:S(2)}, u32[]{:S(2)}) collective-permute-start(bf16[1024,256]{1,0:T(8,128)(2,1)} %collective-permute-done), channel_id=1, source_target_pairs={{0,2},{2,0},{1,3},{3,1},{4,6},{6,4},{5,7},{7,5},{8,10},{10,8},{9,1... | collective-permute-start | bytes 1572872 | tf_op jit(solution)/shard_map/ppermute | solution.py:20
  32.3 13.9 %copy-start = (bf16[128,1024]{1,0:T(8,128)(2,1)S(1)}, bf16[128,1024]{1,0:T(8,128)(2,1)}, u32[]{:S(2)}) copy-start(bf16[128,1024]{1,0:T(8,128)(2,1)} %shard_map.121) | copy-start | bytes 786436
  37.5 26.3 %collective-permute-start.22 = (bf16[128,4096]{1,0:T(8,128)(2,1)S(1)}, bf16[128,4096]{1,0:T(8,128)(2,1)S(1)}, u32[]{:S(2)}, u32[]{:S(2)}) collective-permute-start(bf16[128,4096]{1,0:T(8,128)(2,1)S(1)} %copy-done.1), channel_id=1, source_target_pairs={{0,1},{1,0},{2,3},{3,2},{4,5},{5,4},{6,7},{7,6},{8,9},{9,8},{10,11... | collective-permute-start | bytes 3145736 | tf_op jit(solution)/shard_map/ppermute | solution.py:24
  41.3 27.2 %collective-permute-start.12 = (bf16[1024,256]{1,0:T(8,128)(2,1)S(1)}, bf16[1024,256]{1,0:T(8,128)(2,1)S(1)}, u32[]{:S(2)}, u32[]{:S(2)}) collective-permute-start(bf16[1024,256]{1,0:T(8,128)(2,1)S(1)} %collective-permute-done.3), channel_id=1, source_target_pairs={{0,2},{2,0},{1,3},{3,1},{4,6},{6,4},{5,7},{7,5},{8,10},{10,8},{9,1... | collective-permute-start | bytes 1572872 | tf_op jit(solution)/shard_map/ppermute | solution.py:20
  44.9 17.2 %collective-permute-start.5 = (bf16[1024,256]{1,0:T(8,128)(2,1)S(1)}, bf16[1024,256]{1,0:T(8,128)(2,1)S(1)}, u32[]{:S(2)}, u32[]{:S(2)}) collective-permute-start(bf16[1024,256]{1,0:T(8,128)(2,1)S(1)} %collective-permute-done.3), channel_id=1, source_target_pairs={{0,28},{4,0},{8,4},{12,8},{16,12},{20,16},{24,20},{28,24},{1,29},{... | collective-permute-start | bytes 1572872 | tf_op jit(solution)/shard_map/ppermute | solution.py:294
  47.5 14.7 %collective-permute-start.4 = (bf16[1024,256]{1,0:T(8,128)(2,1)}, bf16[1024,256]{1,0:T(8,128)(2,1)S(1)}, u32[]{:S(2)}, u32[]{:S(2)}) collective-permute-start(bf16[1024,256]{1,0:T(8,128)(2,1)} %collective-permute-done.2), channel_id=1, source_target_pairs={{0,4},{4,8},{8,12},{12,16},{16,20},{20,24},{24,28},{28,0},{1,5},{5... | collective-permute-start | bytes 1572872 | tf_op jit(solution)/shard_map/ppermute | solution.py:294
  48.1 31.4 %copy-start.7 = (bf16[128,512]{1,0:T(8,128)(2,1)}, bf16[128,512]{1,0:T(8,128)(2,1)S(1)}, u32[]{:S(2)}) copy-start(bf16[128,512]{1,0:T(8,128)(2,1)S(1)} %pad_maximum_fusion.3.refs_0_) | copy-start | bytes 393220
  48.2 17.9 %collective-permute-start.11 = (bf16[1024,256]{1,0:T(8,128)(2,1)}, bf16[1024,256]{1,0:T(8,128)(2,1)S(1)}, u32[]{:S(2)}, u32[]{:S(2)}) collective-permute-start(bf16[1024,256]{1,0:T(8,128)(2,1)} %collective-permute-done.2), channel_id=1, source_target_pairs={{0,2},{2,0},{1,3},{3,1},{4,6},{6,4},{5,7},{7,5},{8,10},{10,8},{9,1... | collective-permute-start | bytes 1572872 | tf_op jit(solution)/shard_map/ppermute | solution.py:20
  50.1 28.6 %copy-start.3 = (bf16[128,1024]{1,0:T(8,128)(2,1)}, bf16[128,1024]{1,0:T(8,128)(2,1)S(1)}, u32[]{:S(2)}) copy-start(bf16[128,1024]{1,0:T(8,128)(2,1)S(1)} %pad_maximum_fusion.refs_2_) | copy-start | bytes 786436
  62.2 19.0 %collective-permute-start.15 = (bf16[1024,256]{1,0:T(8,128)(2,1)S(1)}, bf16[1024,256]{1,0:T(8,128)(2,1)S(1)}, u32[]{:S(2)}, u32[]{:S(2)}) collective-permute-start(bf16[1024,256]{1,0:T(8,128)(2,1)S(1)} %collective-permute-done.5), channel_id=1, source_target_pairs={{0,2},{2,0},{1,3},{3,1},{4,6},{6,4},{5,7},{7,5},{8,10},{10,8},{9,1... | collective-permute-start | bytes 1572872 | tf_op jit(solution)/shard_map/ppermute | solution.py:20
  63.3 18.2 %collective-permute-start.14 = (bf16[1024,256]{1,0:T(8,128)(2,1)S(1)}, bf16[1024,256]{1,0:T(8,128)(2,1)S(1)}, u32[]{:S(2)}, u32[]{:S(2)}) collective-permute-start(bf16[1024,256]{1,0:T(8,128)(2,1)S(1)} %collective-permute-done.4), channel_id=1, source_target_pairs={{0,2},{2,0},{1,3},{3,1},{4,6},{6,4},{5,7},{7,5},{8,10},{10,8},{9,1... | collective-permute-start | bytes 1572872 | tf_op jit(solution)/shard_map/ppermute | solution.py:20
  65.4 10.7 %collective-permute-start.18 = (bf16[512,256]{1,0:T(8,128)(2,1)S(1)}, bf16[512,256]{1,0:T(8,128)(2,1)S(1)}, u32[]{:S(2)}, u32[]{:S(2)}) collective-permute-start(bf16[512,256]{1,0:T(8,128)(2,1)S(1)} %slice.77), channel_id=1, source_target_pairs={{0,28},{4,0},{8,4},{12,8},{16,12},{20,16},{24,20},{28,24},{1,29},{... | collective-permute-start | bytes 786440 | tf_op jit(solution)/shard_map/ppermute | solution.py:294
  66.1 11.7 %collective-permute-start.17 = (bf16[512,256]{1,0:T(8,128)(2,1)S(1)}, bf16[512,256]{1,0:T(8,128)(2,1)S(1)}, u32[]{:S(2)}, u32[]{:S(2)}) collective-permute-start(bf16[512,256]{1,0:T(8,128)(2,1)S(1)} %slice.75), channel_id=1, source_target_pairs={{0,4},{4,8},{8,12},{12,16},{16,20},{20,24},{24,28},{28,0},{1,5},{5... | collective-permute-start | bytes 786440 | tf_op jit(solution)/shard_map/ppermute | solution.py:294
  68.7 5.1 %copy-start.4 = (bf16[128,1024]{1,0:T(8,128)(2,1)}, bf16[128,1024]{1,0:T(8,128)(2,1)S(1)}, u32[]{:S(2)}) copy-start(bf16[128,1024]{1,0:T(8,128)(2,1)S(1)} %pad_maximum_fusion.1.refs_4_) | copy-start | bytes 786436
  68.8 22.6 %collective-permute-start.13 = (bf16[128,1024]{1,0:T(8,128)(2,1)S(1)}, bf16[128,1024]{1,0:T(8,128)(2,1)S(1)}, u32[]{:S(2)}, u32[]{:S(2)}) collective-permute-start(bf16[128,1024]{1,0:T(8,128)(2,1)S(1)} %pad_maximum_fusion.1.refs_4_), channel_id=1, source_target_pairs={{0,1},{1,0},{2,3},{3,2},{4,5},{5,4},{6,7},{7,6},{8,9},{9,8},{10,11... | collective-permute-start | bytes 786440 | tf_op jit(solution)/shard_map/ppermute | solution.py:24
  76.1 2.6 %collective-permute-start.20 = (bf16[512,256]{1,0:T(8,128)(2,1)S(1)}, bf16[512,256]{1,0:T(8,128)(2,1)S(1)}, u32[]{:S(2)}, u32[]{:S(2)}) collective-permute-start(bf16[512,256]{1,0:T(8,128)(2,1)S(1)} %collective-permute-done.18), channel_id=1, source_target_pairs={{0,2},{2,0},{1,3},{3,1},{4,6},{6,4},{5,7},{7,5},{8,10},{10,8},{9,1... | collective-permute-start | bytes 786440 | tf_op jit(solution)/shard_map/ppermute | solution.py:20
  77.8 1.7 collective-permute-start.19
  78.7 12.7 %collective-permute-start.10 = (bf16[128,1024]{1,0:T(8,128)(2,1)S(1)}, bf16[128,1024]{1,0:T(8,128)(2,1)S(1)}, u32[]{:S(2)}, u32[]{:S(2)}) collective-permute-start(bf16[128,1024]{1,0:T(8,128)(2,1)S(1)} %pad_maximum_fusion.refs_2_), channel_id=1, source_target_pairs={{0,1},{1,0},{2,3},{3,2},{4,5},{5,4},{6,7},{7,6},{8,9},{9,8},{10,11... | collective-permute-start | bytes 786440 | tf_op jit(solution)/shard_map/ppermute | solution.py:24
  79.5 9.5 %collective-permute-start.9 = (bf16[128,512]{1,0:T(8,128)(2,1)S(1)}, bf16[128,512]{1,0:T(8,128)(2,1)S(1)}, u32[]{:S(2)}, u32[]{:S(2)}) collective-permute-start(bf16[128,512]{1,0:T(8,128)(2,1)S(1)} %pad_maximum_fusion.3.refs_0_), channel_id=1, source_target_pairs={{0,1},{1,0},{2,3},{3,2},{4,5},{5,4},{6,7},{7,6},{8,9},{9,8},{10,11... | collective-permute-start | bytes 393224 | tf_op jit(solution)/shard_map/ppermute | solution.py:24
  82.5 20.6 %copy-start.6 = (bf16[128,1024]{1,0:T(8,128)(2,1)}, bf16[128,1024]{1,0:T(8,128)(2,1)S(1)}, u32[]{:S(2)}) copy-start(bf16[128,1024]{1,0:T(8,128)(2,1)S(1)} %fusion.10.refs_10_) | copy-start | bytes 786436
  82.5 20.6 %collective-permute-start.23 = (bf16[128,1024]{1,0:T(8,128)(2,1)S(1)}, bf16[128,1024]{1,0:T(8,128)(2,1)S(1)}, u32[]{:S(2)}, u32[]{:S(2)}) collective-permute-start(bf16[128,1024]{1,0:T(8,128)(2,1)S(1)} %fusion.10.refs_10_), channel_id=1, source_target_pairs={{0,1},{1,0},{2,3},{3,2},{4,5},{5,4},{6,7},{7,6},{8,9},{9,8},{10,11... | collective-permute-start | bytes 786440 | tf_op jit(solution)/shard_map/ppermute | solution.py:24
  83.6 19.5 %copy-start.5 = (bf16[128,1024]{1,0:T(8,128)(2,1)}, bf16[128,1024]{1,0:T(8,128)(2,1)S(1)}, u32[]{:S(2)}) copy-start(bf16[128,1024]{1,0:T(8,128)(2,1)S(1)} %pad_maximum_fusion.2.refs_6_) | copy-start | bytes 786436
  83.6 19.5 %collective-permute-start.16 = (bf16[128,1024]{1,0:T(8,128)(2,1)S(1)}, bf16[128,1024]{1,0:T(8,128)(2,1)S(1)}, u32[]{:S(2)}, u32[]{:S(2)}) collective-permute-start(bf16[128,1024]{1,0:T(8,128)(2,1)S(1)} %pad_maximum_fusion.2.refs_6_), channel_id=1, source_target_pairs={{0,1},{1,0},{2,3},{3,2},{4,5},{5,4},{6,7},{7,6},{8,9},{9,8},{10,11... | collective-permute-start | bytes 786440 | tf_op jit(solution)/shard_map/ppermute | solution.py:24
  84.6 18.5 %copy-start.8 = (bf16[128,512]{1,0:T(8,128)(2,1)}, bf16[128,512]{1,0:T(8,128)(2,1)S(1)}, u32[]{:S(2)}) copy-start(bf16[128,512]{1,0:T(8,128)(2,1)S(1)} %pad_maximum_fusion.4.refs_8_) | copy-start | bytes 393220
  89.0 0.6 copy-start.14
  89.7 13.4 %collective-permute-start.21 = (bf16[128,512]{1,0:T(8,128)(2,1)S(1)}, bf16[128,512]{1,0:T(8,128)(2,1)S(1)}, u32[]{:S(2)}, u32[]{:S(2)}) collective-permute-start(bf16[128,512]{1,0:T(8,128)(2,1)S(1)} %pad_maximum_fusion.4.refs_8_), channel_id=1, source_target_pairs={{0,1},{1,0},{2,3},{3,2},{4,5},{5,4},{6,7},{7,6},{8,9},{9,8},{10,11... | collective-permute-start | bytes 393224 | tf_op jit(solution)/shard_map/ppermute | solution.py:24
  91.4 11.7 %copy-start.9 = (bf16[128,1024]{1,0:T(8,128)(2,1)}, bf16[128,1024]{1,0:T(8,128)(2,1)S(1)}, u32[]{:S(2)}) copy-start(bf16[128,1024]{1,0:T(8,128)(2,1)S(1)} %collective-permute-done.13.refs_5_) | copy-start | bytes 786436
  91.4 11.7 %copy-start.10 = (bf16[128,1024]{1,0:T(8,128)(2,1)}, bf16[128,1024]{1,0:T(8,128)(2,1)S(1)}, u32[]{:S(2)}) copy-start(bf16[128,1024]{1,0:T(8,128)(2,1)S(1)} %collective-permute-done.10.refs_3_) | copy-start | bytes 786436
  103.1 0.7 copy-start.15
  103.1 0.8 copy-start.11
  103.8 0.7 copy-start.12
  110.2 3.6 %collective-permute-start.24 = (bf16[3840,128]{1,0:T(8,128)(2,1)}, bf16[3840,128]{1,0:T(8,128)(2,1)S(1)}, u32[]{:S(2)}, u32[]{:S(2)}) collective-permute-start(bf16[3840,128]{1,0:T(8,128)(2,1)} %get-tuple-element.37), channel_id=1, source_target_pairs={{0,2},{2,0},{1,3},{3,1},{4,6},{6,4},{5,7},{7,5},{8,10},{10,8},{9,1... | collective-permute-start | bytes 2949128 | tf_op jit(solution)/shard_map/ppermute | solution.py:20
  184.3 9.7 %copy-start.2 = (bf16[8,480,128]{2,1,0:T(8,128)(2,1)}, bf16[8,480,128]{2,1,0:T(8,128)(2,1)S(1)}, u32[]{:S(2)}) copy-start(bf16[8,480,128]{2,1,0:T(8,128)(2,1)S(1)} %all_to_all.17) | copy-start | bytes 2949124
  184.3 9.7 %collective-permute-start.25 = (bf16[3840,128]{1,0:T(8,128)(2,1)S(1)}, bf16[3840,128]{1,0:T(8,128)(2,1)S(1)}, u32[]{:S(2)}, u32[]{:S(2)}) collective-permute-start(bf16[3840,128]{1,0:T(8,128)(2,1)S(1)} %bitcast.58), channel_id=1, source_target_pairs={{0,2},{2,0},{1,3},{3,1},{4,6},{6,4},{5,7},{7,5},{8,10},{10,8},{9,1... | collective-permute-start | bytes 2949128 | tf_op jit(solution)/shard_map/ppermute | solution.py:20
  194.0 1.0 copy-start.13

commit v3 on v2

v3 whole, which is shorter than its diff:
```python
import jax
import jax.numpy as jnp
from jax import lax
from jax.experimental import pallas as pl
from jax.experimental.pallas import tpu as pltpu
from jax.sharding import Mesh
from jax.sharding import PartitionSpec as P


HEAD = 128
HG_OLD = 16
HG_NEW = 20
BO_OLD = 32
PAIR = [(0, 1), (1, 0)]


def swap_cores(x):
    return lax.ppermute(x, "c", PAIR)


def swap_halves(x):
    return lax.ppermute(x, "xl", PAIR)


def add_pair(mine, other):
    return (mine.astype(jnp.float32) + other.astype(jnp.float32)).astype(jnp.bfloat16)


def arrival_place(cols):
    shard = cols // 2
    z = lax.axis_index("z")
    away = (shard // 2 - z) * (2 * (z % 2) - 1) % lax.axis_size("z")
    base = jnp.where(away < 4, 8 * away, 60 - 8 * away)
    return base + 2 * (shard % 2 != lax.axis_index("c")) + cols % 2


def forward(x, piece):
    if isinstance(piece, tuple):
        half = piece[0].shape[0]
        return forward(x[:, :half], piece[0]) + forward(x[:, half:], piece[1])
    return jnp.dot(x, piece, preferred_element_type=jnp.float32)


def backward(g, piece):
    if isinstance(piece, tuple):
        return jnp.concatenate([backward(g, part) for part in piece], axis=1)
    return lax.dot_general(
        g, piece, (((1,), (1,)), ((), ())), preferred_element_type=jnp.float32
    )


SMEM = pl.BlockSpec(memory_space=pltpu.SMEM)


def times(x, w, dims):
    return lax.dot_general(x, w, (dims, ((), ())), preferred_element_type=jnp.float32)


def scatter_blocks(x, blocks, place, slots, used, transposed):
    rows = blocks.shape[0]
    tok = x.shape[0]

    def kernel(place_ref, x_ref, w_ref, o_ref, acc_ref):
        acc_ref[...] = jnp.zeros_like(acc_ref)
        for r in range(rows):
            xr = x_ref[:, r * HEAD : (r + 1) * HEAD]
            if transposed:
                both = times(xr, w_ref[r].reshape(2 * HEAD, HEAD), ((1,), (1,)))
            else:
                both = times(xr, jnp.concatenate([w_ref[r, 0], w_ref[r, 1]], 1), ((1,), (0,)))
            for k in range(2):
                c = place_ref[r, k]
                acc_ref[c] = acc_ref[c] + both[:, k * HEAD : (k + 1) * HEAD]
        for c in range(used):
            o_ref[:, c * HEAD : (c + 1) * HEAD] = acc_ref[c].astype(jnp.bfloat16)

    full = pl.BlockSpec(memory_space=pltpu.VMEM)
    return pl.pallas_call(
        kernel,
        out_shape=jax.ShapeDtypeStruct((tok, used * HEAD), jnp.bfloat16),
        in_specs=[SMEM, full, full],
        out_specs=full,
        scratch_shapes=[pltpu.VMEM((slots, tok, HEAD), jnp.float32)],
    )(place, x, blocks)


def stage(dst, at, mine, other=None):
    for c in range(mine.shape[1] // HEAD):
        cols = slice(c * HEAD, (c + 1) * HEAD)
        block = mine[:, cols]
        if other is not None:
            block = add_pair(block, other[:, cols])
        dst[at + c] = block
    return at + mine.shape[1] // HEAD


def vmem(*shape):
    return pltpu.VMEM(shape, jnp.bfloat16)


def whole(x):
    return pl.BlockSpec(x.shape, lambda i, *_: (0,) * len(x.shape))


def width_rows(where, place, chunks, cotangent, blocks):
    tok = cotangent.shape[0]
    rows = place.shape[0]
    half = rows // 2
    n_chunks = len(chunks)

    def kernel(where_ref, place_ref, *refs):
        chunk_refs, refs = refs[:n_chunks], refs[n_chunks:]
        cot_ref, w_ref, grown_ref, keep_ref, send_ref, sel, cot = refs
        at = 0
        for i in range(0, n_chunks, 2):
            at = stage(sel, at, chunk_refs[i], chunk_refs[i + 1])
        stage(cot, 0, cot_ref)
        for which in range(2):
            core = (where_ref[0] + which) % 2
            dst = (send_ref, keep_ref)[1 - which]
            for i in range(half):
                r = core * half + i
                x = jnp.concatenate([sel[place_ref[r, 0]], sel[place_ref[r, 1]]], 1)
                at = 2 * HEAD * i
                dst[at : at + 2 * HEAD, :] = times(x, cot[r], ((0,), (0,))).astype(dst.dtype)
        for r in range(rows):
            x = jnp.concatenate([sel[place_ref[r, 0]], sel[place_ref[r, 1]]], 1)
            y = times(x, w_ref[r].reshape(2 * HEAD, HEAD), ((1,), (0,)))
            grown_ref[:, r * HEAD : (r + 1) * HEAD] = y.astype(jnp.bfloat16)

    out_shape = [
        jax.ShapeDtypeStruct((tok, rows * HEAD), jnp.bfloat16),
        jax.ShapeDtypeStruct((rows * HEAD, HEAD), jnp.float32),
        jax.ShapeDtypeStruct((rows * HEAD, HEAD), jnp.bfloat16),
    ]
    return pl.pallas_call(
        kernel,
        grid_spec=pltpu.PrefetchScalarGridSpec(
            num_scalar_prefetch=2,
            grid=(1,),
            in_specs=[whole(x) for x in (*chunks, cotangent, blocks)],
            out_specs=[whole(x) for x in out_shape],
            scratch_shapes=[vmem(BO_OLD, tok, HEAD), vmem(rows, tok, HEAD)],
        ),
        out_shape=out_shape,
    )(where, place, *chunks, cotangent, blocks)


def head_terms(where, place, hidden_grads, attn_out):
    tok = attn_out.shape[0]
    rows = place.shape[0]
    half = rows // 2

    def kernel(where_ref, place_ref, hg0, hg1, attn_ref, keep_ref, send_ref, hg, attn):
        stage(hg, stage(hg, 0, hg0), hg1)
        stage(attn, 0, attn_ref)
        for which in range(2):
            core = (where_ref[0] + which) % 2
            dst = (send_ref, keep_ref)[1 - which]
            for i in range(half):
                r = core * half + i
                rhs = jnp.concatenate([hg[place_ref[r, 0]], hg[place_ref[r, 1]]], 1)
                both = times(attn[r], rhs, ((0,), (0,))).astype(dst.dtype)
                for k in range(2):
                    at = (2 * i + k) * HEAD
                    dst[at : at + HEAD, :] = both[:, k * HEAD : (k + 1) * HEAD]

    out_shape = [
        jax.ShapeDtypeStruct((rows * HEAD, HEAD), jnp.float32),
        jax.ShapeDtypeStruct((rows * HEAD, HEAD), jnp.bfloat16),
    ]
    return pl.pallas_call(
        kernel,
        grid_spec=pltpu.PrefetchScalarGridSpec(
            num_scalar_prefetch=2,
            grid=(1,),
            in_specs=[
                *[whole(x) for x in hidden_grads],
                pl.BlockSpec((tok, rows * HEAD), lambda i, w, *_: (0, w[1])),
            ],
            out_specs=[whole(x) for x in out_shape],
            scratch_shapes=[vmem(HG_OLD, tok, HEAD), vmem(rows, tok, HEAD)],
        ),
        out_shape=out_shape,
    )(where, place, *hidden_grads, attn_out)


def head_grads(where, place, hidden_grads, blocks):
    tok = hidden_grads[0].shape[0]
    rows = place.shape[0]

    def kernel(where_ref, place_ref, hg0, hg1, w_ref, grad_ref, hg):
        stage(hg, stage(hg, 0, hg0), hg1)
        for r in range(rows):
            x = jnp.concatenate([hg[place_ref[r, 0]], hg[place_ref[r, 1]]], 1)
            w = jnp.concatenate([w_ref[r, 0], w_ref[r, 1]], 1)
            y = times(x, w, ((1,), (1,)))
            grad_ref[:, r * HEAD : (r + 1) * HEAD] = y.astype(jnp.bfloat16)

    out_shape = jax.ShapeDtypeStruct((tok, rows * HEAD), jnp.bfloat16)
    return pl.pallas_call(
        kernel,
        grid_spec=pltpu.PrefetchScalarGridSpec(
            num_scalar_prefetch=2,
            grid=(1,),
            in_specs=[
                *[whole(x) for x in hidden_grads],
                pl.BlockSpec((rows, 2, HEAD, HEAD), lambda i, w, *_: (w[1], 0, 0, 0)),
            ],
            out_specs=whole(out_shape),
            scratch_shapes=[vmem(HG_OLD, tok, HEAD)],
        ),
        out_shape=out_shape,
    )(where, place, *hidden_grads, blocks)


def mix_layers(pick, coef, weights):
    rows, cols = weights.shape[1:]
    steps = 2

    def kernel(pick_ref, coef_ref, first_ref, second_ref, o_ref):
        total = coef_ref[0] * first_ref[0].astype(jnp.float32)
        total = total + coef_ref[1] * second_ref[0].astype(jnp.float32)
        o_ref[...] = total.astype(jnp.bfloat16)

    def layer(slot):
        return pl.BlockSpec((1, rows // steps, cols), lambda i, p, c: (p[slot], i, 0))

    return pl.pallas_call(
        kernel,
        grid_spec=pltpu.PrefetchScalarGridSpec(
            num_scalar_prefetch=2,
            grid=(steps,),
            in_specs=[layer(0), layer(1)],
            out_specs=pl.BlockSpec((rows // steps, cols), lambda i, p, c: (i, 0)),
        ),
        out_shape=jax.ShapeDtypeStruct((rows, cols), jnp.bfloat16),
    )(pick, coef, weights, weights)


def unpack_sums(where, mine, theirs, cut):
    rows = mine.shape[0]

    def kernel(where_ref, mine_ref, theirs_ref, in_ref, out_ref):
        for step, src in enumerate((mine_ref, theirs_ref)):

            @pl.when(pl.program_id(0) == step)
            def _():
                in_ref[0] = src[:cut, :].astype(jnp.float32)
                out_ref[0] = src[cut:, :].astype(jnp.float32)

    return pl.pallas_call(
        kernel,
        grid_spec=pltpu.PrefetchScalarGridSpec(
            num_scalar_prefetch=1,
            grid=(2,),
            in_specs=[whole(mine), whole(theirs)],
            out_specs=[
                pl.BlockSpec((1, cut, HEAD), lambda i, w: ((w[0] + i) % 2, 0, 0)),
                pl.BlockSpec((1, rows - cut, HEAD), lambda i, w: ((w[0] + i) % 2, 0, 0)),
            ],
        ),
        out_shape=[
            jax.ShapeDtypeStruct((2, cut, HEAD), jnp.float32),
            jax.ShapeDtypeStruct((2, rows - cut, HEAD), jnp.float32),
        ],
    )(where, mine, theirs)


def token_sum(keep, came, scale):
    plane = ("xh", "y")
    n = lax.axis_size(plane)
    mine = [(k + c.astype(jnp.float32)).astype(jnp.bfloat16) for k, c in zip(keep, came)]
    mine = jnp.concatenate(mine, axis=0)
    rows = mine.shape[0]
    parts = lax.all_to_all(mine.reshape(n, rows // n, HEAD), plane, 0, 0, tiled=True)
    part = jnp.sum(parts.astype(jnp.float32), axis=0).astype(jnp.bfloat16)
    spread = jnp.broadcast_to(part[None], (lax.axis_size("z"),) + part.shape)
    parts = lax.all_to_all(spread, "z", 0, 0, tiled=True)
    part = (jnp.sum(parts.astype(jnp.float32), axis=0) * scale).astype(jnp.bfloat16)
    spread = jnp.broadcast_to(part[None], (n,) + part.shape)
    return lax.all_to_all(spread, plane, 0, 0, tiled=True).reshape(rows, HEAD)


def local(
    attn_out,
    cotangent,
    old_weights,
    depth_coef,
    depth_pick,
    in_blocks,
    in_cols,
    out_blocks,
    out_cols,
):
    tok_rows = attn_out.shape[0]
    core = lax.axis_index("c")
    tensor_half = lax.axis_index("xl")
    local_old = old_weights.shape[1]
    local_blocks = local_old // HEAD
    rows_in = HG_NEW // lax.axis_size("xl")
    where = jnp.stack([core, tensor_half]).astype(jnp.int32)
    out_place = arrival_place(out_cols).astype(jnp.int32)
    own = in_cols // local_blocks == tensor_half
    hidden_place = jnp.where(own, in_cols % local_blocks, local_blocks)
    in_place = in_cols % local_blocks + jnp.where(own, 0, local_blocks)
    in_place = lax.dynamic_slice_in_dim(in_place, tensor_half * rows_in, rows_in, 0)

    n = lax.axis_size("z")
    even = [(i, i ^ 1) for i in range(n)]
    odd = [(i, (i - 1 + 2 * (i % 2)) % n) for i in range(n)]

    def hop(a, b):
        return lax.ppermute(b, "z", even), lax.ppermute(a, "z", odd)

    def cores(*pieces):
        return [q for p in pieces for q in (p, swap_cores(p))]

    def forward_chunk(pieces):
        part = jnp.concatenate([forward(hidden, p) for p in pieces], axis=1)
        part = part.astype(jnp.bfloat16)
        return [part, swap_halves(part)]

    def backward_chunk(at, pieces, total):
        for p in pieces:
            total = total + backward(old_grad[:, at * HEAD : (at + 2) * HEAD], p)
            at += 2
        return total

    grad_part = scatter_blocks(cotangent, out_blocks, out_place, BO_OLD, BO_OLD, True)
    grad_other = swap_halves(grad_part)
    mixed = mix_layers(depth_pick, depth_coef, old_weights)
    chunk0 = cores(mixed)
    a, b = hop(mixed, mixed)
    hidden = scatter_blocks(
        attn_out, in_blocks, hidden_place, local_blocks + 1, local_blocks, False
    )
    parts = forward_chunk(chunk0)
    chunk1 = cores(a, b)
    a, b = hop(a, b)
    parts += forward_chunk(chunk1)
    chunk2 = cores(a, b)
    a, b = hop(a, b)
    parts += forward_chunk(chunk2)
    old_grad = add_pair(grad_part, grad_other)
    hidden_grad = backward_chunk(0, chunk0, 0.0)
    hidden_grad = backward_chunk(4, chunk1, hidden_grad)
    chunk3 = cores(a, b)
    half = local_old // 2
    a, b = hop(a[half:], b[:half])
    chunk4 = [(a, b), (swap_cores(a), swap_cores(b))]
    parts += forward_chunk(chunk3)
    hidden_grad = backward_chunk(12, chunk2, hidden_grad)
    hidden_grad = backward_chunk(20, chunk3, hidden_grad)
    parts += forward_chunk(chunk4)
    hidden_grad = backward_chunk(28, chunk4, hidden_grad).astype(jnp.bfloat16)
    hidden_grads = [hidden_grad, swap_halves(hidden_grad)]
    grown_out, keep_out, send_out = width_rows(
        where, out_place, parts, cotangent, out_blocks
    )
    came_out = swap_cores(send_out)
    keep_in, send_in = head_terms(where, in_place, hidden_grads, attn_out)
    came_in = swap_cores(send_in)
    grad_attn = head_grads(where, in_place, hidden_grads, in_blocks)
    grad_scale = float(tok_rows * lax.axis_size(("xh", "y", "z", "c"))) ** (-0.5)
    full = token_sum((keep_in, keep_out), (came_in, came_out), grad_scale)
    theirs = swap_cores(full)
    in_sum, out_sum = unpack_sums(where, full, theirs, rows_in * HEAD)
    in_sum = in_sum.reshape(rows_in, 2, HEAD, HEAD)
    out_sum = out_sum.reshape(out_cols.shape[0], 2, HEAD, HEAD)
    return (grown_out, grad_attn, in_sum, out_sum)


def solution(mesh):
    fine = Mesh(mesh.devices.reshape(2, 4, 8, 2, 2), ("xh", "y", "z", "c", "xl"))
    tokens = ("xh", "y", "z", "c")
    placed = (
        P(tokens, None),
        P(tokens, "xl"),
        P(None, "xl", ("z", "c")),
        P(),
        P(),
        P(),
        P(),
        P("xl", None, None, None),
        P("xl", None),
    )
    return jax.shard_map(
        local,
        mesh=fine,
        in_specs=placed,
        out_specs=(
            P(tokens, "xl"),
            P(tokens, "xl"),
            P("xl", None, None, None),
            P("xl", None, None, None),
        ),
        check_vma=False,
    )
```

time: 200 us -> 189 us (0.945)
  matrix products: 19.5 us -> 11.8 us
  waiting for transfers between devices: 43.5 us -> 37.5 us
  other arithmetic: 9.67 us -> 4.95 us
  Pallas kernels: 21.2 us -> 25.4 us
  starting transfers between devices: 32.5 us -> 36.6 us
    ppermute x8, waiting for transfers between devices: 24.8 us -> 13.1 us  [hop(): return (lax.ppermute(b, 'z', even), lax.ppermute(a, 'z', odd))]
    ppermute x7, waiting for transfers between devices: 16 us -> 21.2 us  [swap_halves(): return lax.ppermute(x, 'xl', PAIR)]
    pallas_call x2 -> x4, Pallas kernels: 10.7 us -> 14.9 us  [the longest x1 5.59 us: width_rows(): pl.pallas_call(kernel, grid_spec=pltpu.PrefetchScalarGridSpec(num_scalar_...]
    dot_general x18, matrix products: 9.35 us -> 5.16 us  [backward(): lax.dot_general(g, piece, (((1,), (1,)), ((), ())), preferred_element_typ...]
    add x1 -> x0, other arithmetic: 3.59 us -> none  [local(): mixed = mixed + weight * old_weights[layer].astype(jnp.float32)]
    dot_general x18, matrix products: 10.2 us -> 6.61 us  [forward(): return jnp.dot(x, piece, preferred_element_type=jnp.float32)]
    ppermute x11 -> x12, starting transfers between devices: 14.1 us -> 16.8 us  [swap_cores(): return lax.ppermute(x, 'c', PAIR)]
  transfers between devices with their start and end apart: 26 -> 27, of which waited for: 7 -> 10; matrix products, arithmetic and copies ran while one was open for 11% -> 9% of each run, Pallas kernels for 6% -> 10%
where the time goes in v3:
time: 189 us; the launch traced here: 188 us
  blocking collectives  67.5 us (36%)
  waiting for transfers between devices  37.5 us (20%)
  starting transfers between devices  36.6 us (19%)
  Pallas kernels  25.4 us (13%)
  matrix products  11.8 us (6%)
  other arithmetic  4.95 us (3%)
  local copies, waits for them, and re-layouts  3.52 us (2%)
    all_to_all x1, blocking collectives, token_sum(): parts = lax.all_to_all(spread, 'z', 0, 0, tiled=True)  28.2 us
    all_to_all x1, blocking collectives, token_sum(): lax.all_to_all(mine.reshape(n, rows // n, HEAD), plane, 0, 0, tiled=True)  21.8 us
    ppermute x7, waiting for transfers between devices, swap_halves(): return lax.ppermute(x, 'xl', PAIR)  21.2 us
    all_to_all x1, blocking collectives, token_sum(): return lax.all_to_all(spread, plane, 0, 0, tiled=True).reshape(rows, HEAD)  17.4 us
    ppermute x12, starting transfers between devices, swap_cores(): return lax.ppermute(x, 'c', PAIR)  16.8 us
    ppermute x8, starting transfers between devices, hop(): return (lax.ppermute(b, 'z', even), lax.ppermute(a, 'z', odd))  13.4 us
    ppermute x8, waiting for transfers between devices, hop(): return (lax.ppermute(b, 'z', even), lax.ppermute(a, 'z', odd))  13.1 us
    dot_general x18, matrix products, forward(): return jnp.dot(x, piece, preferred_element_type=jnp.float32)  6.61 us
  transfers between devices with their start and end apart: 27, of which 10 were waited for; matrix products, arithmetic and copies ran while one was open for 9% of the time, Pallas kernels for 10%

profile of v3, /device:TPU:1, one launch (start us, length us, event | category | flops | bytes accessed | tf_op | source)
XLA Modules:
  0.0 188.4 jit_solution(2870110464590540420)
XLA Ops:
  0.6 2.9 %shard_map.121 = bf16[1024,256]{1,0:T(8,128)(2,1)} custom-call(s32[2]{0:T(128)} %pick_ref.1, f32[2]{0:T(128)} %coef_ref.1, bf16[3,1024,256]{2,1,0:T(8,128)(2,1)} %second_ref.1, bf16[3,1024,256]{2,1,0:T(8,128)(2,1)} %second_ref.1), custom_call_target="tpu_custom_call" | custom-call | tf_op jit(solution)/shard_map/pallas_call | solution.py:229
  3.5 2.5 %collective-permute-start.2 = (bf16[1024,256]{1,0:T(8,128)(2,1)}, bf16[1024,256]{1,0:T(8,128)(2,1)S(1)}, u32[]{:S(2)}, u32[]{:S(2)}) collective-permute-start(bf16[1024,256]{1,0:T(8,128)(2,1)} %shard_map.121), channel_id=1, source_target_pairs={{0,4},{4,0},{8,12},{12,8},{16,20},{20,16},{24,28},{28,24},{1,5},{5... | collective-permute-start | bytes 1572872 | tf_op jit(solution)/shard_map/ppermute | solution.py:314
  6.0 1.0 collective-permute-start
  6.9 4.7 %collective-permute-start.4 = (bf16[1024,256]{1,0:T(8,128)(2,1)}, bf16[1024,256]{1,0:T(8,128)(2,1)S(1)}, u32[]{:S(2)}, u32[]{:S(2)}) collective-permute-start(bf16[1024,256]{1,0:T(8,128)(2,1)} %shard_map.121), channel_id=1, source_target_pairs={{0,28},{4,8},{8,4},{12,16},{16,12},{20,24},{24,20},{28,0},{1,29},{... | collective-permute-start | bytes 1572872 | tf_op jit(solution)/shard_map/ppermute | solution.py:314
  11.7 0.6 fusion.50.place_ref
  12.3 3.4 %shard_map.123 = bf16[128,4096]{1,0:T(8,128)(2,1)} custom-call(s32[20,2]{1,0:T(8,128)} %fusion.50.place_ref, bf16[128,2560]{1,0:T(8,128)(2,1)} %x_ref.3, bf16[20,2,128,128]{3,2,1,0:T(8,128)(2,1)} %w_ref.4), custom_call_target="tpu_custom_call" | custom-call | tf_op jit(solution)/shard_map/pallas_call | solution.py:78
  15.7 1.2 collective-permute-start.22
  17.0 0.6 broadcast_select_fusion
  17.6 2.8 %shard_map.120 = bf16[128,1024]{1,0:T(8,128)(2,1)} custom-call(s32[20,2]{1,0:T(8,128)} %get-tuple-element.18.place_ref, bf16[128,2560]{1,0:T(8,128)(2,1)} %attn_ref.1, bf16[20,2,128,128]{3,2,1,0:T(8,128)(2,1)} %w_ref.5), custom_call_target="tpu_custom_call" | custom-call | tf_op jit(solution)/shard_map/pallas_call | solution.py:78
  20.5 1.9 %convolution_convert_fusion.13 = bf16[128,256]{1,0:T(8,128)(2,1)} fusion(bf16[128,1024]{1,0:T(8,128)(2,1)} %shard_map.120, bf16[1024,256]{1,0:T(8,128)(2,1)S(1)} %copy-done.1), kind=kOutput, calls=%fused_computation.36 | convolution fusion | flops 67141632 | bytes 851968 | tf_op jit(solution)/shard_map/dot_general | solution.py:41
  22.4 0.6 pad_add_fusion.where_ref
  24.2 1.2 convolution_convert_fusion.12
  25.4 0.9 pad_maximum_fusion.4.refs_0_
  27.4 2.3 %collective-permute-start.9 = (bf16[1024,256]{1,0:T(8,128)(2,1)S(1)}, bf16[1024,256]{1,0:T(8,128)(2,1)S(1)}, u32[]{:S(2)}, u32[]{:S(2)}) collective-permute-start(bf16[1024,256]{1,0:T(8,128)(2,1)S(1)} %collective-permute-done.2), channel_id=1, source_target_pairs={{0,28},{4,8},{8,4},{12,16},{16,12},{20,24},{24,20},{28,0},{1,29},{... | collective-permute-start | bytes 1572872 | tf_op jit(solution)/shard_map/ppermute | solution.py:314
  30.2 0.7 pad_maximum_fusion.1.refs_2_
  30.9 0.7 collective-permute-start.6
  31.6 8.8 %collective-permute-done.22 = bf16[128,4096]{1,0:T(8,128)(2,1)S(1)} collective-permute-done((bf16[128,4096]{1,0:T(8,128)(2,1)}, bf16[128,4096]{1,0:T(8,128)(2,1)S(1)}, u32[]{:S(2)}, u32[]{:S(2)}) %collective-permute-start.22) | collective-permute-done | bytes 1048608 | tf_op jit(solution)/shard_map/ppermute | solution.py:22
  41.9 0.9 collective-permute-start.12
  42.8 1.0 collective-permute-start.10
  44.8 1.5 collective-permute-start.14
  47.4 6.4 %collective-permute-done.12 = bf16[1024,256]{1,0:T(8,128)(2,1)S(1)} collective-permute-done((bf16[1024,256]{1,0:T(8,128)(2,1)S(1)}, bf16[1024,256]{1,0:T(8,128)(2,1)S(1)}, u32[]{:S(2)}, u32[]{:S(2)}) %collective-permute-start.12) | collective-permute-done | bytes 524320 | tf_op jit(solution)/shard_map/ppermute | solution.py:314
  53.8 2.5 %collective-permute-start.8 = (bf16[1024,256]{1,0:T(8,128)(2,1)S(1)}, bf16[1024,256]{1,0:T(8,128)(2,1)S(1)}, u32[]{:S(2)}, u32[]{:S(2)}) collective-permute-start(bf16[1024,256]{1,0:T(8,128)(2,1)S(1)} %collective-permute-done.7), channel_id=1, source_target_pairs={{0,2},{2,0},{1,3},{3,1},{4,6},{6,4},{5,7},{7,5},{8,10},{10,8},{9,1... | collective-permute-start | bytes 1572872 | tf_op jit(solution)/shard_map/ppermute | solution.py:18
  56.3 3.2 %collective-permute-done.14 = bf16[1024,256]{1,0:T(8,128)(2,1)S(1)} collective-permute-done((bf16[1024,256]{1,0:T(8,128)(2,1)S(1)}, bf16[1024,256]{1,0:T(8,128)(2,1)S(1)}, u32[]{:S(2)}, u32[]{:S(2)}) %collective-permute-start.14) | collective-permute-done | bytes 524320 | tf_op jit(solution)/shard_map/ppermute | solution.py:314
  59.5 1.5 collective-permute-start.18
  63.4 1.2 collective-permute-start.13
  64.6 3.1 %collective-permute-done.18 = bf16[512,256]{1,0:T(8,128)(2,1)S(1)} collective-permute-done((bf16[512,256]{1,0:T(8,128)(2,1)S(1)}, bf16[512,256]{1,0:T(8,128)(2,1)S(1)}, u32[]{:S(2)}, u32[]{:S(2)}) %collective-permute-start.18) | collective-permute-done | bytes 262176 | tf_op jit(solution)/shard_map/ppermute | solution.py:314
  67.7 1.7 collective-permute-start.15
  69.7 0.6 collective-permute-start.20
  72.3 0.7 collective-permute-done.19
  73.0 1.2 collective-permute-start.11
  76.0 1.3 collective-permute-start.16
  77.5 8.6 %collective-permute-done.23.hg1 = bf16[128,1024]{1,0:T(8,128)(2,1)S(1)} collective-permute-done((bf16[128,1024]{1,0:T(8,128)(2,1)S(1)}, bf16[128,1024]{1,0:T(8,128)(2,1)S(1)}, u32[]{:S(2)}, u32[]{:S(2)}) %collective-permute-start.23) | collective-permute-done | bytes 262176 | tf_op jit(solution)/shard_map/ppermute | solution.py:22
  86.1 0.7 copy-done.8
  86.8 3.3 %shard_map.125 = (f32[1280,128]{1,0:T(8,128)}, bf16[1280,128]{1,0:T(8,128)(2,1)}) custom-call(s32[2]{0:T(128)} %pad_add_fusion.where_ref, s32[10,2]{1,0:T(8,128)} %dynamic-slice_add_fusion.place_ref, bf16[128,1024]{1,0:T(8,128)(2,1)} %copy-done.4, bf16[128,1024]{1,0:T(8,128)(2,1)} %copy-done.8, bf16[128,2560]{1,0:T(8,128)(2,1)} %attn_ref.1), custom_call_target="tpu_custom_call" | custom-call | tf_op jit(solution)/shard_map/pallas_call | solution.py:172
  90.1 2.1 %collective-permute-start.24 = (bf16[1280,128]{1,0:T(8,128)(2,1)}, bf16[1280,128]{1,0:T(8,128)(2,1)S(1)}, u32[]{:S(2)}, u32[]{:S(2)}) collective-permute-start(bf16[1280,128]{1,0:T(8,128)(2,1)} %get-tuple-element.13), channel_id=1, source_target_pairs={{0,2},{2,0},{1,3},{3,1},{4,6},{6,4},{5,7},{7,5},{8,10},{10,8},{9,1... | collective-permute-start | bytes 983048 | tf_op jit(solution)/shard_map/ppermute | solution.py:18
  92.3 1.3 collective-permute-start.21
  93.6 3.8 %collective-permute-done.21.refs_9_ = bf16[128,512]{1,0:T(8,128)(2,1)S(1)} collective-permute-done((bf16[128,512]{1,0:T(8,128)(2,1)S(1)}, bf16[128,512]{1,0:T(8,128)(2,1)S(1)}, u32[]{:S(2)}, u32[]{:S(2)}) %collective-permute-start.21) | collective-permute-done | bytes 131104 | tf_op jit(solution)/shard_map/ppermute | solution.py:22
  98.0 0.7 copy-done.14
  98.7 5.6 %shard_map.122 = (bf16[128,2560]{1,0:T(8,128)(2,1)}, f32[2560,128]{1,0:T(8,128)}, bf16[2560,128]{1,0:T(8,128)(2,1)}) custom-call(s32[2]{0:T(128)} %pad_add_fusion.where_ref, s32[20,2]{1,0:T(8,128)} %fusion.50.place_ref, bf16[128,512]{1,0:T(8,128)(2,1)} %copy-done.11, bf16[128,512]{1,0:T(8,128)(2,1)} %collective-permute-done.1.refs_1_, ...), custom_call_target="tpu_custom_call" | custom-call | tf_op jit(solution)/shard_map/pallas_call | solution.py:136
  104.3 0.9 collective-permute-start.25
  105.3 1.9 collective-permute-done.25
  107.4 21.8 %all_to_all.15 = bf16[8,480,128]{2,1,0:T(8,128)(2,1)S(1)} all-to-all(bf16[8,480,128]{2,1,0:T(8,128)(2,1)S(1)} %bitcast.58), channel_id=1, replica_groups=mesh['xh'=2,'y'=4,'z'=8,'c'=2,'xl'=2] {'xh','y'}, dimensions={0} | all-to-all | bytes 1966080 | tf_op jit(solution)/shard_map/all_to_all | solution.py:276
  129.5 28.2 %all_to_all.16 = bf16[8,480,128]{2,1,0:T(8,128)(2,1)S(1)} all-to-all(bf16[8,480,128]{2,1,0:T(8,128)(2,1)S(1)} %broadcast_in_dim.10), channel_id=1, replica_groups=mesh['xh'=2,'y'=4,'z'=8,'c'=2,'xl'=2] {'z'}, dimensions={0} | all-to-all | bytes 1966080 | tf_op jit(solution)/shard_map/all_to_all | solution.py:279
  158.0 17.4 %all_to_all.17 = bf16[8,480,128]{2,1,0:T(8,128)(2,1)S(1)} all-to-all(bf16[8,480,128]{2,1,0:T(8,128)(2,1)S(1)} %broadcast_in_dim.11), channel_id=1, replica_groups=mesh['xh'=2,'y'=4,'z'=8,'c'=2,'xl'=2] {'xh','y'}, dimensions={0} | all-to-all | bytes 1966080 | tf_op jit(solution)/shard_map/all_to_all | solution.py:282
  175.4 4.6 %collective-permute-start.26 = (bf16[3840,128]{1,0:T(8,128)(2,1)S(1)}, bf16[3840,128]{1,0:T(8,128)(2,1)S(1)}, u32[]{:S(2)}, u32[]{:S(2)}) collective-permute-start(bf16[3840,128]{1,0:T(8,128)(2,1)S(1)} %bitcast.56), channel_id=1, source_target_pairs={{0,2},{2,0},{1,3},{3,1},{4,6},{6,4},{5,7},{7,5},{8,10},{10,8},{9,1... | collective-permute-start | bytes 2949128 | tf_op jit(solution)/shard_map/ppermute | solution.py:18
  180.0 3.2 %shard_map.124 = bf16[128,1280]{1,0:T(8,128)(2,1)} custom-call(s32[2]{0:T(128)} %pad_add_fusion.where_ref, s32[10,2]{1,0:T(8,128)} %dynamic-slice_add_fusion.place_ref, bf16[128,1024]{1,0:T(8,128)(2,1)} %copy-done.4, bf16[128,1024]{1,0:T(8,128)(2,1)} %copy-done.8, bf16[20,2,128,128]{3,2,1,0:T(8,128)(2,1)} %w_ref.5), custom_call_target="tpu_custom_call" | custom-call | tf_op jit(solution)/shard_map/pallas_call | solution.py:201
  183.2 1.0 copy-done.9
  184.2 4.3 %shard_map.126 = (f32[2,1280,128]{2,1,0:T(8,128)}, f32[2,2560,128]{2,1,0:T(8,128)}) custom-call(s32[2]{0:T(128)} %pad_add_fusion.where_ref, bf16[3840,128]{1,0:T(8,128)(2,1)} %bitcast.57, bf16[3840,128]{1,0:T(8,128)(2,1)} %copy-done.9), custom_call_target="tpu_custom_call" | custom-call | tf_op jit(solution)/shard_map/pallas_call | solution.py:252
  (110 shorter events, 14.3 us)
Async XLA Ops:
  0.6 11.0 %copy-start.16 = (s32[20,2]{0,1:T(2,128)S(1)}, s32[20,2]{0,1:T(2,128)}, u32[]{:S(2)}) copy-start(s32[20,2]{0,1:T(2,128)} %param.17) | copy-start | bytes 484
  3.5 13.4 %copy-start.17 = (s32[20,2]{0,1:T(2,128)S(1)}, s32[20,2]{0,1:T(2,128)}, u32[]{:S(2)}) copy-start(s32[20,2]{0,1:T(2,128)} %param.15) | copy-start | bytes 484
  3.5 20.1 %collective-permute-start.2 = (bf16[1024,256]{1,0:T(8,128)(2,1)}, bf16[1024,256]{1,0:T(8,128)(2,1)S(1)}, u32[]{:S(2)}, u32[]{:S(2)}) collective-permute-start(bf16[1024,256]{1,0:T(8,128)(2,1)} %shard_map.121), channel_id=1, source_target_pairs={{0,4},{4,0},{8,12},{12,8},{16,20},{20,16},{24,28},{28,24},{1,5},{5... | collective-permute-start | bytes 1572872 | tf_op jit(solution)/shard_map/ppermute | solution.py:314
  6.0 18.2 %collective-permute-start = (bf16[1024,256]{1,0:T(8,128)(2,1)}, bf16[1024,256]{1,0:T(8,128)(2,1)S(1)}, u32[]{:S(2)}, u32[]{:S(2)}) collective-permute-start(bf16[1024,256]{1,0:T(8,128)(2,1)} %shard_map.121), channel_id=1, source_target_pairs={{0,2},{2,0},{1,3},{3,1},{4,6},{6,4},{5,7},{7,5},{8,10},{10,8},{9,1... | collective-permute-start | bytes 1572872 | tf_op jit(solution)/shard_map/ppermute | solution.py:18
  6.9 19.6 %collective-permute-start.4 = (bf16[1024,256]{1,0:T(8,128)(2,1)}, bf16[1024,256]{1,0:T(8,128)(2,1)S(1)}, u32[]{:S(2)}, u32[]{:S(2)}) collective-permute-start(bf16[1024,256]{1,0:T(8,128)(2,1)} %shard_map.121), channel_id=1, source_target_pairs={{0,28},{4,8},{8,4},{12,16},{16,12},{20,24},{24,20},{28,0},{1,29},{... | collective-permute-start | bytes 1572872 | tf_op jit(solution)/shard_map/ppermute | solution.py:314
  12.3 8.1 %copy-start.1 = (bf16[1024,256]{1,0:T(8,128)(2,1)S(1)}, bf16[1024,256]{1,0:T(8,128)(2,1)}, u32[]{:S(2)}) copy-start(bf16[1024,256]{1,0:T(8,128)(2,1)} %shard_map.121) | copy-start | bytes 1572868
  15.7 24.6 %collective-permute-start.22 = (bf16[128,4096]{1,0:T(8,128)(2,1)}, bf16[128,4096]{1,0:T(8,128)(2,1)S(1)}, u32[]{:S(2)}, u32[]{:S(2)}) collective-permute-start(bf16[128,4096]{1,0:T(8,128)(2,1)} %shard_map.123), channel_id=1, source_target_pairs={{0,1},{1,0},{2,3},{3,2},{4,5},{5,4},{6,7},{7,6},{8,9},{9,8},{10,11... | collective-permute-start | bytes 3145736 | tf_op jit(solution)/shard_map/ppermute | solution.py:22
  20.5 6.4 %copy-start = (bf16[128,1024]{1,0:T(8,128)(2,1)S(1)}, bf16[128,1024]{1,0:T(8,128)(2,1)}, u32[]{:S(2)}) copy-start(bf16[128,1024]{1,0:T(8,128)(2,1)} %shard_map.120) | copy-start | bytes 786436
  23.6 3.8 %collective-permute-start.3 = (bf16[1024,256]{1,0:T(8,128)(2,1)S(1)}, bf16[1024,256]{1,0:T(8,128)(2,1)S(1)}, u32[]{:S(2)}, u32[]{:S(2)}) collective-permute-start(bf16[1024,256]{1,0:T(8,128)(2,1)S(1)} %collective-permute-done.2), channel_id=1, source_target_pairs={{0,2},{2,0},{1,3},{3,1},{4,6},{6,4},{5,7},{7,5},{8,10},{10,8},{9,1... | collective-permute-start | bytes 1572872 | tf_op jit(solution)/shard_map/ppermute | solution.py:18
  26.2 4.7 %copy-start.11 = (bf16[128,512]{1,0:T(8,128)(2,1)}, bf16[128,512]{1,0:T(8,128)(2,1)S(1)}, u32[]{:S(2)}) copy-start(bf16[128,512]{1,0:T(8,128)(2,1)S(1)} %pad_maximum_fusion.4.refs_0_) | copy-start | bytes 393220
  26.2 14.2 %copy-start.2 = (bf16[128,4096]{1,0:T(8,128)(2,1)S(1)}, bf16[128,4096]{1,0:T(8,128)(2,1)}, u32[]{:S(2)}) copy-start(bf16[128,4096]{1,0:T(8,128)(2,1)} %shard_map.123) | copy-start | bytes 3145732
  26.2 66.0 %collective-permute-start.1 = (bf16[128,512]{1,0:T(8,128)(2,1)S(1)}, bf16[128,512]{1,0:T(8,128)(2,1)}, u32[]{:S(2)}, u32[]{:S(2)}) collective-permute-start(bf16[128,512]{1,0:T(8,128)(2,1)S(1)} %pad_maximum_fusion.4.refs_0_), channel_id=1, source_target_pairs={{0,1},{1,0},{2,3},{3,2},{4,5},{5,4},{6,7},{7,6},{8,9},{9,8},{10,11... | collective-permute-start | bytes 393224 | tf_op jit(solution)/shard_map/ppermute | solution.py:22
  26.6 17.9 %collective-permute-start.7 = (bf16[1024,256]{1,0:T(8,128)(2,1)S(1)}, bf16[1024,256]{1,0:T(8,128)(2,1)S(1)}, u32[]{:S(2)}, u32[]{:S(2)}) collective-permute-start(bf16[1024,256]{1,0:T(8,128)(2,1)S(1)} %collective-permute-done.4), channel_id=1, source_target_pairs={{0,4},{4,0},{8,12},{12,8},{16,20},{20,16},{24,28},{28,24},{1,5},{5... | collective-permute-start | bytes 1572872 | tf_op jit(solution)/shard_map/ppermute | solution.py:314
  26.6 3.4 %collective-permute-start.5 = (bf16[1024,256]{1,0:T(8,128)(2,1)S(1)}, bf16[1024,256]{1,0:T(8,128)(2,1)S(1)}, u32[]{:S(2)}, u32[]{:S(2)}) collective-permute-start(bf16[1024,256]{1,0:T(8,128)(2,1)S(1)} %collective-permute-done.4), channel_id=1, source_target_pairs={{0,2},{2,0},{1,3},{3,1},{4,6},{6,4},{5,7},{7,5},{8,10},{10,8},{9,1... | collective-permute-start | bytes 1572872 | tf_op jit(solution)/shard_map/ppermute | solution.py:18
  27.4 14.6 %collective-permute-start.9 = (bf16[1024,256]{1,0:T(8,128)(2,1)S(1)}, bf16[1024,256]{1,0:T(8,128)(2,1)S(1)}, u32[]{:S(2)}, u32[]{:S(2)}) collective-permute-start(bf16[1024,256]{1,0:T(8,128)(2,1)S(1)} %collective-permute-done.2), channel_id=1, source_target_pairs={{0,28},{4,8},{8,4},{12,16},{16,12},{20,24},{24,20},{28,0},{1,29},{... | collective-permute-start | bytes 1572872 | tf_op jit(solution)/shard_map/ppermute | solution.py:314
  30.9 62.6 %collective-permute-start.6 = (bf16[128,1024]{1,0:T(8,128)(2,1)}, bf16[128,1024]{1,0:T(8,128)(2,1)}, u32[]{:S(2)}, u32[]{:S(2)}) collective-permute-start(bf16[128,1024]{1,0:T(8,128)(2,1)} %pad_maximum_fusion.1.refs_2_), channel_id=1, source_target_pairs={{0,1},{1,0},{2,3},{3,2},{4,5},{5,4},{6,7},{7,6},{8,9},{9,8},{10,11... | collective-permute-start | bytes 786440 | tf_op jit(solution)/shard_map/ppermute | solution.py:22
  41.9 11.9 %collective-permute-start.12 = (bf16[1024,256]{1,0:T(8,128)(2,1)S(1)}, bf16[1024,256]{1,0:T(8,128)(2,1)S(1)}, u32[]{:S(2)}, u32[]{:S(2)}) collective-permute-start(bf16[1024,256]{1,0:T(8,128)(2,1)S(1)} %collective-permute-done.9), channel_id=1, source_target_pairs={{0,4},{4,0},{8,12},{12,8},{16,20},{20,16},{24,28},{28,24},{1,5},{5... | collective-permute-start | bytes 1572872 | tf_op jit(solution)/shard_map/ppermute | solution.py:314
  42.8 18.7 %collective-permute-start.10 = (bf16[1024,256]{1,0:T(8,128)(2,1)S(1)}, bf16[1024,256]{1,0:T(8,128)(2,1)S(1)}, u32[]{:S(2)}, u32[]{:S(2)}) collective-permute-start(bf16[1024,256]{1,0:T(8,128)(2,1)S(1)} %collective-permute-done.9), channel_id=1, source_target_pairs={{0,2},{2,0},{1,3},{3,1},{4,6},{6,4},{5,7},{7,5},{8,10},{10,8},{9,1... | collective-permute-start | bytes 1572872 | tf_op jit(solution)/shard_map/ppermute | solution.py:18
  44.8 14.8 %collective-permute-start.14 = (bf16[1024,256]{1,0:T(8,128)(2,1)S(1)}, bf16[1024,256]{1,0:T(8,128)(2,1)S(1)}, u32[]{:S(2)}, u32[]{:S(2)}) collective-permute-start(bf16[1024,256]{1,0:T(8,128)(2,1)S(1)} %collective-permute-done.7), channel_id=1, source_target_pairs={{0,28},{4,8},{8,4},{12,16},{16,12},{20,24},{24,20},{28,0},{1,29},{... | collective-permute-start | bytes 1572872 | tf_op jit(solution)/shard_map/ppermute | solution.py:314
  53.8 8.7 %collective-permute-start.8 = (bf16[1024,256]{1,0:T(8,128)(2,1)S(1)}, bf16[1024,256]{1,0:T(8,128)(2,1)S(1)}, u32[]{:S(2)}, u32[]{:S(2)}) collective-permute-start(bf16[1024,256]{1,0:T(8,128)(2,1)S(1)} %collective-permute-done.7), channel_id=1, source_target_pairs={{0,2},{2,0},{1,3},{3,1},{4,6},{6,4},{5,7},{7,5},{8,10},{10,8},{9,1... | collective-permute-start | bytes 1572872 | tf_op jit(solution)/shard_map/ppermute | solution.py:18
  59.5 8.2 %collective-permute-start.18 = (bf16[512,256]{1,0:T(8,128)(2,1)S(1)}, bf16[512,256]{1,0:T(8,128)(2,1)S(1)}, u32[]{:S(2)}, u32[]{:S(2)}) collective-permute-start(bf16[512,256]{1,0:T(8,128)(2,1)S(1)} %slice.85), channel_id=1, source_target_pairs={{0,28},{4,8},{8,4},{12,16},{16,12},{20,24},{24,20},{28,0},{1,29},{... | collective-permute-start | bytes 786440 | tf_op jit(solution)/shard_map/ppermute | solution.py:314
  61.5 8.2 %collective-permute-start.17 = (bf16[512,256]{1,0:T(8,128)(2,1)S(1)}, bf16[512,256]{1,0:T(8,128)(2,1)S(1)}, u32[]{:S(2)}, u32[]{:S(2)}) collective-permute-start(bf16[512,256]{1,0:T(8,128)(2,1)S(1)} %slice.83), channel_id=1, source_target_pairs={{0,4},{4,0},{8,12},{12,8},{16,20},{20,16},{24,28},{28,24},{1,5},{5... | collective-permute-start | bytes 786440 | tf_op jit(solution)/shard_map/ppermute | solution.py:314
  63.4 11.1 %copy-start.6 = (bf16[128,1024]{1,0:T(8,128)(2,1)}, bf16[128,1024]{1,0:T(8,128)(2,1)S(1)}, u32[]{:S(2)}) copy-start(bf16[128,1024]{1,0:T(8,128)(2,1)S(1)} %pad_maximum_fusion.2.refs_4_) | copy-start | bytes 786436
  63.4 11.1 %collective-permute-start.13 = (bf16[1024,256]{1,0:T(8,128)(2,1)S(1)}, bf16[1024,256]{1,0:T(8,128)(2,1)S(1)}, u32[]{:S(2)}, u32[]{:S(2)}) collective-permute-start(bf16[1024,256]{1,0:T(8,128)(2,1)S(1)} %collective-permute-done.12), channel_id=1, source_target_pairs={{0,2},{2,0},{1,3},{3,1},{4,6},{6,4},{5,7},{7,5},{8,10},{10,8},{9,1... | collective-permute-start | bytes 1572872 | tf_op jit(solution)/shard_map/ppermute | solution.py:18
  67.7 7.1 %collective-permute-start.15 = (bf16[1024,256]{1,0:T(8,128)(2,1)S(1)}, bf16[1024,256]{1,0:T(8,128)(2,1)S(1)}, u32[]{:S(2)}, u32[]{:S(2)}) collective-permute-start(bf16[1024,256]{1,0:T(8,128)(2,1)S(1)} %collective-permute-done.14), channel_id=1, source_target_pairs={{0,2},{2,0},{1,3},{3,1},{4,6},{6,4},{5,7},{7,5},{8,10},{10,8},{9,1... | collective-permute-start | bytes 1572872 | tf_op jit(solution)/shard_map/ppermute | solution.py:18
  69.7 1.8 collective-permute-start.20
  71.5 1.5 collective-permute-start.19
  73.0 20.5 %collective-permute-start.11 = (bf16[128,1024]{1,0:T(8,128)(2,1)S(1)}, bf16[128,1024]{1,0:T(8,128)(2,1)S(1)}, u32[]{:S(2)}, u32[]{:S(2)}) collective-permute-start(bf16[128,1024]{1,0:T(8,128)(2,1)S(1)} %pad_maximum_fusion.2.refs_4_), channel_id=1, source_target_pairs={{0,1},{1,0},{2,3},{3,2},{4,5},{5,4},{6,7},{7,6},{8,9},{9,8},{10,11... | collective-permute-start | bytes 786440 | tf_op jit(solution)/shard_map/ppermute | solution.py:22
  75.1 11.0 %copy-start.4 = (bf16[128,1024]{1,0:T(8,128)(2,1)}, bf16[128,1024]{1,0:T(8,128)(2,1)S(1)}, u32[]{:S(2)}) copy-start(bf16[128,1024]{1,0:T(8,128)(2,1)S(1)} %fusion.8.hg0) | copy-start | bytes 786436
  75.1 11.0 %collective-permute-start.23 = (bf16[128,1024]{1,0:T(8,128)(2,1)S(1)}, bf16[128,1024]{1,0:T(8,128)(2,1)S(1)}, u32[]{:S(2)}, u32[]{:S(2)}) collective-permute-start(bf16[128,1024]{1,0:T(8,128)(2,1)S(1)} %fusion.8.hg0), channel_id=1, source_target_pairs={{0,1},{1,0},{2,3},{3,2},{4,5},{5,4},{6,7},{7,6},{8,9},{9,8},{10,11... | collective-permute-start | bytes 786440 | tf_op jit(solution)/shard_map/ppermute | solution.py:22
  76.0 21.4 %copy-start.7 = (bf16[128,1024]{1,0:T(8,128)(2,1)}, bf16[128,1024]{1,0:T(8,128)(2,1)S(1)}, u32[]{:S(2)}) copy-start(bf16[128,1024]{1,0:T(8,128)(2,1)S(1)} %pad_maximum_fusion.3.refs_6_) | copy-start | bytes 786436
  76.0 21.4 %collective-permute-start.16 = (bf16[128,1024]{1,0:T(8,128)(2,1)S(1)}, bf16[128,1024]{1,0:T(8,128)(2,1)S(1)}, u32[]{:S(2)}, u32[]{:S(2)}) collective-permute-start(bf16[128,1024]{1,0:T(8,128)(2,1)S(1)} %pad_maximum_fusion.3.refs_6_), channel_id=1, source_target_pairs={{0,1},{1,0},{2,3},{3,2},{4,5},{5,4},{6,7},{7,6},{8,9},{9,8},{10,11... | collective-permute-start | bytes 786440 | tf_op jit(solution)/shard_map/ppermute | solution.py:22
  86.1 0.7 copy-start.8
  90.1 15.0 %collective-permute-start.24 = (bf16[1280,128]{1,0:T(8,128)(2,1)}, bf16[1280,128]{1,0:T(8,128)(2,1)S(1)}, u32[]{:S(2)}, u32[]{:S(2)}) collective-permute-start(bf16[1280,128]{1,0:T(8,128)(2,1)} %get-tuple-element.13), channel_id=1, source_target_pairs={{0,2},{2,0},{1,3},{3,1},{4,6},{6,4},{5,7},{7,5},{8,10},{10,8},{9,1... | collective-permute-start | bytes 983048 | tf_op jit(solution)/shard_map/ppermute | solution.py:18
  92.2 5.2 %copy-start.12 = (bf16[128,512]{1,0:T(8,128)(2,1)}, bf16[128,512]{1,0:T(8,128)(2,1)S(1)}, u32[]{:S(2)}) copy-start(bf16[128,512]{1,0:T(8,128)(2,1)S(1)} %pad_maximum_fusion.5.refs_8_) | copy-start | bytes 393220
  92.2 13.0 %copy-start.10 = (f32[1280,128]{1,0:T(8,128)S(1)}, f32[1280,128]{1,0:T(8,128)}, u32[]{:S(2)}) copy-start(f32[1280,128]{1,0:T(8,128)} %get-tuple-element.12) | copy-start | bytes 1966084
  92.3 5.1 %collective-permute-start.21 = (bf16[128,512]{1,0:T(8,128)(2,1)S(1)}, bf16[128,512]{1,0:T(8,128)(2,1)S(1)}, u32[]{:S(2)}, u32[]{:S(2)}) collective-permute-start(bf16[128,512]{1,0:T(8,128)(2,1)S(1)} %pad_maximum_fusion.5.refs_8_), channel_id=1, source_target_pairs={{0,1},{1,0},{2,3},{3,2},{4,5},{5,4},{6,7},{7,6},{8,9},{9,8},{10,11... | collective-permute-start | bytes 393224 | tf_op jit(solution)/shard_map/ppermute | solution.py:22
  93.6 3.9 %copy-start.13 = (bf16[128,1024]{1,0:T(8,128)(2,1)}, bf16[128,1024]{1,0:T(8,128)(2,1)S(1)}, u32[]{:S(2)}) copy-start(bf16[128,1024]{1,0:T(8,128)(2,1)S(1)} %collective-permute-done.11.refs_5_) | copy-start | bytes 786436
  97.4 0.6 copy-start.15
  98.0 0.7 copy-start.14
  104.3 2.8 %copy-start.5 = (f32[2560,128]{1,0:T(8,128)S(1)}, f32[2560,128]{1,0:T(8,128)}, u32[]{:S(2)}) copy-start(f32[2560,128]{1,0:T(8,128)} %get-tuple-element.14) | copy-start | bytes 3932164
  104.3 2.8 %collective-permute-start.25 = (bf16[2560,128]{1,0:T(8,128)(2,1)}, bf16[2560,128]{1,0:T(8,128)(2,1)S(1)}, u32[]{:S(2)}, u32[]{:S(2)}) collective-permute-start(bf16[2560,128]{1,0:T(8,128)(2,1)} %get-tuple-element.15), channel_id=1, source_target_pairs={{0,2},{2,0},{1,3},{3,1},{4,6},{6,4},{5,7},{7,5},{8,10},{10,8},{9,1... | collective-permute-start | bytes 1966088 | tf_op jit(solution)/shard_map/ppermute | solution.py:18
  175.4 7.8 %copy-start.3 = (bf16[8,480,128]{2,1,0:T(8,128)(2,1)}, bf16[8,480,128]{2,1,0:T(8,128)(2,1)S(1)}, u32[]{:S(2)}) copy-start(bf16[8,480,128]{2,1,0:T(8,128)(2,1)S(1)} %all_to_all.17) | copy-start | bytes 2949124
  175.4 7.8 %collective-permute-start.26 = (bf16[3840,128]{1,0:T(8,128)(2,1)S(1)}, bf16[3840,128]{1,0:T(8,128)(2,1)S(1)}, u32[]{:S(2)}, u32[]{:S(2)}) collective-permute-start(bf16[3840,128]{1,0:T(8,128)(2,1)S(1)} %bitcast.56), channel_id=1, source_target_pairs={{0,2},{2,0},{1,3},{3,1},{4,6},{6,4},{5,7},{7,5},{8,10},{10,8},{9,1... | collective-permute-start | bytes 2949128 | tf_op jit(solution)/shard_map/ppermute | solution.py:18
  183.2 1.0 copy-start.9

commit v4 on v3

--- a/solution.py
+++ b/solution.py
@@ -12,6 +12,8 @@
 HG_NEW = 20
 BO_OLD = 32
 PAIR = [(0, 1), (1, 0)]
+Z = ("zh", "zl")
+TOKENS = ("xh", "y", *Z, "c")
 
 
 def swap_cores(x):
@@ -28,8 +30,8 @@
 
 def arrival_place(cols):
     shard = cols // 2
-    z = lax.axis_index("z")
-    away = (shard // 2 - z) * (2 * (z % 2) - 1) % lax.axis_size("z")
+    z = lax.axis_index(Z)
+    away = (shard // 2 - z) * (2 * (z % 2) - 1) % lax.axis_size(Z)
     base = jnp.where(away < 4, 8 * away, 60 - 8 * away)
     return base + 2 * (shard % 2 != lax.axis_index("c")) + cols % 2
 
@@ -49,7 +51,17 @@
     )
 
 
+HERE = pl.BlockSpec(memory_space=pltpu.VMEM)
+VMEM = pltpu.VMEM
 SMEM = pl.BlockSpec(memory_space=pltpu.SMEM)
+
+
+def grant(mib):
+    return pltpu.CompilerParams(vmem_limit_bytes=mib << 20)
+
+
+def near(x):
+    return pltpu.with_memory_space_constraint(x, VMEM)
 
 
 def times(x, w, dims):
@@ -77,10 +89,11 @@
     full = pl.BlockSpec(memory_space=pltpu.VMEM)
     return pl.pallas_call(
         kernel,
-        out_shape=jax.ShapeDtypeStruct((tok, used * HEAD), jnp.bfloat16),
+        out_shape=VMEM((tok, used * HEAD), jnp.bfloat16),
         in_specs=[SMEM, full, full],
         out_specs=full,
         scratch_shapes=[pltpu.VMEM((slots, tok, HEAD), jnp.float32)],
+        compiler_params=grant(16),
     )(place, x, blocks)
 
 
@@ -130,20 +143,21 @@
 
     out_shape = [
         jax.ShapeDtypeStruct((tok, rows * HEAD), jnp.bfloat16),
-        jax.ShapeDtypeStruct((rows * HEAD, HEAD), jnp.float32),
-        jax.ShapeDtypeStruct((rows * HEAD, HEAD), jnp.bfloat16),
+        VMEM((rows * HEAD, HEAD), jnp.float32),
+        VMEM((rows * HEAD, HEAD), jnp.bfloat16),
     ]
     return pl.pallas_call(
         kernel,
         grid_spec=pltpu.PrefetchScalarGridSpec(
             num_scalar_prefetch=2,
             grid=(1,),
-            in_specs=[whole(x) for x in (*chunks, cotangent, blocks)],
-            out_specs=[whole(x) for x in out_shape],
+            in_specs=[*[HERE for _ in chunks], whole(cotangent), whole(blocks)],
+            out_specs=[whole(out_shape[0]), HERE, HERE],
             scratch_shapes=[vmem(BO_OLD, tok, HEAD), vmem(rows, tok, HEAD)],
         ),
         out_shape=out_shape,
-    )(where, place, *chunks, cotangent, blocks)
+        compiler_params=grant(20),
+    )(where, place, *map(near, chunks), cotangent, blocks)
 
 
 def head_terms(where, place, hidden_grads, attn_out):
@@ -166,8 +180,8 @@
                     dst[at : at + HEAD, :] = both[:, k * HEAD : (k + 1) * HEAD]
 
     out_shape = [
-        jax.ShapeDtypeStruct((rows * HEAD, HEAD), jnp.float32),
-        jax.ShapeDtypeStruct((rows * HEAD, HEAD), jnp.bfloat16),
+        VMEM((rows * HEAD, HEAD), jnp.float32),
+        VMEM((rows * HEAD, HEAD), jnp.bfloat16),
     ]
     return pl.pallas_call(
         kernel,
@@ -175,14 +189,15 @@
             num_scalar_prefetch=2,
             grid=(1,),
             in_specs=[
-                *[whole(x) for x in hidden_grads],
+                *[HERE for _ in hidden_grads],
                 pl.BlockSpec((tok, rows * HEAD), lambda i, w, *_: (0, w[1])),
             ],
-            out_specs=[whole(x) for x in out_shape],
+            out_specs=[HERE, HERE],
             scratch_shapes=[vmem(HG_OLD, tok, HEAD), vmem(rows, tok, HEAD)],
         ),
         out_shape=out_shape,
-    )(where, place, *hidden_grads, attn_out)
+        compiler_params=grant(12),
+    )(where, place, *map(near, hidden_grads), attn_out)
 
 
 def head_grads(where, place, hidden_grads, blocks):
@@ -204,14 +219,15 @@
             num_scalar_prefetch=2,
             grid=(1,),
             in_specs=[
-                *[whole(x) for x in hidden_grads],
+                *[HERE for _ in hidden_grads],
                 pl.BlockSpec((rows, 2, HEAD, HEAD), lambda i, w, *_: (w[1], 0, 0, 0)),
             ],
             out_specs=whole(out_shape),
             scratch_shapes=[vmem(HG_OLD, tok, HEAD)],
         ),
         out_shape=out_shape,
-    )(where, place, *hidden_grads, blocks)
+        compiler_params=grant(12),
+    )(where, place, *map(near, hidden_grads), blocks)
 
 
 def mix_layers(pick, coef, weights):
@@ -221,7 +237,8 @@
     def kernel(pick_ref, coef_ref, first_ref, second_ref, o_ref):
         total = coef_ref[0] * first_ref[0].astype(jnp.float32)
         total = total + coef_ref[1] * second_ref[0].astype(jnp.float32)
-        o_ref[...] = total.astype(jnp.bfloat16)
+        at = pl.multiple_of(pl.program_id(0) * (rows // steps), rows // steps)
+        o_ref[pl.ds(at, rows // steps), :] = total.astype(jnp.bfloat16)
 
     def layer(slot):
         return pl.BlockSpec((1, rows // steps, cols), lambda i, p, c: (p[slot], i, 0))
@@ -232,51 +249,58 @@
             num_scalar_prefetch=2,
             grid=(steps,),
             in_specs=[layer(0), layer(1)],
-            out_specs=pl.BlockSpec((rows // steps, cols), lambda i, p, c: (i, 0)),
-        ),
-        out_shape=jax.ShapeDtypeStruct((rows, cols), jnp.bfloat16),
+            out_specs=HERE,
+        ),
+        out_shape=VMEM((rows, cols), jnp.bfloat16),
+        compiler_params=grant(6),
     )(pick, coef, weights, weights)
 
 
 def unpack_sums(where, mine, theirs, cut):
-    rows = mine.shape[0]
+    steps = 2
+    most = mine.shape[0] - cut
+    small, large = cut // steps, most // steps
 
     def kernel(where_ref, mine_ref, theirs_ref, in_ref, out_ref):
-        for step, src in enumerate((mine_ref, theirs_ref)):
-
-            @pl.when(pl.program_id(0) == step)
+        i = pl.program_id(1)
+        for turn, src in enumerate((mine_ref, theirs_ref)):
+
+            @pl.when(pl.program_id(0) == turn)
             def _():
-                in_ref[0] = src[:cut, :].astype(jnp.float32)
-                out_ref[0] = src[cut:, :].astype(jnp.float32)
+                at = pl.multiple_of(i * small, small)
+                in_ref[0] = src[pl.ds(at, small), :].astype(jnp.float32)
+                at = pl.multiple_of(cut + i * large, small)
+                out_ref[0] = src[pl.ds(at, large), :].astype(jnp.float32)
+
+    def result(rows):
+        return pl.BlockSpec((1, rows, HEAD), lambda t, i, w: ((w[0] + t) % 2, i, 0))
 
     return pl.pallas_call(
         kernel,
         grid_spec=pltpu.PrefetchScalarGridSpec(
             num_scalar_prefetch=1,
-            grid=(2,),
-            in_specs=[whole(mine), whole(theirs)],
-            out_specs=[
-                pl.BlockSpec((1, cut, HEAD), lambda i, w: ((w[0] + i) % 2, 0, 0)),
-                pl.BlockSpec((1, rows - cut, HEAD), lambda i, w: ((w[0] + i) % 2, 0, 0)),
-            ],
+            grid=(2, steps),
+            in_specs=[HERE, HERE],
+            out_specs=[result(small), result(large)],
         ),
         out_shape=[
             jax.ShapeDtypeStruct((2, cut, HEAD), jnp.float32),
-            jax.ShapeDtypeStruct((2, rows - cut, HEAD), jnp.float32),
+            jax.ShapeDtypeStruct((2, most, HEAD), jnp.float32),
         ],
-    )(where, mine, theirs)
+        compiler_params=grant(14),
+    )(where, near(mine), near(theirs))
 
 
 def token_sum(keep, came, scale):
-    plane = ("xh", "y")
+    plane = ("xh", "y", "zl")
     n = lax.axis_size(plane)
     mine = [(k + c.astype(jnp.float32)).astype(jnp.bfloat16) for k, c in zip(keep, came)]
     mine = jnp.concatenate(mine, axis=0)
     rows = mine.shape[0]
     parts = lax.all_to_all(mine.reshape(n, rows // n, HEAD), plane, 0, 0, tiled=True)
     part = jnp.sum(parts.astype(jnp.float32), axis=0).astype(jnp.bfloat16)
-    spread = jnp.broadcast_to(part[None], (lax.axis_size("z"),) + part.shape)
-    parts = lax.all_to_all(spread, "z", 0, 0, tiled=True)
+    spread = jnp.broadcast_to(part[None], (lax.axis_size("zh"),) + part.shape)
+    parts = lax.all_to_all(spread, "zh", 0, 0, tiled=True)
     part = (jnp.sum(parts.astype(jnp.float32), axis=0) * scale).astype(jnp.bfloat16)
     spread = jnp.broadcast_to(part[None], (n,) + part.shape)
     return lax.all_to_all(spread, plane, 0, 0, tiled=True).reshape(rows, HEAD)
@@ -303,15 +327,16 @@
     out_place = arrival_place(out_cols).astype(jnp.int32)
     own = in_cols // local_blocks == tensor_half
     hidden_place = jnp.where(own, in_cols % local_blocks, local_blocks)
-    in_place = in_cols % local_blocks + jnp.where(own, 0, local_blocks)
-    in_place = lax.dynamic_slice_in_dim(in_place, tensor_half * rows_in, rows_in, 0)
-
-    n = lax.axis_size("z")
+    my_cols = lax.dynamic_slice_in_dim(in_cols, tensor_half * rows_in, rows_in, 0)
+    away = my_cols // local_blocks != tensor_half
+    in_place = my_cols % local_blocks + jnp.where(away, local_blocks, 0)
+
+    n = lax.axis_size(Z)
     even = [(i, i ^ 1) for i in range(n)]
     odd = [(i, (i - 1 + 2 * (i % 2)) % n) for i in range(n)]
 
     def hop(a, b):
-        return lax.ppermute(b, "z", even), lax.ppermute(a, "z", odd)
+        return lax.ppermute(b, Z, even), lax.ppermute(a, Z, odd)
 
     def cores(*pieces):
         return [q for p in pieces for q in (p, swap_cores(p))]
@@ -327,11 +352,11 @@
             at += 2
         return total
 
-    grad_part = scatter_blocks(cotangent, out_blocks, out_place, BO_OLD, BO_OLD, True)
-    grad_other = swap_halves(grad_part)
     mixed = mix_layers(depth_pick, depth_coef, old_weights)
     chunk0 = cores(mixed)
     a, b = hop(mixed, mixed)
+    grad_part = scatter_blocks(cotangent, out_blocks, out_place, BO_OLD, BO_OLD, True)
+    grad_other = swap_halves(grad_part)
     hidden = scatter_blocks(
         attn_out, in_blocks, hidden_place, local_blocks + 1, local_blocks, False
     )
@@ -362,7 +387,7 @@
     keep_in, send_in = head_terms(where, in_place, hidden_grads, attn_out)
     came_in = swap_cores(send_in)
     grad_attn = head_grads(where, in_place, hidden_grads, in_blocks)
-    grad_scale = float(tok_rows * lax.axis_size(("xh", "y", "z", "c"))) ** (-0.5)
+    grad_scale = float(tok_rows * lax.axis_size(TOKENS)) ** (-0.5)
     full = token_sum((keep_in, keep_out), (came_in, came_out), grad_scale)
     theirs = swap_cores(full)
     in_sum, out_sum = unpack_sums(where, full, theirs, rows_in * HEAD)
@@ -372,12 +397,11 @@
 
 
 def solution(mesh):
-    fine = Mesh(mesh.devices.reshape(2, 4, 8, 2, 2), ("xh", "y", "z", "c", "xl"))
-    tokens = ("xh", "y", "z", "c")
+    fine = Mesh(mesh.devices.reshape(2, 4, 4, 2, 2, 2), (*TOKENS, "xl"))
     placed = (
-        P(tokens, None),
-        P(tokens, "xl"),
-        P(None, "xl", ("z", "c")),
+        P(TOKENS, None),
+        P(TOKENS, "xl"),
+        P(None, "xl", (*Z, "c")),
         P(),
         P(),
         P(),
@@ -390,8 +414,8 @@
         mesh=fine,
         in_specs=placed,
         out_specs=(
-            P(tokens, "xl"),
-            P(tokens, "xl"),
+            P(TOKENS, "xl"),
+            P(TOKENS, "xl"),
             P("xl", None, None, None),
             P("xl", None, None, None),
         ),

time: 189 us -> 167 us (0.88)
  blocking collectives: 67.5 us -> 50.1 us
  Pallas kernels: 25.4 us -> 13.5 us
  matrix products: 11.8 us -> 15.4 us
  starting transfers between devices: 36.6 us -> 39.4 us
  other arithmetic: 4.95 us -> 2.51 us
    all_to_all x1, blocking collectives: 28.2 us -> 12.6 us  [token_sum(): parts = lax.all_to_all(spread, 'zh', 0, 0, tiled=True)]
    dot_general x18, matrix products: 5.16 us -> 8.29 us  [backward(): lax.dot_general(g, piece, (((1,), (1,)), ((), ())), preferred_element_typ...]
    pallas_call x1, Pallas kernels: 5.59 us -> 2.87 us  [width_rows(): pl.pallas_call(kernel, grid_spec=pltpu.PrefetchScalarGridSpec(num_scalar_...]
    pallas_call x2, Pallas kernels: 6.21 us -> 3.91 us  [scatter_blocks(): pl.pallas_call(kernel, out_shape=VMEM((tok, used * HEAD), jnp.bfloat16),...]
    pallas_call x1, Pallas kernels: 2.87 us -> 0.78 us  [mix_layers(): pl.pallas_call(kernel, grid_spec=pltpu.PrefetchScalarGridSpec(num_scalar_...]
    pallas_call x1, Pallas kernels: 3.3 us -> 1.23 us  [head_terms(): pl.pallas_call(kernel, grid_spec=pltpu.PrefetchScalarGridSpec(num_scalar_...]
    ppermute x12, starting transfers between devices: 16.8 us -> 18.8 us  [swap_cores(): return lax.ppermute(x, 'c', PAIR)]
    unnamed x38 -> x24, local copies, waits for them, and re-layouts: 3.22 us -> 5.18 us
  transfers between devices with their start and end apart: 27 -> 27, of which waited for: 10 -> 11; matrix products, arithmetic and copies ran while one was open for 9% -> 11% of each run, Pallas kernels for 10% -> 6%
where the time goes in v4:
time: 167 us
  blocking collectives  50.1 us (30%)
  starting transfers between devices  39.4 us (24%)
  waiting for transfers between devices  39 us (23%)
  matrix products  15.4 us (9%)
  Pallas kernels  13.5 us (8%)
  local copies, waits for them, and re-layouts  5.38 us (3%)
  other arithmetic  2.51 us (2%)
    all_to_all x1, blocking collectives, token_sum(): lax.all_to_all(mine.reshape(n, rows // n, HEAD), plane, 0, 0, tiled=True)  22 us
    ppermute x7, waiting for transfers between devices, swap_halves(): return lax.ppermute(x, 'xl', PAIR)  21.4 us
    ppermute x12, starting transfers between devices, swap_cores(): return lax.ppermute(x, 'c', PAIR)  18.8 us
    all_to_all x1, blocking collectives, token_sum(): return lax.all_to_all(spread, plane, 0, 0, tiled=True).reshape(rows, HEAD)  15.5 us
    ppermute x8, starting transfers between devices, hop(): return (lax.ppermute(b, Z, even), lax.ppermute(a, Z, odd))  14.5 us
    ppermute x8, waiting for transfers between devices, hop(): return (lax.ppermute(b, Z, even), lax.ppermute(a, Z, odd))  14.2 us
    all_to_all x1, blocking collectives, token_sum(): parts = lax.all_to_all(spread, 'zh', 0, 0, tiled=True)  12.6 us
    dot_general x18, matrix products, backward(): lax.dot_general(g, piece, (((1,), (1,)), ((), ())), preferred_element_typ...  8.29 us
  transfers between devices with their start and end apart: 27, of which 11 were waited for; matrix products, arithmetic and copies ran while one was open for 11% of the time, Pallas kernels for 6%

profile of v4, /device:TPU:1, one launch (start us, length us, event | category | flops | bytes accessed | tf_op | source)
XLA Modules:
  0.0 166.6 jit_solution(18003842424895807983)
XLA Ops:
  0.6 1.4 copy-done
  2.0 0.7 copy-done.7
  2.7 0.7 copy-done.8
  3.4 0.8 shard_map.121
  4.2 2.5 %collective-permute-start.2 = (bf16[1024,256]{1,0:T(8,128)(2,1)S(1)}, bf16[1024,256]{1,0:T(8,128)(2,1)}, u32[]{:S(2)}, u32[]{:S(2)}) collective-permute-start(bf16[1024,256]{1,0:T(8,128)(2,1)S(1)} %shard_map.121), channel_id=1, source_target_pairs={{0,4},{4,0},{8,12},{12,8},{16,20},{20,16},{24,28},{28,24},{1,5},{5... | collective-permute-start | bytes 1572872 | tf_op jit(solution)/shard_map/ppermute | solution.py:339
  6.7 1.0 collective-permute-start
  7.7 4.7 %collective-permute-start.4 = (bf16[1024,256]{1,0:T(8,128)(2,1)S(1)}, bf16[1024,256]{1,0:T(8,128)(2,1)}, u32[]{:S(2)}, u32[]{:S(2)}) collective-permute-start(bf16[1024,256]{1,0:T(8,128)(2,1)S(1)} %shard_map.121), channel_id=1, source_target_pairs={{0,28},{4,8},{8,4},{12,16},{16,12},{20,24},{24,20},{28,0},{1,29},{... | collective-permute-start | bytes 1572872 | tf_op jit(solution)/shard_map/ppermute | solution.py:339
  12.5 1.2 copy-done.3
  13.7 2.6 %shard_map.123 = bf16[128,4096]{1,0:T(8,128)(2,1)} custom-call(s32[20,2]{1,0:T(8,128)S(1)} %fusion.50.place_ref, bf16[128,2560]{1,0:T(8,128)(2,1)S(1)} %copy-done.3, bf16[20,2,128,128]{3,2,1,0:T(8,128)(2,1)S(1)} %copy-done.1), custom_call_target="tpu_custom_call" | custom-call | tf_op jit(solution)/shard_map/pallas_call | solution.py:90
  16.2 1.2 collective-permute-start.22
  17.6 1.1 copy-done.5
  18.7 1.3 shard_map.120
  21.0 1.3 convolution_convert_fusion.12
  22.7 2.1 %collective-permute-done.4 = bf16[1024,256]{1,0:T(8,128)(2,1)} collective-permute-done((bf16[1024,256]{1,0:T(8,128)(2,1)S(1)}, bf16[1024,256]{1,0:T(8,128)(2,1)}, u32[]{:S(2)}, u32[]{:S(2)}) %collective-permute-start.4) | collective-permute-done | bytes 524320 | tf_op jit(solution)/shard_map/ppermute | solution.py:339
  25.3 1.3 convolution_convert_fusion.11
  26.6 1.3 convolution_convert_fusion.9
  27.9 3.8 %collective-permute-start.9 = (bf16[1024,256]{1,0:T(8,128)(2,1)}, bf16[1024,256]{1,0:T(8,128)(2,1)S(1)}, u32[]{:S(2)}, u32[]{:S(2)}) collective-permute-start(bf16[1024,256]{1,0:T(8,128)(2,1)} %collective-permute-done.2), channel_id=1, source_target_pairs={{0,28},{4,8},{8,4},{12,16},{16,12},{20,24},{24,20},{28,0},{1,29},{... | collective-permute-start | bytes 1572872 | tf_op jit(solution)/shard_map/ppermute | solution.py:339
  32.5 8.4 %collective-permute-done.22 = bf16[128,4096]{1,0:T(8,128)(2,1)} collective-permute-done((bf16[128,4096]{1,0:T(8,128)(2,1)}, bf16[128,4096]{1,0:T(8,128)(2,1)}, u32[]{:S(2)}, u32[]{:S(2)}) %collective-permute-start.22) | collective-permute-done | bytes 1048608 | tf_op jit(solution)/shard_map/ppermute | solution.py:24
  40.9 1.8 %add_convert_fusion = bf16[128,4096]{1,0:T(8,128)(2,1)S(1)} fusion(bf16[128,4096]{1,0:T(8,128)(2,1)} %collective-permute-done.22, bf16[128,4096]{1,0:T(8,128)(2,1)} %shard_map.123), kind=kLoop, calls=%fused_computation | loop fusion | flops 2097152 | bytes 3145728 | tf_op jit(solution)/shard_map/convert_element_type | solution.py:28
  42.7 1.3 fusion.33
  44.1 1.3 fusion.35
  45.4 1.3 fusion.30
  46.9 2.0 %collective-permute-start.10 = (bf16[1024,256]{1,0:T(8,128)(2,1)S(1)}, bf16[1024,256]{1,0:T(8,128)(2,1)S(1)}, u32[]{:S(2)}, u32[]{:S(2)}) collective-permute-start(bf16[1024,256]{1,0:T(8,128)(2,1)S(1)} %collective-permute-done.9), channel_id=1, source_target_pairs={{0,2},{2,0},{1,3},{3,1},{4,6},{6,4},{5,7},{7,5},{8,10},{10,8},{9,1... | collective-permute-start | bytes 1572872 | tf_op jit(solution)/shard_map/ppermute | solution.py:20
  49.8 1.7 %collective-permute-start.14 = (bf16[1024,256]{1,0:T(8,128)(2,1)S(1)}, bf16[1024,256]{1,0:T(8,128)(2,1)S(1)}, u32[]{:S(2)}, u32[]{:S(2)}) collective-permute-start(bf16[1024,256]{1,0:T(8,128)(2,1)S(1)} %collective-permute-done.7), channel_id=1, source_target_pairs={{0,28},{4,8},{8,4},{12,16},{16,12},{20,24},{24,20},{28,0},{1,29},{... | collective-permute-start | bytes 1572872 | tf_op jit(solution)/shard_map/ppermute | solution.py:339
  52.7 5.8 %collective-permute-done.12 = bf16[1024,256]{1,0:T(8,128)(2,1)S(1)} collective-permute-done((bf16[1024,256]{1,0:T(8,128)(2,1)S(1)}, bf16[1024,256]{1,0:T(8,128)(2,1)S(1)}, u32[]{:S(2)}, u32[]{:S(2)}) %collective-permute-start.12) | collective-permute-done | bytes 524320 | tf_op jit(solution)/shard_map/ppermute | solution.py:339
  58.5 2.8 %collective-permute-start.8 = (bf16[1024,256]{1,0:T(8,128)(2,1)S(1)}, bf16[1024,256]{1,0:T(8,128)(2,1)S(1)}, u32[]{:S(2)}, u32[]{:S(2)}) collective-permute-start(bf16[1024,256]{1,0:T(8,128)(2,1)S(1)} %collective-permute-done.7), channel_id=1, source_target_pairs={{0,2},{2,0},{1,3},{3,1},{4,6},{6,4},{5,7},{7,5},{8,10},{10,8},{9,1... | collective-permute-start | bytes 1572872 | tf_op jit(solution)/shard_map/ppermute | solution.py:20
  61.2 3.4 %collective-permute-done.14 = bf16[1024,256]{1,0:T(8,128)(2,1)S(1)} collective-permute-done((bf16[1024,256]{1,0:T(8,128)(2,1)S(1)}, bf16[1024,256]{1,0:T(8,128)(2,1)S(1)}, u32[]{:S(2)}, u32[]{:S(2)}) %collective-permute-start.14) | collective-permute-done | bytes 524320 | tf_op jit(solution)/shard_map/ppermute | solution.py:339
  64.6 1.6 collective-permute-start.18
  68.7 1.2 collective-permute-start.13
  69.9 2.9 %collective-permute-done.18 = bf16[512,256]{1,0:T(8,128)(2,1)S(1)} collective-permute-done((bf16[512,256]{1,0:T(8,128)(2,1)S(1)}, bf16[512,256]{1,0:T(8,128)(2,1)S(1)}, u32[]{:S(2)}, u32[]{:S(2)}) %collective-permute-start.18) | collective-permute-done | bytes 262176 | tf_op jit(solution)/shard_map/ppermute | solution.py:339
  72.8 1.7 %collective-permute-start.15 = (bf16[1024,256]{1,0:T(8,128)(2,1)S(1)}, bf16[1024,256]{1,0:T(8,128)(2,1)S(1)}, u32[]{:S(2)}, u32[]{:S(2)}) collective-permute-start(bf16[1024,256]{1,0:T(8,128)(2,1)S(1)} %collective-permute-done.14), channel_id=1, source_target_pairs={{0,2},{2,0},{1,3},{3,1},{4,6},{6,4},{5,7},{7,5},{8,10},{10,8},{9,1... | collective-permute-start | bytes 1572872 | tf_op jit(solution)/shard_map/ppermute | solution.py:20
  74.8 0.8 collective-permute-start.20
  77.5 0.7 collective-permute-done.19
  78.3 1.2 collective-permute-start.11
  81.2 1.3 collective-permute-start.16
  82.7 8.7 %collective-permute-done.23.hg1 = bf16[128,1024]{1,0:T(8,128)(2,1)S(1)} collective-permute-done((bf16[128,1024]{1,0:T(8,128)(2,1)S(1)}, bf16[128,1024]{1,0:T(8,128)(2,1)S(1)}, u32[]{:S(2)}, u32[]{:S(2)}) %collective-permute-start.23) | collective-permute-done | bytes 262176 | tf_op jit(solution)/shard_map/ppermute | solution.py:24
  91.4 1.2 shard_map.125
  92.6 2.1 %collective-permute-start.24 = (bf16[1280,128]{1,0:T(8,128)(2,1)S(1)}, bf16[1280,128]{1,0:T(8,128)(2,1)S(1)}, u32[]{:S(2)}, u32[]{:S(2)}) collective-permute-start(bf16[1280,128]{1,0:T(8,128)(2,1)S(1)} %get-tuple-element.13), channel_id=1, source_target_pairs={{0,2},{2,0},{1,3},{3,1},{4,6},{6,4},{5,7},{7,5},{8,10},{10,8},{9,1... | collective-permute-start | bytes 983048 | tf_op jit(solution)/shard_map/ppermute | solution.py:20
  94.8 1.3 collective-permute-start.21
  96.1 4.3 %collective-permute-done.21.refs_9_ = bf16[128,512]{1,0:T(8,128)(2,1)S(1)} collective-permute-done((bf16[128,512]{1,0:T(8,128)(2,1)S(1)}, bf16[128,512]{1,0:T(8,128)(2,1)S(1)}, u32[]{:S(2)}, u32[]{:S(2)}) %collective-permute-start.21) | collective-permute-done | bytes 131104 | tf_op jit(solution)/shard_map/ppermute | solution.py:24
  100.4 2.9 %shard_map.122 = (bf16[128,2560]{1,0:T(8,128)(2,1)}, f32[2560,128]{1,0:T(8,128)S(1)}, bf16[2560,128]{1,0:T(8,128)(2,1)S(1)}) custom-call(s32[2]{0:T(128)S(1)} %pad_add_fusion.where_ref, s32[20,2]{1,0:T(8,128)S(1)} %fusion.50.place_ref, bf16[128,512]{1,0:T(8,128)(2,1)S(1)} %pad_maximum_fusion.4.refs_0_, bf16[128,512]{1,0:T(8,128)(2,1)S(1)} %collective-permute-done.1.refs_1_, ...), custom_call_target="tpu_custom_call" | custom-call | tf_op jit(solution)/shard_map/pallas_call | solution.py:149
  104.0 1.6 collective-permute-done.25
  105.9 22.0 %all_to_all.15 = bf16[16,240,128]{2,1,0:T(8,128)(2,1)S(1)} all-to-all(bf16[16,240,128]{2,1,0:T(8,128)(2,1)S(1)} %bitcast.58), channel_id=1, replica_groups=mesh['xh'=2,'y'=4,'zh'=4,'zl'=2,'c'=2,'xl'=2] {'xh','y','zl'}, dimensions={0} | all-to-all | bytes 1966080 | tf_op jit(solution)/shard_map/all_to_all | solution.py:300
  128.0 12.6 %all_to_all.16 = bf16[4,240,128]{2,1,0:T(8,128)(2,1)S(1)} all-to-all(bf16[4,240,128]{2,1,0:T(8,128)(2,1)S(1)} %broadcast_in_dim.10), channel_id=1, replica_groups=mesh['xh'=2,'y'=4,'zh'=4,'zl'=2,'c'=2,'xl'=2] {'zh'}, dimensions={0} | all-to-all | bytes 491520 | tf_op jit(solution)/shard_map/all_to_all | solution.py:303
  140.9 15.5 %all_to_all.17 = bf16[16,240,128]{2,1,0:T(8,128)(2,1)S(1)} all-to-all(bf16[16,240,128]{2,1,0:T(8,128)(2,1)S(1)} %broadcast_in_dim.11), channel_id=1, replica_groups=mesh['xh'=2,'y'=4,'zh'=4,'zl'=2,'c'=2,'xl'=2] {'xh','y','zl'}, dimensions={0} | all-to-all | bytes 1966080 | tf_op jit(solution)/shard_map/all_to_all | solution.py:306
  156.4 5.0 %collective-permute-start.26 = (bf16[3840,128]{1,0:T(8,128)(2,1)S(1)}, bf16[3840,128]{1,0:T(8,128)(2,1)S(1)}, u32[]{:S(2)}, u32[]{:S(2)}) collective-permute-start(bf16[3840,128]{1,0:T(8,128)(2,1)S(1)} %bitcast.56), channel_id=1, source_target_pairs={{0,2},{2,0},{1,3},{3,1},{4,6},{6,4},{5,7},{7,5},{8,10},{10,8},{9,1... | collective-permute-start | bytes 2949128 | tf_op jit(solution)/shard_map/ppermute | solution.py:20
  161.4 1.8 %shard_map.124 = bf16[128,1280]{1,0:T(8,128)(2,1)} custom-call(s32[2]{0:T(128)S(1)} %pad_add_fusion.where_ref, s32[10,2]{1,0:T(8,128)S(1)} %fusion.58.place_ref, bf16[128,1024]{1,0:T(8,128)(2,1)S(1)} %fusion.8.hg0, bf16[128,1024]{1,0:T(8,128)(2,1)S(1)} %collective-permute-done.23.hg1, bf16[20,2,128,128]{3,2,1,0:T(8,128)(2,1)S(1)} %copy-done.2), custom_call_target="tpu_custom_call" | custom-call | tf_op jit(solution)/shard_map/pallas_call | solution.py:216
  163.6 3.0 %shard_map.126 = (f32[2,1280,128]{2,1,0:T(8,128)}, f32[2,2560,128]{2,1,0:T(8,128)}) custom-call(s32[2]{0:T(128)S(1)} %pad_add_fusion.where_ref, bf16[3840,128]{1,0:T(8,128)(2,1)S(1)} %bitcast.57, bf16[3840,128]{1,0:T(8,128)(2,1)S(1)} %collective-permute-done.26.theirs_ref), custom_call_target="tpu_custom_call" | custom-call | tf_op jit(solution)/shard_map/pallas_call | solution.py:278
  (96 shorter events, 13.2 us)
Async XLA Ops:
  0.6 1.4 copy-start
  2.0 0.7 copy-start.7
  2.7 0.7 copy-start.8
  3.4 9.0 %copy-start.9 = (s32[20,2]{0,1:T(2,128)S(1)}, s32[20,2]{0,1:T(2,128)}, u32[]{:S(2)}) copy-start(s32[20,2]{0,1:T(2,128)} %param.17) | copy-start | bytes 484
  3.4 9.1 %copy-start.1 = (bf16[20,2,128,128]{3,2,1,0:T(8,128)(2,1)S(1)}, bf16[20,2,128,128]{3,2,1,0:T(8,128)(2,1)}, u32[]{:S(2)}) copy-start(bf16[20,2,128,128]{3,2,1,0:T(8,128)(2,1)} %w_ref.4) | copy-start | bytes 3932164
  4.2 13.3 %copy-start.10 = (s32[20,2]{0,1:T(2,128)S(1)}, s32[20,2]{0,1:T(2,128)}, u32[]{:S(2)}) copy-start(s32[20,2]{0,1:T(2,128)} %param.15) | copy-start | bytes 484
  4.2 16.2 %collective-permute-start.2 = (bf16[1024,256]{1,0:T(8,128)(2,1)S(1)}, bf16[1024,256]{1,0:T(8,128)(2,1)}, u32[]{:S(2)}, u32[]{:S(2)}) collective-permute-start(bf16[1024,256]{1,0:T(8,128)(2,1)S(1)} %shard_map.121), channel_id=1, source_target_pairs={{0,4},{4,0},{8,12},{12,8},{16,20},{20,16},{24,28},{28,24},{1,5},{5... | collective-permute-start | bytes 1572872 | tf_op jit(solution)/shard_map/ppermute | solution.py:339
  6.7 14.3 %collective-permute-start = (bf16[1024,256]{1,0:T(8,128)(2,1)S(1)}, bf16[1024,256]{1,0:T(8,128)(2,1)}, u32[]{:S(2)}, u32[]{:S(2)}) collective-permute-start(bf16[1024,256]{1,0:T(8,128)(2,1)S(1)} %shard_map.121), channel_id=1, source_target_pairs={{0,2},{2,0},{1,3},{3,1},{4,6},{6,4},{5,7},{7,5},{8,10},{10,8},{9,1... | collective-permute-start | bytes 1572872 | tf_op jit(solution)/shard_map/ppermute | solution.py:20
  7.7 17.1 %collective-permute-start.4 = (bf16[1024,256]{1,0:T(8,128)(2,1)S(1)}, bf16[1024,256]{1,0:T(8,128)(2,1)}, u32[]{:S(2)}, u32[]{:S(2)}) collective-permute-start(bf16[1024,256]{1,0:T(8,128)(2,1)S(1)} %shard_map.121), channel_id=1, source_target_pairs={{0,28},{4,8},{8,4},{12,16},{16,12},{20,24},{24,20},{28,0},{1,29},{... | collective-permute-start | bytes 1572872 | tf_op jit(solution)/shard_map/ppermute | solution.py:339
  12.3 5.2 %copy-start.2 = (bf16[20,2,128,128]{3,2,1,0:T(8,128)(2,1)S(1)}, bf16[20,2,128,128]{3,2,1,0:T(8,128)(2,1)}, u32[]{:S(2)}) copy-start(bf16[20,2,128,128]{3,2,1,0:T(8,128)(2,1)} %w_ref.5) | copy-start | bytes 3932164
  12.5 1.2 copy-start.3
  16.2 24.7 %collective-permute-start.22 = (bf16[128,4096]{1,0:T(8,128)(2,1)}, bf16[128,4096]{1,0:T(8,128)(2,1)}, u32[]{:S(2)}, u32[]{:S(2)}) collective-permute-start(bf16[128,4096]{1,0:T(8,128)(2,1)} %shard_map.123), channel_id=1, source_target_pairs={{0,1},{1,0},{2,3},{3,2},{4,5},{5,4},{6,7},{7,6},{8,9},{9,8},{10,11... | collective-permute-start | bytes 3145736 | tf_op jit(solution)/shard_map/ppermute | solution.py:24
  17.6 1.1 copy-start.5
  20.4 7.5 %collective-permute-start.3 = (bf16[1024,256]{1,0:T(8,128)(2,1)}, bf16[1024,256]{1,0:T(8,128)(2,1)S(1)}, u32[]{:S(2)}, u32[]{:S(2)}) collective-permute-start(bf16[1024,256]{1,0:T(8,128)(2,1)} %collective-permute-done.2), channel_id=1, source_target_pairs={{0,2},{2,0},{1,3},{3,1},{4,6},{6,4},{5,7},{7,5},{8,10},{10,8},{9,1... | collective-permute-start | bytes 1572872 | tf_op jit(solution)/shard_map/ppermute | solution.py:20
  22.3 72.5 %collective-permute-start.1 = (bf16[128,512]{1,0:T(8,128)(2,1)S(1)}, bf16[128,512]{1,0:T(8,128)(2,1)S(1)}, u32[]{:S(2)}, u32[]{:S(2)}) collective-permute-start(bf16[128,512]{1,0:T(8,128)(2,1)S(1)} %pad_maximum_fusion.4.refs_0_), channel_id=1, source_target_pairs={{0,1},{1,0},{2,3},{3,2},{4,5},{5,4},{6,7},{7,6},{8,9},{9,8},{10,11... | collective-permute-start | bytes 393224 | tf_op jit(solution)/shard_map/ppermute | solution.py:24
  24.7 24.8 %collective-permute-start.7 = (bf16[1024,256]{1,0:T(8,128)(2,1)}, bf16[1024,256]{1,0:T(8,128)(2,1)S(1)}, u32[]{:S(2)}, u32[]{:S(2)}) collective-permute-start(bf16[1024,256]{1,0:T(8,128)(2,1)} %collective-permute-done.4), channel_id=1, source_target_pairs={{0,4},{4,0},{8,12},{12,8},{16,20},{20,16},{24,28},{28,24},{1,5},{5... | collective-permute-start | bytes 1572872 | tf_op jit(solution)/shard_map/ppermute | solution.py:339
  24.7 7.2 %collective-permute-start.5 = (bf16[1024,256]{1,0:T(8,128)(2,1)}, bf16[1024,256]{1,0:T(8,128)(2,1)S(1)}, u32[]{:S(2)}, u32[]{:S(2)}) collective-permute-start(bf16[1024,256]{1,0:T(8,128)(2,1)} %collective-permute-done.4), channel_id=1, source_target_pairs={{0,2},{2,0},{1,3},{3,1},{4,6},{6,4},{5,7},{7,5},{8,10},{10,8},{9,1... | collective-permute-start | bytes 1572872 | tf_op jit(solution)/shard_map/ppermute | solution.py:20
  27.9 18.9 %collective-permute-start.9 = (bf16[1024,256]{1,0:T(8,128)(2,1)}, bf16[1024,256]{1,0:T(8,128)(2,1)S(1)}, u32[]{:S(2)}, u32[]{:S(2)}) collective-permute-start(bf16[1024,256]{1,0:T(8,128)(2,1)} %collective-permute-done.2), channel_id=1, source_target_pairs={{0,28},{4,8},{8,4},{12,16},{16,12},{20,24},{24,20},{28,0},{1,29},{... | collective-permute-start | bytes 1572872 | tf_op jit(solution)/shard_map/ppermute | solution.py:339
  32.2 63.9 %collective-permute-start.6 = (bf16[128,1024]{1,0:T(8,128)(2,1)S(1)}, bf16[128,1024]{1,0:T(8,128)(2,1)S(1)}, u32[]{:S(2)}, u32[]{:S(2)}) collective-permute-start(bf16[128,1024]{1,0:T(8,128)(2,1)S(1)} %pad_maximum_fusion.1.refs_2_), channel_id=1, source_target_pairs={{0,1},{1,0},{2,3},{3,2},{4,5},{5,4},{6,7},{7,6},{8,9},{9,8},{10,11... | collective-permute-start | bytes 786440 | tf_op jit(solution)/shard_map/ppermute | solution.py:24
  46.8 11.7 %collective-permute-start.12 = (bf16[1024,256]{1,0:T(8,128)(2,1)S(1)}, bf16[1024,256]{1,0:T(8,128)(2,1)S(1)}, u32[]{:S(2)}, u32[]{:S(2)}) collective-permute-start(bf16[1024,256]{1,0:T(8,128)(2,1)S(1)} %collective-permute-done.9), channel_id=1, source_target_pairs={{0,4},{4,0},{8,12},{12,8},{16,20},{20,16},{24,28},{28,24},{1,5},{5... | collective-permute-start | bytes 1572872 | tf_op jit(solution)/shard_map/ppermute | solution.py:339
  46.9 19.9 %collective-permute-start.10 = (bf16[1024,256]{1,0:T(8,128)(2,1)S(1)}, bf16[1024,256]{1,0:T(8,128)(2,1)S(1)}, u32[]{:S(2)}, u32[]{:S(2)}) collective-permute-start(bf16[1024,256]{1,0:T(8,128)(2,1)S(1)} %collective-permute-done.9), channel_id=1, source_target_pairs={{0,2},{2,0},{1,3},{3,1},{4,6},{6,4},{5,7},{7,5},{8,10},{10,8},{9,1... | collective-permute-start | bytes 1572872 | tf_op jit(solution)/shard_map/ppermute | solution.py:20
  49.8 14.8 %collective-permute-start.14 = (bf16[1024,256]{1,0:T(8,128)(2,1)S(1)}, bf16[1024,256]{1,0:T(8,128)(2,1)S(1)}, u32[]{:S(2)}, u32[]{:S(2)}) collective-permute-start(bf16[1024,256]{1,0:T(8,128)(2,1)S(1)} %collective-permute-done.7), channel_id=1, source_target_pairs={{0,28},{4,8},{8,4},{12,16},{16,12},{20,24},{24,20},{28,0},{1,29},{... | collective-permute-start | bytes 1572872 | tf_op jit(solution)/shard_map/ppermute | solution.py:339
  58.5 9.3 %collective-permute-start.8 = (bf16[1024,256]{1,0:T(8,128)(2,1)S(1)}, bf16[1024,256]{1,0:T(8,128)(2,1)S(1)}, u32[]{:S(2)}, u32[]{:S(2)}) collective-permute-start(bf16[1024,256]{1,0:T(8,128)(2,1)S(1)} %collective-permute-done.7), channel_id=1, source_target_pairs={{0,2},{2,0},{1,3},{3,1},{4,6},{6,4},{5,7},{7,5},{8,10},{10,8},{9,1... | collective-permute-start | bytes 1572872 | tf_op jit(solution)/shard_map/ppermute | solution.py:20
  64.6 8.2 %collective-permute-start.18 = (bf16[512,256]{1,0:T(8,128)(2,1)S(1)}, bf16[512,256]{1,0:T(8,128)(2,1)S(1)}, u32[]{:S(2)}, u32[]{:S(2)}) collective-permute-start(bf16[512,256]{1,0:T(8,128)(2,1)S(1)} %slice.85), channel_id=1, source_target_pairs={{0,28},{4,8},{8,4},{12,16},{16,12},{20,24},{24,20},{28,0},{1,29},{... | collective-permute-start | bytes 786440 | tf_op jit(solution)/shard_map/ppermute | solution.py:339
  66.8 8.0 %collective-permute-start.17 = (bf16[512,256]{1,0:T(8,128)(2,1)S(1)}, bf16[512,256]{1,0:T(8,128)(2,1)S(1)}, u32[]{:S(2)}, u32[]{:S(2)}) collective-permute-start(bf16[512,256]{1,0:T(8,128)(2,1)S(1)} %slice.83), channel_id=1, source_target_pairs={{0,4},{4,0},{8,12},{12,8},{16,20},{20,16},{24,28},{28,24},{1,5},{5... | collective-permute-start | bytes 786440 | tf_op jit(solution)/shard_map/ppermute | solution.py:339
  68.7 11.1 %collective-permute-start.13 = (bf16[1024,256]{1,0:T(8,128)(2,1)S(1)}, bf16[1024,256]{1,0:T(8,128)(2,1)S(1)}, u32[]{:S(2)}, u32[]{:S(2)}) collective-permute-start(bf16[1024,256]{1,0:T(8,128)(2,1)S(1)} %collective-permute-done.12), channel_id=1, source_target_pairs={{0,2},{2,0},{1,3},{3,1},{4,6},{6,4},{5,7},{7,5},{8,10},{10,8},{9,1... | collective-permute-start | bytes 1572872 | tf_op jit(solution)/shard_map/ppermute | solution.py:20
  72.8 7.2 %collective-permute-start.15 = (bf16[1024,256]{1,0:T(8,128)(2,1)S(1)}, bf16[1024,256]{1,0:T(8,128)(2,1)S(1)}, u32[]{:S(2)}, u32[]{:S(2)}) collective-permute-start(bf16[1024,256]{1,0:T(8,128)(2,1)S(1)} %collective-permute-done.14), channel_id=1, source_target_pairs={{0,2},{2,0},{1,3},{3,1},{4,6},{6,4},{5,7},{7,5},{8,10},{10,8},{9,1... | collective-permute-start | bytes 1572872 | tf_op jit(solution)/shard_map/ppermute | solution.py:20
  74.8 2.0 %collective-permute-start.20 = (bf16[512,256]{1,0:T(8,128)(2,1)S(1)}, bf16[512,256]{1,0:T(8,128)(2,1)S(1)}, u32[]{:S(2)}, u32[]{:S(2)}) collective-permute-start(bf16[512,256]{1,0:T(8,128)(2,1)S(1)} %collective-permute-done.18), channel_id=1, source_target_pairs={{0,2},{2,0},{1,3},{3,1},{4,6},{6,4},{5,7},{7,5},{8,10},{10,8},{9,1... | collective-permute-start | bytes 786440 | tf_op jit(solution)/shard_map/ppermute | solution.py:20
  76.7 1.5 collective-permute-start.19
  78.3 17.8 %collective-permute-start.11 = (bf16[128,1024]{1,0:T(8,128)(2,1)S(1)}, bf16[128,1024]{1,0:T(8,128)(2,1)S(1)}, u32[]{:S(2)}, u32[]{:S(2)}) collective-permute-start(bf16[128,1024]{1,0:T(8,128)(2,1)S(1)} %pad_maximum_fusion.2.refs_4_), channel_id=1, source_target_pairs={{0,1},{1,0},{2,3},{3,2},{4,5},{5,4},{6,7},{7,6},{8,9},{9,8},{10,11... | collective-permute-start | bytes 786440 | tf_op jit(solution)/shard_map/ppermute | solution.py:24
  80.4 11.0 %copy-start.6 = (bf16[128,2560]{1,0:T(8,128)(2,1)S(1)}, bf16[128,2560]{1,0:T(8,128)(2,1)}, u32[]{:S(2)}) copy-start(bf16[128,2560]{1,0:T(8,128)(2,1)} %attn_ref.1) | copy-start | bytes 1966084
  80.4 11.0 %collective-permute-start.23 = (bf16[128,1024]{1,0:T(8,128)(2,1)S(1)}, bf16[128,1024]{1,0:T(8,128)(2,1)S(1)}, u32[]{:S(2)}, u32[]{:S(2)}) collective-permute-start(bf16[128,1024]{1,0:T(8,128)(2,1)S(1)} %fusion.8.hg0), channel_id=1, source_target_pairs={{0,1},{1,0},{2,3},{3,2},{4,5},{5,4},{6,7},{7,6},{8,9},{9,8},{10,11... | collective-permute-start | bytes 786440 | tf_op jit(solution)/shard_map/ppermute | solution.py:24
  81.0 19.4 %copy-start.4 = (bf16[128,2560]{1,0:T(8,128)(2,1)S(1)}, bf16[128,2560]{1,0:T(8,128)(2,1)}, u32[]{:S(2)}) copy-start(bf16[128,2560]{1,0:T(8,128)(2,1)} %x_ref.3) | copy-start | bytes 1966084
  81.2 19.2 %collective-permute-start.16 = (bf16[128,1024]{1,0:T(8,128)(2,1)S(1)}, bf16[128,1024]{1,0:T(8,128)(2,1)S(1)}, u32[]{:S(2)}, u32[]{:S(2)}) collective-permute-start(bf16[128,1024]{1,0:T(8,128)(2,1)S(1)} %pad_maximum_fusion.3.refs_6_), channel_id=1, source_target_pairs={{0,1},{1,0},{2,3},{3,2},{4,5},{5,4},{6,7},{7,6},{8,9},{9,8},{10,11... | collective-permute-start | bytes 786440 | tf_op jit(solution)/shard_map/ppermute | solution.py:24
  92.6 11.3 %collective-permute-start.24 = (bf16[1280,128]{1,0:T(8,128)(2,1)S(1)}, bf16[1280,128]{1,0:T(8,128)(2,1)S(1)}, u32[]{:S(2)}, u32[]{:S(2)}) collective-permute-start(bf16[1280,128]{1,0:T(8,128)(2,1)S(1)} %get-tuple-element.13), channel_id=1, source_target_pairs={{0,2},{2,0},{1,3},{3,1},{4,6},{6,4},{5,7},{7,5},{8,10},{10,8},{9,1... | collective-permute-start | bytes 983048 | tf_op jit(solution)/shard_map/ppermute | solution.py:20
  94.8 5.6 %collective-permute-start.21 = (bf16[128,512]{1,0:T(8,128)(2,1)S(1)}, bf16[128,512]{1,0:T(8,128)(2,1)S(1)}, u32[]{:S(2)}, u32[]{:S(2)}) collective-permute-start(bf16[128,512]{1,0:T(8,128)(2,1)S(1)} %pad_maximum_fusion.5.refs_8_), channel_id=1, source_target_pairs={{0,1},{1,0},{2,3},{3,2},{4,5},{5,4},{6,7},{7,6},{8,9},{9,8},{10,11... | collective-permute-start | bytes 393224 | tf_op jit(solution)/shard_map/ppermute | solution.py:24
  103.3 2.4 %collective-permute-start.25 = (bf16[2560,128]{1,0:T(8,128)(2,1)S(1)}, bf16[2560,128]{1,0:T(8,128)(2,1)S(1)}, u32[]{:S(2)}, u32[]{:S(2)}) collective-permute-start(bf16[2560,128]{1,0:T(8,128)(2,1)S(1)} %get-tuple-element.15), channel_id=1, source_target_pairs={{0,2},{2,0},{1,3},{3,1},{4,6},{6,4},{5,7},{7,5},{8,10},{10,8},{9,1... | collective-permute-start | bytes 1966088 | tf_op jit(solution)/shard_map/ppermute | solution.py:20
  156.4 7.2 %collective-permute-start.26 = (bf16[3840,128]{1,0:T(8,128)(2,1)S(1)}, bf16[3840,128]{1,0:T(8,128)(2,1)S(1)}, u32[]{:S(2)}, u32[]{:S(2)}) collective-permute-start(bf16[3840,128]{1,0:T(8,128)(2,1)S(1)} %bitcast.56), channel_id=1, source_target_pairs={{0,2},{2,0},{1,3},{3,1},{4,6},{6,4},{5,7},{7,5},{8,10},{10,8},{9,1... | collective-permute-start | bytes 2949128 | tf_op jit(solution)/shard_map/ppermute | solution.py:20

commit v5 on v4

--- a/solution.py
+++ b/solution.py
@@ -256,39 +256,37 @@
     )(pick, coef, weights, weights)
 
 
-def unpack_sums(where, mine, theirs, cut):
+def unpack_half(where, turn, half, cut, so_far=()):
     steps = 2
-    most = mine.shape[0] - cut
+    most = half.shape[0] - cut
     small, large = cut // steps, most // steps
 
-    def kernel(where_ref, mine_ref, theirs_ref, in_ref, out_ref):
-        i = pl.program_id(1)
-        for turn, src in enumerate((mine_ref, theirs_ref)):
-
-            @pl.when(pl.program_id(0) == turn)
-            def _():
-                at = pl.multiple_of(i * small, small)
-                in_ref[0] = src[pl.ds(at, small), :].astype(jnp.float32)
-                at = pl.multiple_of(cut + i * large, small)
-                out_ref[0] = src[pl.ds(at, large), :].astype(jnp.float32)
+    def kernel(where_ref, half_ref, *refs):
+        in_ref, out_ref = refs[-2:]
+        i = pl.program_id(0)
+        at = pl.multiple_of(i * small, small)
+        in_ref[0] = half_ref[pl.ds(at, small), :].astype(jnp.float32)
+        at = pl.multiple_of(cut + i * large, small)
+        out_ref[0] = half_ref[pl.ds(at, large), :].astype(jnp.float32)
 
     def result(rows):
-        return pl.BlockSpec((1, rows, HEAD), lambda t, i, w: ((w[0] + t) % 2, i, 0))
+        return pl.BlockSpec((1, rows, HEAD), lambda i, w: ((w[0] + turn) % 2, i, 0))
 
     return pl.pallas_call(
         kernel,
         grid_spec=pltpu.PrefetchScalarGridSpec(
             num_scalar_prefetch=1,
-            grid=(2, steps),
-            in_specs=[HERE, HERE],
+            grid=(steps,),
+            in_specs=[HERE, *[pl.BlockSpec(memory_space=pl.ANY) for _ in so_far]],
             out_specs=[result(small), result(large)],
         ),
         out_shape=[
             jax.ShapeDtypeStruct((2, cut, HEAD), jnp.float32),
             jax.ShapeDtypeStruct((2, most, HEAD), jnp.float32),
         ],
+        input_output_aliases={2 + i: i for i in range(len(so_far))},
         compiler_params=grant(14),
-    )(where, near(mine), near(theirs))
+    )(where, near(half), *so_far)
 
 
 def token_sum(keep, came, scale):
@@ -390,7 +388,8 @@
     grad_scale = float(tok_rows * lax.axis_size(TOKENS)) ** (-0.5)
     full = token_sum((keep_in, keep_out), (came_in, came_out), grad_scale)
     theirs = swap_cores(full)
-    in_sum, out_sum = unpack_sums(where, full, theirs, rows_in * HEAD)
+    sums = unpack_half(where, 0, full, rows_in * HEAD)
+    in_sum, out_sum = unpack_half(where, 1, theirs, rows_in * HEAD, sums)
     in_sum = in_sum.reshape(rows_in, 2, HEAD, HEAD)
     out_sum = out_sum.reshape(out_cols.shape[0], 2, HEAD, HEAD)
     return (grown_out, grad_attn, in_sum, out_sum)

time: 167 us -> 168 us (level)
    pallas_call x1 -> x2, Pallas kernels: 2.96 us -> 3.76 us  [unpack_half(): pl.pallas_call(kernel, grid_spec=pltpu.PrefetchScalarGridSpec(num_scalar_...]
  transfers between devices with their start and end apart: 27 -> 27, of which waited for: 11 -> 10; matrix products, arithmetic and copies ran while one was open for 11% -> 11% of each run, Pallas kernels for 6% -> 7%
where the time goes in v5:
time: 168 us; the launch traced here: 167 us
  blocking collectives  50.1 us (30%)
  starting transfers between devices  39.4 us (23%)
  waiting for transfers between devices  38.6 us (23%)
  matrix products  15.4 us (9%)
  Pallas kernels  14.3 us (9%)
  local copies, waits for them, and re-layouts  5.38 us (3%)
  other arithmetic  2.51 us (1%)
    all_to_all x1, blocking collectives, token_sum(): lax.all_to_all(mine.reshape(n, rows // n, HEAD), plane, 0, 0, tiled=True)  22 us
    ppermute x7, waiting for transfers between devices, swap_halves(): return lax.ppermute(x, 'xl', PAIR)  21.4 us
    ppermute x12, starting transfers between devices, swap_cores(): return lax.ppermute(x, 'c', PAIR)  18.8 us
    all_to_all x1, blocking collectives, token_sum(): return lax.all_to_all(spread, plane, 0, 0, tiled=True).reshape(rows, HEAD)  15.5 us
    ppermute x8, starting transfers between devices, hop(): return (lax.ppermute(b, Z, even), lax.ppermute(a, Z, odd))  14.5 us
    ppermute x8, waiting for transfers between devices, hop(): return (lax.ppermute(b, Z, even), lax.ppermute(a, Z, odd))  14.2 us
    all_to_all x1, blocking collectives, token_sum(): parts = lax.all_to_all(spread, 'zh', 0, 0, tiled=True)  12.6 us
    dot_general x18, matrix products, backward(): lax.dot_general(g, piece, (((1,), (1,)), ((), ())), preferred_element_typ...  8.29 us
  transfers between devices with their start and end apart: 27, of which 10 were waited for; matrix products, arithmetic and copies ran while one was open for 11% of the time, Pallas kernels for 7%

profile of v5, /device:TPU:1, one launch (start us, length us, event | category | flops | bytes accessed | tf_op | source)
XLA Modules:
  0.0 167.0 jit_solution(6736332135802090108)
XLA Ops:
  0.6 1.4 copy-done
  2.7 0.7 copy-done.8
  3.4 0.8 shard_map.121
  4.2 2.5 %collective-permute-start.2 = (bf16[1024,256]{1,0:T(8,128)(2,1)S(1)}, bf16[1024,256]{1,0:T(8,128)(2,1)}, u32[]{:S(2)}, u32[]{:S(2)}) collective-permute-start(bf16[1024,256]{1,0:T(8,128)(2,1)S(1)} %shard_map.121), channel_id=1, source_target_pairs={{0,4},{4,0},{8,12},{12,8},{16,20},{20,16},{24,28},{28,24},{1,5},{5... | collective-permute-start | bytes 1572872 | tf_op jit(solution)/shard_map/ppermute | solution.py:337
  6.7 1.0 collective-permute-start
  7.7 4.7 %collective-permute-start.4 = (bf16[1024,256]{1,0:T(8,128)(2,1)S(1)}, bf16[1024,256]{1,0:T(8,128)(2,1)}, u32[]{:S(2)}, u32[]{:S(2)}) collective-permute-start(bf16[1024,256]{1,0:T(8,128)(2,1)S(1)} %shard_map.121), channel_id=1, source_target_pairs={{0,28},{4,8},{8,4},{12,16},{16,12},{20,24},{24,20},{28,0},{1,29},{... | collective-permute-start | bytes 1572872 | tf_op jit(solution)/shard_map/ppermute | solution.py:337
  12.5 1.2 copy-done.3
  13.7 2.6 %shard_map.123 = bf16[128,4096]{1,0:T(8,128)(2,1)} custom-call(s32[20,2]{1,0:T(8,128)S(1)} %fusion.50.place_ref, bf16[128,2560]{1,0:T(8,128)(2,1)S(1)} %copy-done.3, bf16[20,2,128,128]{3,2,1,0:T(8,128)(2,1)S(1)} %copy-done.1), custom_call_target="tpu_custom_call" | custom-call | tf_op jit(solution)/shard_map/pallas_call | solution.py:90
  16.2 1.2 collective-permute-start.22
  17.6 1.1 copy-done.5
  18.7 1.3 shard_map.120
  21.0 1.3 convolution_convert_fusion.12
  22.7 2.1 %collective-permute-done.4 = bf16[1024,256]{1,0:T(8,128)(2,1)} collective-permute-done((bf16[1024,256]{1,0:T(8,128)(2,1)S(1)}, bf16[1024,256]{1,0:T(8,128)(2,1)}, u32[]{:S(2)}, u32[]{:S(2)}) %collective-permute-start.4) | collective-permute-done | bytes 524320 | tf_op jit(solution)/shard_map/ppermute | solution.py:337
  25.3 1.3 convolution_convert_fusion.11
  26.6 1.3 convolution_convert_fusion.9
  27.9 3.8 %collective-permute-start.9 = (bf16[1024,256]{1,0:T(8,128)(2,1)}, bf16[1024,256]{1,0:T(8,128)(2,1)S(1)}, u32[]{:S(2)}, u32[]{:S(2)}) collective-permute-start(bf16[1024,256]{1,0:T(8,128)(2,1)} %collective-permute-done.2), channel_id=1, source_target_pairs={{0,28},{4,8},{8,4},{12,16},{16,12},{20,24},{24,20},{28,0},{1,29},{... | collective-permute-start | bytes 1572872 | tf_op jit(solution)/shard_map/ppermute | solution.py:337
  32.5 8.4 %collective-permute-done.22 = bf16[128,4096]{1,0:T(8,128)(2,1)} collective-permute-done((bf16[128,4096]{1,0:T(8,128)(2,1)}, bf16[128,4096]{1,0:T(8,128)(2,1)}, u32[]{:S(2)}, u32[]{:S(2)}) %collective-permute-start.22) | collective-permute-done | bytes 1048608 | tf_op jit(solution)/shard_map/ppermute | solution.py:24
  40.9 1.8 %add_convert_fusion = bf16[128,4096]{1,0:T(8,128)(2,1)S(1)} fusion(bf16[128,4096]{1,0:T(8,128)(2,1)} %collective-permute-done.22, bf16[128,4096]{1,0:T(8,128)(2,1)} %shard_map.123), kind=kLoop, calls=%fused_computation | loop fusion | flops 2097152 | bytes 3145728 | tf_op jit(solution)/shard_map/convert_element_type | solution.py:28
  42.7 1.3 fusion.33
  44.1 1.3 fusion.35
  45.4 1.3 fusion.30
  46.9 2.0 %collective-permute-start.10 = (bf16[1024,256]{1,0:T(8,128)(2,1)S(1)}, bf16[1024,256]{1,0:T(8,128)(2,1)S(1)}, u32[]{:S(2)}, u32[]{:S(2)}) collective-permute-start(bf16[1024,256]{1,0:T(8,128)(2,1)S(1)} %collective-permute-done.9), channel_id=1, source_target_pairs={{0,2},{2,0},{1,3},{3,1},{4,6},{6,4},{5,7},{7,5},{8,10},{10,8},{9,1... | collective-permute-start | bytes 1572872 | tf_op jit(solution)/shard_map/ppermute | solution.py:20
  49.8 1.7 %collective-permute-start.14 = (bf16[1024,256]{1,0:T(8,128)(2,1)S(1)}, bf16[1024,256]{1,0:T(8,128)(2,1)S(1)}, u32[]{:S(2)}, u32[]{:S(2)}) collective-permute-start(bf16[1024,256]{1,0:T(8,128)(2,1)S(1)} %collective-permute-done.7), channel_id=1, source_target_pairs={{0,28},{4,8},{8,4},{12,16},{16,12},{20,24},{24,20},{28,0},{1,29},{... | collective-permute-start | bytes 1572872 | tf_op jit(solution)/shard_map/ppermute | solution.py:337
  52.7 5.8 %collective-permute-done.12 = bf16[1024,256]{1,0:T(8,128)(2,1)S(1)} collective-permute-done((bf16[1024,256]{1,0:T(8,128)(2,1)S(1)}, bf16[1024,256]{1,0:T(8,128)(2,1)S(1)}, u32[]{:S(2)}, u32[]{:S(2)}) %collective-permute-start.12) | collective-permute-done | bytes 524320 | tf_op jit(solution)/shard_map/ppermute | solution.py:337
  58.5 2.8 %collective-permute-start.8 = (bf16[1024,256]{1,0:T(8,128)(2,1)S(1)}, bf16[1024,256]{1,0:T(8,128)(2,1)S(1)}, u32[]{:S(2)}, u32[]{:S(2)}) collective-permute-start(bf16[1024,256]{1,0:T(8,128)(2,1)S(1)} %collective-permute-done.7), channel_id=1, source_target_pairs={{0,2},{2,0},{1,3},{3,1},{4,6},{6,4},{5,7},{7,5},{8,10},{10,8},{9,1... | collective-permute-start | bytes 1572872 | tf_op jit(solution)/shard_map/ppermute | solution.py:20
  61.2 3.4 %collective-permute-done.14 = bf16[1024,256]{1,0:T(8,128)(2,1)S(1)} collective-permute-done((bf16[1024,256]{1,0:T(8,128)(2,1)S(1)}, bf16[1024,256]{1,0:T(8,128)(2,1)S(1)}, u32[]{:S(2)}, u32[]{:S(2)}) %collective-permute-start.14) | collective-permute-done | bytes 524320 | tf_op jit(solution)/shard_map/ppermute | solution.py:337
  64.6 1.6 collective-permute-start.18
  68.7 1.2 collective-permute-start.13
  69.9 2.9 %collective-permute-done.18 = bf16[512,256]{1,0:T(8,128)(2,1)S(1)} collective-permute-done((bf16[512,256]{1,0:T(8,128)(2,1)S(1)}, bf16[512,256]{1,0:T(8,128)(2,1)S(1)}, u32[]{:S(2)}, u32[]{:S(2)}) %collective-permute-start.18) | collective-permute-done | bytes 262176 | tf_op jit(solution)/shard_map/ppermute | solution.py:337
  72.8 1.7 %collective-permute-start.15 = (bf16[1024,256]{1,0:T(8,128)(2,1)S(1)}, bf16[1024,256]{1,0:T(8,128)(2,1)S(1)}, u32[]{:S(2)}, u32[]{:S(2)}) collective-permute-start(bf16[1024,256]{1,0:T(8,128)(2,1)S(1)} %collective-permute-done.14), channel_id=1, source_target_pairs={{0,2},{2,0},{1,3},{3,1},{4,6},{6,4},{5,7},{7,5},{8,10},{10,8},{9,1... | collective-permute-start | bytes 1572872 | tf_op jit(solution)/shard_map/ppermute | solution.py:20
  74.8 0.8 collective-permute-start.20
  77.5 0.7 collective-permute-done.19
  78.3 1.2 collective-permute-start.11
  81.2 1.3 collective-permute-start.16
  82.7 8.7 %collective-permute-done.23.hg1 = bf16[128,1024]{1,0:T(8,128)(2,1)S(1)} collective-permute-done((bf16[128,1024]{1,0:T(8,128)(2,1)S(1)}, bf16[128,1024]{1,0:T(8,128)(2,1)S(1)}, u32[]{:S(2)}, u32[]{:S(2)}) %collective-permute-start.23) | collective-permute-done | bytes 262176 | tf_op jit(solution)/shard_map/ppermute | solution.py:24
  91.4 1.2 shard_map.125
  92.6 2.1 %collective-permute-start.24 = (bf16[1280,128]{1,0:T(8,128)(2,1)S(1)}, bf16[1280,128]{1,0:T(8,128)(2,1)S(1)}, u32[]{:S(2)}, u32[]{:S(2)}) collective-permute-start(bf16[1280,128]{1,0:T(8,128)(2,1)S(1)} %get-tuple-element.15), channel_id=1, source_target_pairs={{0,2},{2,0},{1,3},{3,1},{4,6},{6,4},{5,7},{7,5},{8,10},{10,8},{9,1... | collective-permute-start | bytes 983048 | tf_op jit(solution)/shard_map/ppermute | solution.py:20
  94.8 1.3 collective-permute-start.21
  96.1 4.3 %collective-permute-done.21.refs_9_ = bf16[128,512]{1,0:T(8,128)(2,1)S(1)} collective-permute-done((bf16[128,512]{1,0:T(8,128)(2,1)S(1)}, bf16[128,512]{1,0:T(8,128)(2,1)S(1)}, u32[]{:S(2)}, u32[]{:S(2)}) %collective-permute-start.21) | collective-permute-done | bytes 131104 | tf_op jit(solution)/shard_map/ppermute | solution.py:24
  100.4 2.9 %shard_map.122 = (bf16[128,2560]{1,0:T(8,128)(2,1)}, f32[2560,128]{1,0:T(8,128)S(1)}, bf16[2560,128]{1,0:T(8,128)(2,1)S(1)}) custom-call(s32[2]{0:T(128)S(1)} %pad_add_fusion.where_ref, s32[20,2]{1,0:T(8,128)S(1)} %fusion.50.place_ref, bf16[128,512]{1,0:T(8,128)(2,1)S(1)} %pad_maximum_fusion.4.refs_0_, bf16[128,512]{1,0:T(8,128)(2,1)S(1)} %collective-permute-done.1.refs_1_, ...), custom_call_target="tpu_custom_call" | custom-call | tf_op jit(solution)/shard_map/pallas_call | solution.py:149
  104.0 1.6 collective-permute-done.25
  105.9 22.0 %all_to_all.15 = bf16[16,240,128]{2,1,0:T(8,128)(2,1)S(1)} all-to-all(bf16[16,240,128]{2,1,0:T(8,128)(2,1)S(1)} %bitcast.58), channel_id=1, replica_groups=mesh['xh'=2,'y'=4,'zh'=4,'zl'=2,'c'=2,'xl'=2] {'xh','y','zl'}, dimensions={0} | all-to-all | bytes 1966080 | tf_op jit(solution)/shard_map/all_to_all | solution.py:298
  128.0 12.6 %all_to_all.16 = bf16[4,240,128]{2,1,0:T(8,128)(2,1)S(1)} all-to-all(bf16[4,240,128]{2,1,0:T(8,128)(2,1)S(1)} %broadcast_in_dim.10), channel_id=1, replica_groups=mesh['xh'=2,'y'=4,'zh'=4,'zl'=2,'c'=2,'xl'=2] {'zh'}, dimensions={0} | all-to-all | bytes 491520 | tf_op jit(solution)/shard_map/all_to_all | solution.py:301
  140.9 15.5 %all_to_all.17 = bf16[16,240,128]{2,1,0:T(8,128)(2,1)S(1)} all-to-all(bf16[16,240,128]{2,1,0:T(8,128)(2,1)S(1)} %broadcast_in_dim.11), channel_id=1, replica_groups=mesh['xh'=2,'y'=4,'zh'=4,'zl'=2,'c'=2,'xl'=2] {'xh','y','zl'}, dimensions={0} | all-to-all | bytes 1966080 | tf_op jit(solution)/shard_map/all_to_all | solution.py:304
  156.4 5.0 %collective-permute-start.26 = (bf16[3840,128]{1,0:T(8,128)(2,1)S(1)}, bf16[3840,128]{1,0:T(8,128)(2,1)S(1)}, u32[]{:S(2)}, u32[]{:S(2)}) collective-permute-start(bf16[3840,128]{1,0:T(8,128)(2,1)S(1)} %bitcast.56), channel_id=1, source_target_pairs={{0,2},{2,0},{1,3},{3,1},{4,6},{6,4},{5,7},{7,5},{8,10},{10,8},{9,1... | collective-permute-start | bytes 2949128 | tf_op jit(solution)/shard_map/ppermute | solution.py:20
  161.4 1.8 %shard_map.124 = bf16[128,1280]{1,0:T(8,128)(2,1)} custom-call(s32[2]{0:T(128)S(1)} %pad_add_fusion.where_ref, s32[10,2]{1,0:T(8,128)S(1)} %fusion.58.place_ref, bf16[128,1024]{1,0:T(8,128)(2,1)S(1)} %fusion.8.hg0, bf16[128,1024]{1,0:T(8,128)(2,1)S(1)} %collective-permute-done.23.hg1, bf16[20,2,128,128]{3,2,1,0:T(8,128)(2,1)S(1)} %copy-done.2), custom_call_target="tpu_custom_call" | custom-call | tf_op jit(solution)/shard_map/pallas_call | solution.py:216
  163.2 1.9 %shard_map.126 = (f32[2,1280,128]{2,1,0:T(8,128)}, f32[2,2560,128]{2,1,0:T(8,128)}) custom-call(s32[2]{0:T(128)S(1)} %pad_add_fusion.where_ref, bf16[3840,128]{1,0:T(8,128)(2,1)S(1)} %bitcast.57), custom_call_target="tpu_custom_call" | custom-call | tf_op jit(solution)/shard_map/pallas_call | solution.py:275
  165.1 1.9 %shard_map.127 = (f32[2,1280,128]{2,1,0:T(8,128)}, f32[2,2560,128]{2,1,0:T(8,128)}) custom-call(s32[2]{0:T(128)S(1)} %pad_add_fusion.where_ref, bf16[3840,128]{1,0:T(8,128)(2,1)S(1)} %collective-permute-done.26.half_ref, f32[2,1280,128]{2,1,0:T(8,128)} %get-tuple-element.18.refs_0_, ...), custom_call_target="tpu_custom_call", output_to_operand_aliasing={{0}: (2, {}), {1}: (3, {})} | custom-call | tf_op jit(solution)/shard_map/pallas_call | solution.py:275
  (97 shorter events, 13.4 us)
Async XLA Ops:
  0.6 1.4 copy-start
  2.0 0.7 copy-start.7
  2.7 0.7 copy-start.8
  3.4 9.0 %copy-start.9 = (s32[20,2]{0,1:T(2,128)S(1)}, s32[20,2]{0,1:T(2,128)}, u32[]{:S(2)}) copy-start(s32[20,2]{0,1:T(2,128)} %param.17) | copy-start | bytes 484
  3.4 9.1 %copy-start.1 = (bf16[20,2,128,128]{3,2,1,0:T(8,128)(2,1)S(1)}, bf16[20,2,128,128]{3,2,1,0:T(8,128)(2,1)}, u32[]{:S(2)}) copy-start(bf16[20,2,128,128]{3,2,1,0:T(8,128)(2,1)} %w_ref.4) | copy-start | bytes 3932164
  4.2 13.3 %copy-start.10 = (s32[20,2]{0,1:T(2,128)S(1)}, s32[20,2]{0,1:T(2,128)}, u32[]{:S(2)}) copy-start(s32[20,2]{0,1:T(2,128)} %param.15) | copy-start | bytes 484
  4.2 16.2 %collective-permute-start.2 = (bf16[1024,256]{1,0:T(8,128)(2,1)S(1)}, bf16[1024,256]{1,0:T(8,128)(2,1)}, u32[]{:S(2)}, u32[]{:S(2)}) collective-permute-start(bf16[1024,256]{1,0:T(8,128)(2,1)S(1)} %shard_map.121), channel_id=1, source_target_pairs={{0,4},{4,0},{8,12},{12,8},{16,20},{20,16},{24,28},{28,24},{1,5},{5... | collective-permute-start | bytes 1572872 | tf_op jit(solution)/shard_map/ppermute | solution.py:337
  6.7 14.3 %collective-permute-start = (bf16[1024,256]{1,0:T(8,128)(2,1)S(1)}, bf16[1024,256]{1,0:T(8,128)(2,1)}, u32[]{:S(2)}, u32[]{:S(2)}) collective-permute-start(bf16[1024,256]{1,0:T(8,128)(2,1)S(1)} %shard_map.121), channel_id=1, source_target_pairs={{0,2},{2,0},{1,3},{3,1},{4,6},{6,4},{5,7},{7,5},{8,10},{10,8},{9,1... | collective-permute-start | bytes 1572872 | tf_op jit(solution)/shard_map/ppermute | solution.py:20
  7.7 17.1 %collective-permute-start.4 = (bf16[1024,256]{1,0:T(8,128)(2,1)S(1)}, bf16[1024,256]{1,0:T(8,128)(2,1)}, u32[]{:S(2)}, u32[]{:S(2)}) collective-permute-start(bf16[1024,256]{1,0:T(8,128)(2,1)S(1)} %shard_map.121), channel_id=1, source_target_pairs={{0,28},{4,8},{8,4},{12,16},{16,12},{20,24},{24,20},{28,0},{1,29},{... | collective-permute-start | bytes 1572872 | tf_op jit(solution)/shard_map/ppermute | solution.py:337
  12.3 5.2 %copy-start.2 = (bf16[20,2,128,128]{3,2,1,0:T(8,128)(2,1)S(1)}, bf16[20,2,128,128]{3,2,1,0:T(8,128)(2,1)}, u32[]{:S(2)}) copy-start(bf16[20,2,128,128]{3,2,1,0:T(8,128)(2,1)} %w_ref.5) | copy-start | bytes 3932164
  12.5 1.2 copy-start.3
  16.2 24.7 %collective-permute-start.22 = (bf16[128,4096]{1,0:T(8,128)(2,1)}, bf16[128,4096]{1,0:T(8,128)(2,1)}, u32[]{:S(2)}, u32[]{:S(2)}) collective-permute-start(bf16[128,4096]{1,0:T(8,128)(2,1)} %shard_map.123), channel_id=1, source_target_pairs={{0,1},{1,0},{2,3},{3,2},{4,5},{5,4},{6,7},{7,6},{8,9},{9,8},{10,11... | collective-permute-start | bytes 3145736 | tf_op jit(solution)/shard_map/ppermute | solution.py:24
  17.6 1.1 copy-start.5
  20.4 7.5 %collective-permute-start.3 = (bf16[1024,256]{1,0:T(8,128)(2,1)}, bf16[1024,256]{1,0:T(8,128)(2,1)S(1)}, u32[]{:S(2)}, u32[]{:S(2)}) collective-permute-start(bf16[1024,256]{1,0:T(8,128)(2,1)} %collective-permute-done.2), channel_id=1, source_target_pairs={{0,2},{2,0},{1,3},{3,1},{4,6},{6,4},{5,7},{7,5},{8,10},{10,8},{9,1... | collective-permute-start | bytes 1572872 | tf_op jit(solution)/shard_map/ppermute | solution.py:20
  22.3 72.5 %collective-permute-start.1 = (bf16[128,512]{1,0:T(8,128)(2,1)S(1)}, bf16[128,512]{1,0:T(8,128)(2,1)S(1)}, u32[]{:S(2)}, u32[]{:S(2)}) collective-permute-start(bf16[128,512]{1,0:T(8,128)(2,1)S(1)} %pad_maximum_fusion.4.refs_0_), channel_id=1, source_target_pairs={{0,1},{1,0},{2,3},{3,2},{4,5},{5,4},{6,7},{7,6},{8,9},{9,8},{10,11... | collective-permute-start | bytes 393224 | tf_op jit(solution)/shard_map/ppermute | solution.py:24
  24.7 24.8 %collective-permute-start.7 = (bf16[1024,256]{1,0:T(8,128)(2,1)}, bf16[1024,256]{1,0:T(8,128)(2,1)S(1)}, u32[]{:S(2)}, u32[]{:S(2)}) collective-permute-start(bf16[1024,256]{1,0:T(8,128)(2,1)} %collective-permute-done.4), channel_id=1, source_target_pairs={{0,4},{4,0},{8,12},{12,8},{16,20},{20,16},{24,28},{28,24},{1,5},{5... | collective-permute-start | bytes 1572872 | tf_op jit(solution)/shard_map/ppermute | solution.py:337
  24.7 7.2 %collective-permute-start.5 = (bf16[1024,256]{1,0:T(8,128)(2,1)}, bf16[1024,256]{1,0:T(8,128)(2,1)S(1)}, u32[]{:S(2)}, u32[]{:S(2)}) collective-permute-start(bf16[1024,256]{1,0:T(8,128)(2,1)} %collective-permute-done.4), channel_id=1, source_target_pairs={{0,2},{2,0},{1,3},{3,1},{4,6},{6,4},{5,7},{7,5},{8,10},{10,8},{9,1... | collective-permute-start | bytes 1572872 | tf_op jit(solution)/shard_map/ppermute | solution.py:20
  27.9 18.9 %collective-permute-start.9 = (bf16[1024,256]{1,0:T(8,128)(2,1)}, bf16[1024,256]{1,0:T(8,128)(2,1)S(1)}, u32[]{:S(2)}, u32[]{:S(2)}) collective-permute-start(bf16[1024,256]{1,0:T(8,128)(2,1)} %collective-permute-done.2), channel_id=1, source_target_pairs={{0,28},{4,8},{8,4},{12,16},{16,12},{20,24},{24,20},{28,0},{1,29},{... | collective-permute-start | bytes 1572872 | tf_op jit(solution)/shard_map/ppermute | solution.py:337
  32.2 63.9 %collective-permute-start.6 = (bf16[128,1024]{1,0:T(8,128)(2,1)S(1)}, bf16[128,1024]{1,0:T(8,128)(2,1)S(1)}, u32[]{:S(2)}, u32[]{:S(2)}) collective-permute-start(bf16[128,1024]{1,0:T(8,128)(2,1)S(1)} %pad_maximum_fusion.1.refs_2_), channel_id=1, source_target_pairs={{0,1},{1,0},{2,3},{3,2},{4,5},{5,4},{6,7},{7,6},{8,9},{9,8},{10,11... | collective-permute-start | bytes 786440 | tf_op jit(solution)/shard_map/ppermute | solution.py:24
  46.8 11.7 %collective-permute-start.12 = (bf16[1024,256]{1,0:T(8,128)(2,1)S(1)}, bf16[1024,256]{1,0:T(8,128)(2,1)S(1)}, u32[]{:S(2)}, u32[]{:S(2)}) collective-permute-start(bf16[1024,256]{1,0:T(8,128)(2,1)S(1)} %collective-permute-done.9), channel_id=1, source_target_pairs={{0,4},{4,0},{8,12},{12,8},{16,20},{20,16},{24,28},{28,24},{1,5},{5... | collective-permute-start | bytes 1572872 | tf_op jit(solution)/shard_map/ppermute | solution.py:337
  46.9 19.9 %collective-permute-start.10 = (bf16[1024,256]{1,0:T(8,128)(2,1)S(1)}, bf16[1024,256]{1,0:T(8,128)(2,1)S(1)}, u32[]{:S(2)}, u32[]{:S(2)}) collective-permute-start(bf16[1024,256]{1,0:T(8,128)(2,1)S(1)} %collective-permute-done.9), channel_id=1, source_target_pairs={{0,2},{2,0},{1,3},{3,1},{4,6},{6,4},{5,7},{7,5},{8,10},{10,8},{9,1... | collective-permute-start | bytes 1572872 | tf_op jit(solution)/shard_map/ppermute | solution.py:20
  49.8 14.8 %collective-permute-start.14 = (bf16[1024,256]{1,0:T(8,128)(2,1)S(1)}, bf16[1024,256]{1,0:T(8,128)(2,1)S(1)}, u32[]{:S(2)}, u32[]{:S(2)}) collective-permute-start(bf16[1024,256]{1,0:T(8,128)(2,1)S(1)} %collective-permute-done.7), channel_id=1, source_target_pairs={{0,28},{4,8},{8,4},{12,16},{16,12},{20,24},{24,20},{28,0},{1,29},{... | collective-permute-start | bytes 1572872 | tf_op jit(solution)/shard_map/ppermute | solution.py:337
  58.5 9.3 %collective-permute-start.8 = (bf16[1024,256]{1,0:T(8,128)(2,1)S(1)}, bf16[1024,256]{1,0:T(8,128)(2,1)S(1)}, u32[]{:S(2)}, u32[]{:S(2)}) collective-permute-start(bf16[1024,256]{1,0:T(8,128)(2,1)S(1)} %collective-permute-done.7), channel_id=1, source_target_pairs={{0,2},{2,0},{1,3},{3,1},{4,6},{6,4},{5,7},{7,5},{8,10},{10,8},{9,1... | collective-permute-start | bytes 1572872 | tf_op jit(solution)/shard_map/ppermute | solution.py:20
  64.6 8.2 %collective-permute-start.18 = (bf16[512,256]{1,0:T(8,128)(2,1)S(1)}, bf16[512,256]{1,0:T(8,128)(2,1)S(1)}, u32[]{:S(2)}, u32[]{:S(2)}) collective-permute-start(bf16[512,256]{1,0:T(8,128)(2,1)S(1)} %slice.85), channel_id=1, source_target_pairs={{0,28},{4,8},{8,4},{12,16},{16,12},{20,24},{24,20},{28,0},{1,29},{... | collective-permute-start | bytes 786440 | tf_op jit(solution)/shard_map/ppermute | solution.py:337
  66.8 8.0 %collective-permute-start.17 = (bf16[512,256]{1,0:T(8,128)(2,1)S(1)}, bf16[512,256]{1,0:T(8,128)(2,1)S(1)}, u32[]{:S(2)}, u32[]{:S(2)}) collective-permute-start(bf16[512,256]{1,0:T(8,128)(2,1)S(1)} %slice.83), channel_id=1, source_target_pairs={{0,4},{4,0},{8,12},{12,8},{16,20},{20,16},{24,28},{28,24},{1,5},{5... | collective-permute-start | bytes 786440 | tf_op jit(solution)/shard_map/ppermute | solution.py:337
  68.7 11.1 %collective-permute-start.13 = (bf16[1024,256]{1,0:T(8,128)(2,1)S(1)}, bf16[1024,256]{1,0:T(8,128)(2,1)S(1)}, u32[]{:S(2)}, u32[]{:S(2)}) collective-permute-start(bf16[1024,256]{1,0:T(8,128)(2,1)S(1)} %collective-permute-done.12), channel_id=1, source_target_pairs={{0,2},{2,0},{1,3},{3,1},{4,6},{6,4},{5,7},{7,5},{8,10},{10,8},{9,1... | collective-permute-start | bytes 1572872 | tf_op jit(solution)/shard_map/ppermute | solution.py:20
  72.8 7.2 %collective-permute-start.15 = (bf16[1024,256]{1,0:T(8,128)(2,1)S(1)}, bf16[1024,256]{1,0:T(8,128)(2,1)S(1)}, u32[]{:S(2)}, u32[]{:S(2)}) collective-permute-start(bf16[1024,256]{1,0:T(8,128)(2,1)S(1)} %collective-permute-done.14), channel_id=1, source_target_pairs={{0,2},{2,0},{1,3},{3,1},{4,6},{6,4},{5,7},{7,5},{8,10},{10,8},{9,1... | collective-permute-start | bytes 1572872 | tf_op jit(solution)/shard_map/ppermute | solution.py:20
  74.8 2.0 %collective-permute-start.20 = (bf16[512,256]{1,0:T(8,128)(2,1)S(1)}, bf16[512,256]{1,0:T(8,128)(2,1)S(1)}, u32[]{:S(2)}, u32[]{:S(2)}) collective-permute-start(bf16[512,256]{1,0:T(8,128)(2,1)S(1)} %collective-permute-done.18), channel_id=1, source_target_pairs={{0,2},{2,0},{1,3},{3,1},{4,6},{6,4},{5,7},{7,5},{8,10},{10,8},{9,1... | collective-permute-start | bytes 786440 | tf_op jit(solution)/shard_map/ppermute | solution.py:20
  76.7 1.5 collective-permute-start.19
  78.3 17.8 %collective-permute-start.11 = (bf16[128,1024]{1,0:T(8,128)(2,1)S(1)}, bf16[128,1024]{1,0:T(8,128)(2,1)S(1)}, u32[]{:S(2)}, u32[]{:S(2)}) collective-permute-start(bf16[128,1024]{1,0:T(8,128)(2,1)S(1)} %pad_maximum_fusion.2.refs_4_), channel_id=1, source_target_pairs={{0,1},{1,0},{2,3},{3,2},{4,5},{5,4},{6,7},{7,6},{8,9},{9,8},{10,11... | collective-permute-start | bytes 786440 | tf_op jit(solution)/shard_map/ppermute | solution.py:24
  80.4 11.0 %copy-start.6 = (bf16[128,2560]{1,0:T(8,128)(2,1)S(1)}, bf16[128,2560]{1,0:T(8,128)(2,1)}, u32[]{:S(2)}) copy-start(bf16[128,2560]{1,0:T(8,128)(2,1)} %attn_ref.1) | copy-start | bytes 1966084
  80.4 11.0 %collective-permute-start.23 = (bf16[128,1024]{1,0:T(8,128)(2,1)S(1)}, bf16[128,1024]{1,0:T(8,128)(2,1)S(1)}, u32[]{:S(2)}, u32[]{:S(2)}) collective-permute-start(bf16[128,1024]{1,0:T(8,128)(2,1)S(1)} %fusion.8.hg0), channel_id=1, source_target_pairs={{0,1},{1,0},{2,3},{3,2},{4,5},{5,4},{6,7},{7,6},{8,9},{9,8},{10,11... | collective-permute-start | bytes 786440 | tf_op jit(solution)/shard_map/ppermute | solution.py:24
  81.0 19.4 %copy-start.4 = (bf16[128,2560]{1,0:T(8,128)(2,1)S(1)}, bf16[128,2560]{1,0:T(8,128)(2,1)}, u32[]{:S(2)}) copy-start(bf16[128,2560]{1,0:T(8,128)(2,1)} %x_ref.3) | copy-start | bytes 1966084
  81.2 19.2 %collective-permute-start.16 = (bf16[128,1024]{1,0:T(8,128)(2,1)S(1)}, bf16[128,1024]{1,0:T(8,128)(2,1)S(1)}, u32[]{:S(2)}, u32[]{:S(2)}) collective-permute-start(bf16[128,1024]{1,0:T(8,128)(2,1)S(1)} %pad_maximum_fusion.3.refs_6_), channel_id=1, source_target_pairs={{0,1},{1,0},{2,3},{3,2},{4,5},{5,4},{6,7},{7,6},{8,9},{9,8},{10,11... | collective-permute-start | bytes 786440 | tf_op jit(solution)/shard_map/ppermute | solution.py:24
  92.6 11.3 %collective-permute-start.24 = (bf16[1280,128]{1,0:T(8,128)(2,1)S(1)}, bf16[1280,128]{1,0:T(8,128)(2,1)S(1)}, u32[]{:S(2)}, u32[]{:S(2)}) collective-permute-start(bf16[1280,128]{1,0:T(8,128)(2,1)S(1)} %get-tuple-element.15), channel_id=1, source_target_pairs={{0,2},{2,0},{1,3},{3,1},{4,6},{6,4},{5,7},{7,5},{8,10},{10,8},{9,1... | collective-permute-start | bytes 983048 | tf_op jit(solution)/shard_map/ppermute | solution.py:20
  94.8 5.6 %collective-permute-start.21 = (bf16[128,512]{1,0:T(8,128)(2,1)S(1)}, bf16[128,512]{1,0:T(8,128)(2,1)S(1)}, u32[]{:S(2)}, u32[]{:S(2)}) collective-permute-start(bf16[128,512]{1,0:T(8,128)(2,1)S(1)} %pad_maximum_fusion.5.refs_8_), channel_id=1, source_target_pairs={{0,1},{1,0},{2,3},{3,2},{4,5},{5,4},{6,7},{7,6},{8,9},{9,8},{10,11... | collective-permute-start | bytes 393224 | tf_op jit(solution)/shard_map/ppermute | solution.py:24
  103.3 2.4 %collective-permute-start.25 = (bf16[2560,128]{1,0:T(8,128)(2,1)S(1)}, bf16[2560,128]{1,0:T(8,128)(2,1)S(1)}, u32[]{:S(2)}, u32[]{:S(2)}) collective-permute-start(bf16[2560,128]{1,0:T(8,128)(2,1)S(1)} %get-tuple-element.17), channel_id=1, source_target_pairs={{0,2},{2,0},{1,3},{3,1},{4,6},{6,4},{5,7},{7,5},{8,10},{10,8},{9,1... | collective-permute-start | bytes 1966088 | tf_op jit(solution)/shard_map/ppermute | solution.py:20
  156.4 8.7 %collective-permute-start.26 = (bf16[3840,128]{1,0:T(8,128)(2,1)S(1)}, bf16[3840,128]{1,0:T(8,128)(2,1)S(1)}, u32[]{:S(2)}, u32[]{:S(2)}) collective-permute-start(bf16[3840,128]{1,0:T(8,128)(2,1)S(1)} %bitcast.56), channel_id=1, source_target_pairs={{0,2},{2,0},{1,3},{3,1},{4,6},{6,4},{5,7},{7,5},{8,10},{10,8},{9,1... | collective-permute-start | bytes 2949128 | tf_op jit(solution)/shard_map/ppermute | solution.py:20
